TPU v7x, 32 devices: a whole 2x2x4 slice. The times are simulated.
32 devices in a mesh: member: 2 (over x), sub: 8 (over z, y), var: 2 (over core).
Axes of the slice: x: 2, y: 2, z: 4, core: 2. Of those that a mesh axis runs over, the one named last changes fastest.
Arguments:
- innovations: float32 [8, 65536], P('var', ('member', 'sub')), parts along dimension 1, may hold values from -6 to 6
- obs_owner: int32 [65536, 1], P(('member', 'sub')), parts along dimension 0, may hold values from 0 to 7; in each aligned block of 4096 rows (0 to 4095, 4096 to 8191, ...) at most 1024 rows name the same one
- obs_local: int32 [65536], P(('member', 'sub')), parts along dimension 0, may hold values from 0 to 2047
- obs_level: int32 [65536, 1], P(('member', 'sub')), parts along dimension 0, may hold values from 0 to 63; in each aligned block of 4096 rows (0 to 4095, 4096 to 8191, ...) at most 128 rows name the same one
- band_width: int32 [64], replicated, may hold values from 2 to 16
- vert_scale: float32 [8, 64], P('var'), may hold values from 1 to 4
- sigma: float32 [8, 64], P('var'), may hold values from 0.5 to 2
- balance: float32 [8, 8], P('var')
Outputs:
- increment: float32 [8, 64, 64, 512], P('var', None, ('member', 'sub')), parts along dimension 2
There are 2 independent parts, one for each index of `member`. A program takes and returns all parts, laid end to end along the dimension named above; an argument that names none is the same for every part. Nothing has to cross between parts.
Inputs may be any that keep to these rules, and one draw needn't show every extreme that they name: `obs_owner`: in the rows of one device no subdomain is named more than 1024 times, a bound that some block reaches. `obs_level`: in the rows of one device no level is named more than 128 times, a bound that some block reaches.
All inputs are finite; a program needn't handle non-finite values.
Results may differ from a plain program's by a relative error of at most 0.00008.
Values sent between devices are 32-bit elements; how exact they have to be, the bound alone decides.
No kernel may reach another device: no remote copies, remote signals or barrier semaphores. Data moves between devices by JAX's collectives and lax.ppermute only.
A program may use at most 192 MiB of HBM per device.

v0:
```python
import jax
import jax.numpy as jnp
from jax import lax
from jax.sharding import PartitionSpec as P

VB = 6
NX_DEV = 4
NY = 512


def filter_matrix(width, count):
    rate = width.astype(jnp.float32)[:, None, None]
    index = jnp.arange(count)
    dist = jnp.abs(index[:, None] - index[None, :]).astype(jnp.float32)
    far = (count - jnp.maximum(index[:, None], index[None, :])).astype(jnp.float32)
    return jnp.exp(-dist / rate) * (1.0 - jnp.exp(-2.0 * far / rate))


def vertical_matrix(scale, levels):
    index = jnp.arange(levels)
    dist = (index[:, None] - index[None, :]).astype(jnp.float32)
    corr = jnp.exp(-dist * dist / (2.0 * scale[:, :, None] * scale[:, None, :]))
    return jnp.where(jnp.abs(dist) <= VB, corr, jnp.float32(0.0))


def smooth(field, across, along):
    high = lax.Precision.HIGHEST
    part = jnp.einsum("lij,vljy->vliy", across, field, precision=high)
    return jnp.einsum("vlxj,lyj->vlxy", part, along, precision=high)


def slot_rank(target, count):
    hits = (target[:, None] == jnp.arange(count)[None, :]).astype(jnp.int32)
    return jnp.sum((jnp.cumsum(hits, 0) - hits) * hits, 1)


def on_device(innovations, obs_owner, obs_local, obs_level, band_width, vert_scale, sigma, balance):
    groups = lax.axis_size("sub")
    here = lax.axis_index("sub")
    nvar, nobs = innovations.shape
    levels = band_width.shape[0]
    depth = levels // groups
    wide = NX_DEV * groups
    mine = lax.dynamic_slice_in_dim(band_width, here * depth, depth)
    across = filter_matrix(mine, wide)
    along = filter_matrix(mine, NY)
    owner = obs_owner[:, 0]
    level = obs_level[:, 0]
    limit = 2 * nobs // groups
    target = owner * limit + slot_rank(owner, groups)
    place = level * (NX_DEV * NY) + obs_local
    values = jnp.zeros((nvar, groups * limit), jnp.float32).at[:, target].set(innovations)
    spots = jnp.zeros((groups * limit,), jnp.int32).at[target].set(place)
    values, spots = (
        lax.all_to_all(
            values.reshape(nvar, groups, limit), "sub", split_axis=1, concat_axis=1, tiled=True
        ),
        lax.all_to_all(
            spots.reshape(1, groups, limit), "sub", split_axis=1, concat_axis=1, tiled=True
        ),
    )
    column = jnp.zeros((nvar, levels * NX_DEV * NY), jnp.float32)
    column = column.at[:, spots.reshape(-1)].add(values.reshape(nvar, -1))
    column = column.reshape(nvar, levels, NX_DEV, NY)
    slab = smooth(
        lax.all_to_all(column, "sub", split_axis=1, concat_axis=2, tiled=True), across, along
    )
    corr = vertical_matrix(vert_scale, levels)
    correlated = jnp.einsum(
        "vlm,vmxy->vlxy",
        corr,
        lax.all_to_all(slab, "sub", split_axis=2, concat_axis=1, tiled=True),
        precision=lax.Precision.HIGHEST,
    )
    mixed = jnp.einsum(
        "vu,ulxy->vlxy",
        balance,
        lax.all_gather(correlated, "var", axis=0, tiled=True),
        precision=lax.Precision.HIGHEST,
    )
    return mixed * sigma[:, :, None, None]


def solution(mesh):
    in_specs = (
        P("var", ("member", "sub")),
        P(("member", "sub"), None),
        P(("member", "sub")),
        P(("member", "sub"), None),
        P(),
        P("var", None),
        P("var", None),
        P("var", None),
    )
    out_specs = P("var", None, ("member", "sub"), None)
    return jax.shard_map(
        on_device, mesh=mesh, in_specs=in_specs, out_specs=out_specs, check_vma=False
    )
```

profile of v0, /device:TPU:0, one launch (start us, length us, event | category | flops | bytes accessed | tf_op | source)
XLA Modules:
  0.0 394.5 jit_solution(10532747100811612458)
XLA Ops:
  6.5 0.0 copy-start
  6.5 0.7 fusion.44
  7.3 2.3 reduce-window.6
  9.6 0.3 slice_reduce_fusion
  9.9 0.2 reduce-window.9
  10.1 0.1 add_bitcast_fusion
  10.2 0.8 fusion.38
  11.0 0.7 compare_select_fusion.1
  11.8 0.7 broadcast_multiply_fusion
  12.5 0.7 add.33
  13.2 16.1 %scatter_custom_fusion = s32[8192]{0:T(1024)} fusion(s32[4096]{0:T(1024)S(1)} %bitcast.89, s32[4096]{0:T(1024)S(1)} %add.33, s32[]{:T(128)} %constant.22.clone.1), kind=kCustom, calls=%fused_computation.68 | custom fusion | bytes 32772 | tf_op jit(solution)/shard_map/scatter | solution.py:53
  29.3 7.3 %all-to-all-start = ((s32[1,8,1024]{2,0,1:T(1,128)}), s32[1,8,1024]{2,0,1:T(1,128)S(1)}, u32[]{:S(2)}, u32[]{:S(2)}) async-start(s32[1,8,1024]{2,0,1:T(1,128)} %bitcast.10), calls=%async_computation | async-start | bytes 65536 | tf_op jit(solution)/shard_map/all_to_all | solution.py:58
  36.6 1.5 copy.34
  38.1 12.8 %scatter_custom_fusion.1 = f32[4,8192]{0,1:T(8,128)} fusion(s32[4096]{0:T(1024)S(1)} %bitcast.90, f32[4096,4]{1,0:T(8,128)S(1)} %copy.34, f32[]{:T(128)} %constant.18.clone.1), kind=kCustom, calls=%fused_computation.27 | custom fusion | bytes 131076 | tf_op jit(solution)/shard_map/scatter | solution.py:52
  50.8 3.5 copy.35
  54.3 0.0 all-to-all-done
  54.3 6.5 %all-to-all-start.1 = ((f32[4,8,1024]{2,0,1:T(4,128)}), f32[4,8,1024]{2,0,1:T(4,128)S(1)}, u32[]{:S(2)}, u32[]{:S(2)}) async-start(f32[4,8,1024]{2,0,1:T(4,128)} %copy.35), calls=%async_computation.1 | async-start | bytes 262144 | tf_op jit(solution)/shard_map/all_to_all | solution.py:55
  60.9 5.9 %sort = (s32[8192]{0:T(1024)S(1)}, s32[8192]{0:T(1024)S(1)}) sort(s32[8192]{0:T(1024)S(1)} %bitcast.84, s32[8192]{0:T(1024)S(1)} %iota.70), dimensions={0}, to_apply=%compare | sort | flops 106496 | bytes 131072 | tf_op jit(solution)/shard_map/scatter-add | solution.py:63
  66.8 1.3 all-to-all-done.1
  68.1 2.6 copy.36
  70.8 127.5 %scatter_custom_fusion.2 = f32[4,131072]{0,1:T(8,128)} fusion(s32[8192]{0:T(1024)S(1)} %get-tuple-element.5, f32[]{:T(128)} %constant.18.clone.1, f32[8192,4]{1,0:T(8,128)} %copy.36, s32[8192]{0:T(1024)S(1)} %broadcast_clamp_fusion), kind=kCustom, calls=%fused_computation.4 | custom fusion | flops 32768 | bytes 2097664 | tf_op jit(solution)/shard_map/scatter-add | solution.py:63
  198.2 35.3 %copy.37 = f32[4,64,4,512]{3,2,0,1:T(4,128)} copy(f32[4,64,4,512]{0,3,2,1:T(8,128)} %bitcast.17) | data formatting | bytes 4194304 | tf_op jit(solution)/shard_map/reshape | solution.py:64
  233.5 9.2 %all-to-all-start.2 = ((f32[4,64,4,512]{3,2,0,1:T(4,128)}), f32[4,64,4,512]{3,2,0,1:T(4,128)S(1)}, u32[]{:S(2)}, u32[]{:S(2)}) async-start(f32[4,64,4,512]{3,2,0,1:T(4,128)} %copy.37), calls=%async_computation.2 | async-start | bytes 4194304 | tf_op jit(solution)/shard_map/all_to_all | solution.py:66
  242.8 0.0 copy-done.4
  242.8 0.1 dynamic-slice_convert_fusion
  242.9 1.3 convert_multiply_fusion
  244.2 45.3 %all-to-all-done.2 = f32[4,64,4,512]{3,2,0,1:T(4,128)S(1)} async-done(((f32[4,64,4,512]{3,2,0,1:T(4,128)}), f32[4,64,4,512]{3,2,0,1:T(4,128)S(1)}, u32[]{:S(2)}, u32[]{:S(2)}) %all-to-all-start.2) | async-done | bytes 2097184 | tf_op jit(solution)/shard_map/all_to_all | solution.py:66
  289.5 1.2 copy.64
  290.7 0.0 copy-start.1
  290.7 0.2 copy.39
  291.0 3.7 fusion.21
  294.7 0.0 copy-done.1
  294.7 11.0 %fusion.27 = f32[4,8,32,512]{3,2,0,1:T(8,128)S(1)} fusion(f32[8,4,512,32]{2,3,1,0:T(8,128)S(1)} %fusion.21, f32[512,512]{1,0:T(8,128)S(1)} %get-tuple-element.9, f32[8]{0:T(128)S(1)} %dynamic-slice_convert_fusion, f32[512,512]{1,0:T(8,128)S(1)} %copy-done.1), kind=kOutput, calls=%fused_computation.29 | convolution fusion | flops 3229614080 | bytes 6291488 | tf_op jit(solution)/shard_map/vlxj,lyj->vlxy/dot_general | solution.py:29
  305.7 0.0 copy-start.2
  305.7 2.7 copy.41
  308.4 3.6 all-to-all-start.3
  312.0 0.0 all-gather.2.cloned.1.call-start
  312.1 0.0 copy-done.2
  312.1 48.3 %all-to-all-done.3 = f32[4,8,32,512]{3,0,1,2:T(4,128)S(1)} async-done(((f32[4,8,32,512]{3,0,1,2:T(4,128)}), f32[4,8,32,512]{3,0,1,2:T(4,128)S(1)}, u32[]{:S(2)}, u32[]{:S(2)}) %all-to-all-start.3) | async-done | bytes 2097184 | tf_op jit(solution)/shard_map/all_to_all | solution.py:72
  360.4 0.7 copy.42
  361.1 0.0 copy-start.3
  361.1 3.3 fusion.17
  364.4 0.0 all-gather.2.cloned.1.call-update
  364.4 0.0 copy-done.3
  364.5 0.1 copy.45
  364.6 12.3 %all-gather.2.cloned.1.call-done = f32[8,64,4,512]{3,1,2,0:T(8,128)} async-done(((f32[4,64,4,512]{3,1,2,0:T(8,128)}), f32[8,64,4,512]{3,1,2,0:T(8,128)}) %all-gather.2.cloned.1.call-update) | async-done | bytes 4194320 | tf_op jit(solution)/shard_map/all_gather | solution.py:78
  376.8 8.5 %bitcast_multiply_fusion = f32[4,64,4,512]{3,0,2,1:T(4,128)S(1)} fusion(f32[8,64,4,512]{3,1,2,0:T(8,128)} %all-gather.2.cloned.1.call-done, f32[4,64]{0,1:T(8,128)S(1)} %copy.45, f32[4,8]{1,0:T(4,128)S(1)} %copy-done), kind=kOutput, calls=%fused_computation.19 | convolution fusion | flops 50855936 | bytes 6292608 | tf_op jit(solution)/shard_map/vu,ulxy->vlxy/dot_general | solution.py:75
  385.4 2.1 copy.46
  (9 shorter events, 0.1 us)
Async XLA Ops:
  6.5 370.3 %copy-start = (f32[4,8]{1,0:T(4,128)S(1)}, f32[4,8]{1,0:T(4,128)}, u32[]{:S(2)}) copy-start(f32[4,8]{1,0:T(4,128)} %param.15) | copy-start | bytes 388
  29.3 25.0 %all-to-all-start = ((s32[1,8,1024]{2,0,1:T(1,128)}), s32[1,8,1024]{2,0,1:T(1,128)S(1)}, u32[]{:S(2)}, u32[]{:S(2)}) async-start(s32[1,8,1024]{2,0,1:T(1,128)} %bitcast.10), calls=%async_computation | async-start | bytes 65536 | tf_op jit(solution)/shard_map/all_to_all | solution.py:58
  54.3 13.8 %all-to-all-start.1 = ((f32[4,8,1024]{2,0,1:T(4,128)}), f32[4,8,1024]{2,0,1:T(4,128)S(1)}, u32[]{:S(2)}, u32[]{:S(2)}) async-start(f32[4,8,1024]{2,0,1:T(4,128)} %copy.35), calls=%async_computation.1 | async-start | bytes 262144 | tf_op jit(solution)/shard_map/all_to_all | solution.py:55
  233.5 9.2 %copy-start.4 = (s32[64]{0:T(128)S(1)}, s32[64]{0:T(128)}, u32[]{:S(2)}) copy-start(s32[64]{0:T(128)} %param.12) | copy-start | bytes 772
  233.5 56.0 %all-to-all-start.2 = ((f32[4,64,4,512]{3,2,0,1:T(4,128)}), f32[4,64,4,512]{3,2,0,1:T(4,128)S(1)}, u32[]{:S(2)}, u32[]{:S(2)}) async-start(f32[4,64,4,512]{3,2,0,1:T(4,128)} %copy.37), calls=%async_computation.2 | async-start | bytes 4194304 | tf_op jit(solution)/shard_map/all_to_all | solution.py:66
  290.7 4.0 %copy-start.1 = (f32[512,512]{1,0:T(8,128)S(1)}, f32[512,512]{1,0:T(8,128)}, u32[]{:S(2)}) copy-start(f32[512,512]{1,0:T(8,128)} %get-tuple-element.10) | copy-start | bytes 3145732
  305.7 6.4 %copy-start.2 = (f32[4,64]{1,0:T(4,128)S(1)}, f32[4,64]{1,0:T(4,128)}, u32[]{:S(2)}) copy-start(f32[4,64]{1,0:T(4,128)} %param.13) | copy-start | bytes 3076
  308.4 52.1 %all-to-all-start.3 = ((f32[4,8,32,512]{3,0,1,2:T(4,128)}), f32[4,8,32,512]{3,0,1,2:T(4,128)S(1)}, u32[]{:S(2)}, u32[]{:S(2)}) async-start(f32[4,8,32,512]{3,0,1,2:T(4,128)} %copy.41), calls=%async_computation.3 | async-start | bytes 4194304 | tf_op jit(solution)/shard_map/all_to_all | solution.py:72
  312.0 64.8 %all-gather.2.cloned.1.call-start = ((), (), s32[]{:S(2)}) async-start(), calls=%async_computation.4 | async-start | bytes 6291456 | tf_op jit(solution)/shard_map/all_gather | solution.py:78
  361.1 3.3 copy-start.3
Sparse Core Ops, SparseCore 0:
  364.6 12.2 all-gather.1
where the time goes:
time: 400 us; the launch traced here: 395 us
  other arithmetic  141 us (35%)
  waiting for transfers between devices  107 us (27%)
  local copies, waits for them, and re-layouts  79.1 us (20%)
  starting transfers between devices  26.7 us (7%)
  matrix products  26.5 us (7%)
  between operations  13.8 us (3%)
    scatter-add x3, other arithmetic, on_device(): column = column.at[:, spots.reshape(-1)].add(values.reshape(nvar, -1))  133 us
    all_to_all x1, waiting for transfers between devices, on_device(): lax.all_to_all(slab, 'sub', split_axis=2, concat_axis=1, tiled=True)  48.3 us
    all_to_all x1, waiting for transfers between devices, on_device(): lax.all_to_all(column, 'sub', split_axis=1, concat_axis=2, tiled=True)  45.3 us
    reshape x1, local copies, waits for them, and re-layouts, on_device(): column = column.reshape(nvar, levels, NX_DEV, NY)  35.3 us
    scatter x1, local copies, waits for them, and re-layouts, on_device(): spots = jnp.zeros((groups * limit,), jnp.int32).at[target].set(place)  16.1 us
    scatter x1, local copies, waits for them, and re-layouts, on_device(): jnp.zeros((nvar, groups * limit), jnp.float32).at[:, target]  12.8 us
    all_gather x1, waiting for transfers between devices, on_device(): lax.all_gather(correlated, 'var', axis=0, tiled=True)  12.3 us
    dot_general x1, matrix products, smooth(): return jnp.einsum('vlxj,lyj->vlxy', part, along, precision=high)  11 us
  transfers between devices with their start and end apart: 5, of which 4 were waited for; matrix products, arithmetic and copies ran while one was open for 6% of the time, Pallas kernels for 0%

commit v1 on v0

v1 whole, which is shorter than its diff:
```python
import functools

import jax
import jax.numpy as jnp
from jax import lax
from jax.experimental import pallas as pl
from jax.experimental.pallas import tpu as pltpu
from jax.sharding import PartitionSpec as P

VB = 6
NX_DEV = 4
NY = 512
LANES = 128
HALF = 256
F32 = jnp.float32
BF16 = jnp.bfloat16


def nt_dot(a, b):
    return lax.dot_general(a, b, (((1,), (1,)), ((), ())), preferred_element_type=F32)


def nn_dot(a, b):
    return jnp.dot(a, b, preferred_element_type=F32)


def iota(shape, dim):
    return lax.broadcasted_iota(jnp.int32, shape, dim)


def route_kernel(inn, level, owner, local, pay, hot, pre, dest, left, right):
    nvar, nobs = inn.shape
    chunks = nobs // LANES
    levels = hot.shape[0] // chunks
    rows = iota((levels, LANES), 0)
    for c in range(chunks):
        hit = jnp.where(rows == level[c : c + 1, :], 1.0, 0.0)
        hot[c * levels : (c + 1) * levels, :] = hit.astype(BF16)
    before = iota((LANES, 2 * LANES), 0) < iota((LANES, 2 * LANES), 1)
    pre[...] = nn_dot(hot[...], jnp.where(before, 1.0, 0.0).astype(BF16))
    count = jnp.zeros((levels, LANES), F32)
    for c in range(chunks):
        count = count + pre[c * levels : (c + 1) * levels, LANES:]
    lower = iota((levels, levels), 1) < iota((levels, levels), 0)
    base = nn_dot(jnp.where(lower, 1.0, 0.0).astype(BF16), count.astype(BF16))
    lane = iota((levels, LANES), 1)
    starts = jnp.sum(jnp.where(lane == rows, base, 0.0), 0, keepdims=True)
    starts = jnp.where(iota((8, LANES), 1) < levels, starts, float(nobs))
    for c in range(chunks):
        part = pre[c * levels : (c + 1) * levels, :]
        slot = jnp.where(rows == level[c : c + 1, :], part[:, :LANES] + base, 0.0)
        dest[c : c + 1, :] = jnp.sum(slot, 0, keepdims=True).astype(jnp.int32)
        base = base + part[:, LANES:]
    place = owner[...] * (NX_DEV * NY) + local[...]
    rows_hi, rows_lo = iota((chunks, LANES), 0), iota((LANES, LANES), 0)
    for c in range(chunks):
        at = slice(c * LANES, (c + 1) * LANES)
        slot = dest[c : c + 1, :]
        mask = rows_hi == slot // LANES
        right[:, at] = jnp.where(rows_lo == slot % LANES, 1.0, 0.0).astype(BF16)
        pieces = []
        for v in range(nvar):
            value = inn[v : v + 1, at]
            high = value.astype(BF16).astype(F32)
            pieces += [high, value - high]
        spot = place[c : c + 1, :]
        pieces += [(spot // HALF).astype(F32), (spot % HALF).astype(F32)]
        for q, piece in enumerate(pieces):
            left[q * chunks : (q + 1) * chunks, at] = jnp.where(mask, piece, 0.0).astype(BF16)
    packed = nt_dot(left[...], right[...])
    for v in range(nvar):
        both = packed[2 * v * chunks : (2 * v + 1) * chunks] + packed[(2 * v + 1) * chunks : (2 * v + 2) * chunks]
        pay[pl.ds(v, chunks, stride=nvar), :] = both
    high, low = packed[2 * nvar * chunks : (2 * nvar + 1) * chunks], packed[(2 * nvar + 1) * chunks :]
    pay[nvar * chunks : (nvar + 1) * chunks, :] = high * float(HALF) + low
    pay[(nvar + 1) * chunks :, :] = starts


def route(innovations, owner, level, local, levels):
    nvar, nobs = innovations.shape
    chunks = nobs // LANES
    pieces = 2 * nvar + 2
    return pl.pallas_call(
        route_kernel,
        out_shape=jax.ShapeDtypeStruct(((nvar + 1) * chunks + 8, LANES), F32),
        scratch_shapes=[
            pltpu.VMEM((chunks * levels, LANES), BF16),
            pltpu.VMEM((chunks * levels, 2 * LANES), F32),
            pltpu.VMEM((chunks, LANES), jnp.int32),
            pltpu.VMEM((pieces * chunks, nobs), BF16),
            pltpu.VMEM((LANES, nobs), BF16),
        ],
        compiler_params=pltpu.CompilerParams(vmem_limit_bytes=32 << 20),
        name="route",
    )(innovations, level.reshape(chunks, LANES), owner.reshape(chunks, LANES), local.reshape(chunks, LANES))


def table_kernel(width, high, low):
    depth = high.shape[0]
    row, col = iota((LANES, LANES), 0), iota((LANES, LANES), 1)
    near = jnp.abs(row - col).astype(F32)
    far = jnp.where(col < LANES // 2, LANES - row, row + 1).astype(F32)
    for k in range(depth):
        rate = width[pl.program_id(0) * depth + k].astype(F32)
        for at, dist in ((0, near), (LANES, far)):
            full = jnp.exp(-dist / rate)
            top = full.astype(BF16)
            high[k, :, at : at + LANES] = top
            low[k, :, at : at + LANES] = (full - top.astype(F32)).astype(BF16)


def tables(band_width):
    levels = band_width.shape[0]
    depth = 8
    spec = pl.BlockSpec((depth, LANES, 2 * LANES), lambda i: (i, 0, 0))
    shape = jax.ShapeDtypeStruct((levels, LANES, 2 * LANES), BF16)
    return pl.pallas_call(
        table_kernel,
        grid=(levels // depth,),
        in_specs=[pl.BlockSpec(memory_space=pltpu.SMEM)],
        out_specs=(spec, spec),
        out_shape=(shape, shape),
        name="tables",
    )(band_width)


def mix_matrix(scale, sigma, balance):
    nvar, levels = scale.shape
    index = jnp.arange(levels)
    dist = index[:, None] - jnp.repeat(index, nvar)[None, :]
    own = jnp.tile(scale.T, (1, levels))
    gap = dist.astype(F32)
    corr = jnp.exp(-gap * gap / (2.0 * own * scale.T.reshape(1, -1)))
    corr = jnp.where(jnp.abs(dist) <= VB, corr, F32(0.0))
    mix = sigma[:, :, None] * jnp.tile(balance, (1, levels))[:, None, :] * corr[None]
    mix = mix.reshape(-1, levels * nvar)
    high = lax.reduce_precision(mix, 8, 7)
    return high.astype(BF16), (mix - high).astype(BF16)


def field_kernel(sources, wide, nvar, width, first, *refs):
    own, oth, marks = refs[:sources], refs[sources : 2 * sources], refs[2 * sources : 3 * sources]
    high, low, mix_high, mix_low, out, vals, spots, left, right, slab = refs[3 * sources :]
    step = pl.program_id(0)
    depth = high.shape[0]
    chunks = (own[0].shape[0] - 8) // (nvar + 1)
    lane8 = iota((8, LANES), 1)
    sub8 = iota((8, LANES), 0)

    @pl.when(step == 0)
    def _():
        for s in range(sources):
            for c in range(0, chunks, 2):
                here, there = own[s][4 * c : 4 * c + 8, :], oth[s][4 * c : 4 * c + 8, :]
                vals[s, 8 * c : 8 * c + 8, :] = jnp.where(sub8 < 4, here, pltpu.roll(there, 4, 0))
                vals[s, 8 * c + 8 : 8 * c + 16, :] = jnp.where(sub8 < 4, pltpu.roll(here, 4, 0), there)
            vals[s, 8 * chunks :, :] = jnp.zeros((8, LANES), F32)
            spots[s, :chunks, :] = own[s][nvar * chunks : (nvar + 1) * chunks, :]
            spots[s, chunks:, :] = jnp.zeros((8, LANES), F32)

    col = first[0] + sub8 % 4
    reach = jnp.where(sub8 < 4, col, 2 * wide - col).astype(F32)
    tall = iota((HALF, LANES), 0).astype(F32).astype(BF16)
    one, zero = jnp.ones((HALF, LANES), BF16), jnp.zeros((HALF, LANES), BF16)
    line = iota((8, LANES), 1).astype(F32)

    def per_level(k, carry):
        lev = step * depth + k
        rate = width[lev].astype(F32)
        slope = -1.0 / jnp.full((8, LANES), rate, F32)
        for s in range(sources):
            start = marks[s][0, lev].astype(jnp.int32)
            size = marks[s][0, lev + 1].astype(jnp.int32) - start
            c, off = start // LANES, start % LANES
            back = lax.rem(LANES - off, LANES)
            row = pl.multiple_of(8 * c, 8)
            value = jnp.where(lane8 >= off, vals[s, pl.ds(row, 8), :], vals[s, pl.ds(row + 8, 8), :])
            value = pltpu.roll(value, back, 1)
            spot = jnp.where(lane8[:1] >= off, spots[s, pl.ds(c, 1), :], spots[s, pl.ds(c + 1, 1), :])
            spot = pltpu.roll(jnp.broadcast_to(spot, (8, LANES)), back, 1).astype(jnp.int32)
            xpos = (spot // (2 * HALF)).astype(F32)
            side = ((spot // HALF) % 2).astype(F32)
            ypos = (spot % HALF).astype(F32)
            gain = jnp.exp(jnp.abs(reach - xpos) * slope)
            gain = gain - pltpu.roll(gain, 4, 0)
            gain = jnp.where(lane8 < size, gain, 0.0)
            upper = jnp.concatenate([side, side], 0).astype(BF16)
            lower = jnp.concatenate([1.0 - side, 1.0 - side], 0).astype(BF16)
            at = slice(s * LANES, (s + 1) * LANES)
            for x in range(NX_DEV):
                term = value * jnp.broadcast_to(gain[x : x + 1, :], (8, LANES))
                top = term.astype(BF16).astype(F32)
                pair = jnp.concatenate([top, term - top], 0).astype(BF16)
                left[32 * x : 32 * x + 16, at] = pair * lower
                left[32 * x + 16 : 32 * x + 32, at] = pair * upper
            mark = jnp.broadcast_to(ypos[:1], (HALF, LANES)).astype(BF16)
            right[:, at] = jnp.where(tall == mark, one, zero)
        both = nt_dot(left[...], right[...])
        blocks = []
        for x in range(NX_DEV):
            for h in range(2):
                row = 32 * x + 16 * h
                total = both[row : row + 8] + both[row + 8 : row + 16]
                blocks += [total[:, :LANES], total[:, LANES:]]
        field = jnp.concatenate(blocks, 0)
        top = field.astype(BF16)
        rest = (field - top.astype(F32)).astype(BF16)
        mat = high[k]
        done = nn_dot(top, mat) + nn_dot(rest, mat) + nn_dot(top, low[k])
        rise = jnp.exp(line * slope)
        fall = jnp.exp((LANES - 1.0 - line) * slope)
        edge = jnp.exp((LANES - line) * slope)
        hop = jnp.exp(LANES * slope)
        for x in range(NX_DEV):
            ahead, behind, here = [], [], []
            for b in range(4):
                row = (4 * x + b) * 8
                here.append(done[row : row + 8, :LANES])
                moments = done[row : row + 8, LANES:]
                turned = pltpu.roll(moments, LANES // 2, 1)
                ahead.append(jnp.where(lane8 < LANES // 2, moments, turned))
                behind.append(jnp.where(lane8 < LANES // 2, turned, moments))
            run = ahead[0]
            for b in range(1, 4):
                here[b] = here[b] + rise * run
                run = ahead[b] + hop * run
            bound = edge * run
            run = behind[3]
            for b in (2, 1, 0):
                here[b] = here[b] + fall * run
                run = behind[b] + hop * run
            for b in (3, 2, 1, 0):
                slab[4 * x + b, pl.ds(pl.multiple_of(8 * lev, 8), 8), :] = here[b] - bound
                bound = bound * hop
        return carry

    lax.fori_loop(0, depth, per_level, 0)

    @pl.when(step == pl.num_programs(0) - 1)
    def _():
        for x in range(NX_DEV):
            for h in range(2):
                part = jnp.concatenate([slab[4 * x + 2 * h], slab[4 * x + 2 * h + 1]], 1)
                top = part.astype(BF16)
                rest = (part - top.astype(F32)).astype(BF16)
                total = nn_dot(mix_high[...], top) + nn_dot(mix_high[...], rest) + nn_dot(mix_low[...], top)
                out[:, x, h * HALF : (h + 1) * HALF] = total


def field(own, oth, band_width, first, high, low, mix_high, mix_low, nvar, levels, wide):
    sources = len(own)
    rows = own[0].shape[0]
    chunks = (rows - 8) // (nvar + 1)
    depth = 8
    whole = pl.BlockSpec((rows, LANES), lambda i: (0, 0))
    marks = pl.BlockSpec((8, LANES), lambda i: (rows // 8 - 1, 0), memory_space=pltpu.SMEM)
    table = pl.BlockSpec((depth, LANES, 2 * LANES), lambda i: (i, 0, 0))
    matrix = pl.BlockSpec(mix_high.shape, lambda i: (0, 0))
    smem = pl.BlockSpec(memory_space=pltpu.SMEM)
    out_shape = (mix_high.shape[0], NX_DEV, NY)
    return pl.pallas_call(
        functools.partial(field_kernel, sources, wide, nvar),
        grid=(levels // depth,),
        in_specs=[smem, smem] + [whole] * (2 * sources) + [marks] * sources + [table, table, matrix, matrix],
        out_specs=pl.BlockSpec(out_shape, lambda i: (0, 0, 0)),
        out_shape=jax.ShapeDtypeStruct(out_shape, F32),
        scratch_shapes=[
            pltpu.VMEM((sources, 8 * chunks + 8, LANES), F32),
            pltpu.VMEM((sources, chunks + 8, LANES), F32),
            pltpu.VMEM((32 * NX_DEV, sources * LANES), BF16),
            pltpu.VMEM((HALF, sources * LANES), BF16),
            pltpu.VMEM((4 * NX_DEV, 8 * levels, LANES), F32),
        ],
        compiler_params=pltpu.CompilerParams(vmem_limit_bytes=48 << 20),
        name="field",
    )(band_width, first, *own, *oth, *own, high, low, mix_high, mix_low)


def on_device(innovations, obs_owner, obs_local, obs_level, band_width, vert_scale, sigma, balance):
    groups = lax.axis_size("sub")
    nvar, _ = innovations.shape
    levels = band_width.shape[0]
    swap = [(0, 1), (1, 0)]
    unit = route(innovations, obs_owner, obs_level, obs_local, levels)
    own = [unit]
    for k in range(2, groups, 2):
        own.append(lax.ppermute(unit, "sub", [(i, (i + k) % groups) for i in range(groups)]))
    own += [lax.ppermute(held, "sub", [(i, i ^ 1) for i in range(groups)]) for held in own]
    oth = [lax.ppermute(held, "var", swap) for held in own]
    scale = jnp.concatenate([vert_scale, lax.ppermute(vert_scale, "var", swap)], 0)
    weights = jnp.where(lax.axis_index("var") == 0, balance, jnp.roll(balance, nvar, 1))
    mix_high, mix_low = mix_matrix(scale, sigma, weights)
    high, low = tables(band_width)
    first = (lax.axis_index("sub") * NX_DEV).astype(jnp.int32).reshape(1)
    out = field(own, oth, band_width, first, high, low, mix_high, mix_low, nvar, levels, NX_DEV * groups)
    return out.reshape(nvar, levels, NX_DEV, NY)


def solution(mesh):
    in_specs = (
        P("var", ("member", "sub")),
        P(("member", "sub"), None),
        P(("member", "sub")),
        P(("member", "sub"), None),
        P(),
        P("var", None),
        P("var", None),
        P("var", None),
    )
    out_specs = P("var", None, ("member", "sub"), None)
    return jax.shard_map(on_device, mesh=mesh, in_specs=in_specs, out_specs=out_specs, check_vma=False)
```

time: 400 us -> 95 us (0.24); the launches traced: 395 us -> 94.4 us
  other arithmetic: 141 us -> 2.51 us
  waiting for transfers between devices: 107 us -> 5.42 us
  local copies, waits for them, and re-layouts: 79.1 us -> 7.94 us
  Pallas kernels: 0 us -> 67.2 us
  matrix products: 26.5 us -> 0 us
  starting transfers between devices: 26.7 us -> 11.2 us
  between operations: 13.8 us -> 0.13 us
    scatter-add x3 -> x0, other arithmetic: 133 us -> none  [on_device(): column = column.at[:, spots.reshape(-1)].add(values.reshape(nvar, -1))]
    all_to_all x4 -> x0, waiting for transfers between devices: 94.9 us -> none  [the longest x1 48.3 us: on_device(): lax.all_to_all(slab, 'sub', split_axis=2, concat_axis=1, tiled=True)]
    pallas_call x0 -> x3, Pallas kernels: none -> 67.2 us  [the longest x1 58.4 us: field(): pl.pallas_call(functools.partial(field_kernel, sources, wide, nvar), grid...]
    reshape x3 -> x0, local copies, waits for them, and re-layouts: 41.4 us -> none  [the longest x1 35.3 us: on_device(): column = column.reshape(nvar, levels, NX_DEV, NY)]
    scatter x2 -> x0, local copies, waits for them, and re-layouts: 28.8 us -> none  [the longest x1 16.1 us: on_device(): spots = jnp.zeros((groups * limit,), jnp.int32).at[target].set(place)]
    all_to_all x4 -> x0, starting transfers between devices: 26.6 us -> none  [the longest x1 9.22 us: on_device(): lax.all_to_all(column, 'sub', split_axis=1, concat_axis=2, tiled=True)]
    dot_general x4 -> x0, matrix products: 26.5 us -> none  [the longest x1 11 us: smooth(): return jnp.einsum('vlxj,lyj->vlxy', part, along, precision=high)]
    all_gather x1 -> x0, waiting for transfers between devices: 12.3 us -> none  [on_device(): lax.all_gather(correlated, 'var', axis=0, tiled=True)]
  transfers between devices with their start and end apart: 5 -> 16, of which waited for: 4 -> 4; matrix products, arithmetic and copies ran while one was open for 6% -> 5% of each run, Pallas kernels for 0% -> 7%
where the time goes in v1:
time: 95 us; the launch traced here: 94.4 us
  Pallas kernels  67.2 us (71%)
  starting transfers between devices  11.2 us (12%)
  local copies, waits for them, and re-layouts  7.94 us (8%)
  waiting for transfers between devices  5.42 us (6%)
  other arithmetic  2.51 us (3%)
    pallas_call x1, Pallas kernels, field(): pl.pallas_call(functools.partial(field_kernel, sources, wide, nvar), grid...  58.4 us
    pallas_call x1, Pallas kernels, tables(): pl.pallas_call(table_kernel, grid=(levels // depth,), in_specs=[pl.BlockS...  6.16 us
    unnamed x12, local copies, waits for them, and re-layouts  5.83 us
    ppermute x4, starting transfers between devices, on_device(): lax.ppermute(held, 'sub', [(i, i ^ 1) for i in range(groups)])  5.19 us
    ppermute x3, starting transfers between devices, on_device(): lax.ppermute(unit, 'sub', [(i, (i + k) % groups) for i in range(groups)])  4.61 us
    pallas_call x1, Pallas kernels, route(): pl.pallas_call(route_kernel, out_shape=jax.ShapeDtypeStruct(((nvar + 1) *...  2.67 us
    ppermute x4, waiting for transfers between devices, on_device(): lax.ppermute(held, 'sub', [(i, i ^ 1) for i in range(groups)])  2.62 us
    ppermute x3, waiting for transfers between devices, on_device(): lax.ppermute(unit, 'sub', [(i, (i + k) % groups) for i in range(groups)])  2.05 us
  transfers between devices with their start and end apart: 16, of which 4 were waited for; matrix products, arithmetic and copies ran while one was open for 5% of the time, Pallas kernels for 7%

profile of v1, /device:TPU:0, one launch (start us, length us, event | category | flops | bytes accessed | tf_op | source)
XLA Modules:
  0.0 94.4 jit_solution(1360607419657997116)
XLA Ops:
  0.0 0.8 copy-done.1
  0.8 0.7 copy-done.2
  1.6 0.7 copy-done.3
  2.3 0.7 copy-done.4
  3.0 2.7 %route.1.refs_0_.refs_16_ = f32[168,128]{1,0:T(8,128)S(1)} custom-call(f32[4,4096]{1,0:T(4,128)S(1)} %copy-done.1, s32[32,128]{1,0:T(8,128)S(1)} %bitcast.27, s32[32,128]{1,0:T(8,128)S(1)} %bitcast.28, s32[32,128]{1,0:T(8,128)S(1)} %bitcast.29), custom_call_target="tpu_custom_call" | custom-call | tf_op jit(solution)/shard_map/route/pallas_call | solution.py:83
  5.7 0.5 collective-permute-start.7
  6.2 2.6 %collective-permute-start.3 = (f32[168,128]{1,0:T(8,128)S(1)}, f32[168,128]{1,0:T(8,128)S(1)}, u32[]{:S(2)}, u32[]{:S(2)}) collective-permute-start(f32[168,128]{1,0:T(8,128)S(1)} %route.1.refs_0_.refs_16_), channel_id=1, source_target_pairs={{0,2},{2,0},{4,6},{6,4},{8,10},{10,8},{12,14},{14,12},{1,3},{3,1},... | collective-permute-start | bytes 258056 | tf_op jit(solution)/shard_map/ppermute | solution.py:288
  8.8 3.6 %collective-permute-start.2 = (f32[168,128]{1,0:T(8,128)S(1)}, f32[168,128]{1,0:T(8,128)S(1)}, u32[]{:S(2)}, u32[]{:S(2)}) collective-permute-start(f32[168,128]{1,0:T(8,128)S(1)} %route.1.refs_0_.refs_16_), channel_id=1, source_target_pairs={{0,12},{2,14},{4,0},{6,2},{8,4},{10,6},{12,8},{14,10},{1,13},{3,15... | collective-permute-start | bytes 258056 | tf_op jit(solution)/shard_map/ppermute | solution.py:287
  12.4 0.0 collective-permute-start.1
  12.4 0.0 collective-permute-start.15
  12.4 0.8 fusion.4
  13.2 0.8 maximum_select_fusion
  14.0 0.8 mul.60
  14.7 0.1 sub.31
  14.9 0.1 tile.18
  15.0 6.2 %tables.1 = (bf16[64,128,256]{2,1,0:T(8,128)(2,1)}, bf16[64,128,256]{2,1,0:T(8,128)(2,1)}) custom-call(s32[64]{0:T(128)} %width.3), custom_call_target="tpu_custom_call" | custom-call | tf_op jit(solution)/shard_map/tables/pallas_call | solution.py:117
  21.1 0.0 collective-permute-done.15
  21.1 1.0 %collective-permute-start = (f32[168,128]{1,0:T(8,128)S(1)}, f32[168,128]{1,0:T(8,128)S(1)}, u32[]{:S(2)}, u32[]{:S(2)}) collective-permute-start(f32[168,128]{1,0:T(8,128)S(1)} %route.1.refs_0_.refs_16_), channel_id=1, source_target_pairs={{0,4},{2,6},{4,8},{6,10},{8,12},{10,14},{12,0},{14,2},{1,5},{3,7},... | collective-permute-start | bytes 258056 | tf_op jit(solution)/shard_map/ppermute | solution.py:287
  22.1 0.7 broadcast_multiply_fusion
  22.8 0.1 copy.10
  22.9 0.1 mul.68
  23.0 0.0 collective-permute-done.2.refs_3_.refs_19_
  23.0 0.1 collective-permute-start.10
  23.1 0.6 collective-permute-start.6
  23.7 0.0 collective-permute-done.3.refs_4_.refs_20_
  23.7 0.2 collective-permute-start.11
  23.9 0.0 collective-permute-done.1.refs_2_.refs_18_
  23.9 1.5 %collective-permute-start.5 = (f32[168,128]{1,0:T(8,128)S(1)}, f32[168,128]{1,0:T(8,128)S(1)}, u32[]{:S(2)}, u32[]{:S(2)}) collective-permute-start(f32[168,128]{1,0:T(8,128)S(1)} %collective-permute-done.1.refs_2_.refs_18_), channel_id=1, source_target_pairs={{0,2},{2,0},{4,6},{6,4},{8,10},{10,8},{12,14},{14,12},{1,3},{3,1},... | collective-permute-start | bytes 258056 | tf_op jit(solution)/shard_map/ppermute | solution.py:288
  25.4 2.0 %collective-permute-done.refs_1_.refs_17_ = f32[168,128]{1,0:T(8,128)S(1)} collective-permute-done((f32[168,128]{1,0:T(8,128)S(1)}, f32[168,128]{1,0:T(8,128)S(1)}, u32[]{:S(2)}, u32[]{:S(2)}) %collective-permute-start) | collective-permute-done | bytes 86048 | tf_op jit(solution)/shard_map/ppermute | solution.py:287
  27.4 0.5 collective-permute-start.4
  27.9 0.7 maximum_bitcast_fusion
  28.6 0.0 collective-permute-done.11.refs_12_
  28.6 0.1 collective-permute-start.9
  28.7 0.0 collective-permute-done.10.refs_11_
  28.7 0.5 collective-permute-start.8
  29.2 0.1 collective-permute-start.14
  29.3 1.1 %collective-permute-done.5.refs_6_.refs_22_ = f32[168,128]{1,0:T(8,128)S(1)} collective-permute-done((f32[168,128]{1,0:T(8,128)S(1)}, f32[168,128]{1,0:T(8,128)S(1)}, u32[]{:S(2)}, u32[]{:S(2)}) %collective-permute-start.5) | collective-permute-done | bytes 86048 | tf_op jit(solution)/shard_map/ppermute | solution.py:288
  30.4 1.5 %collective-permute-done.4.refs_5_.refs_21_ = f32[168,128]{1,0:T(8,128)S(1)} collective-permute-done((f32[168,128]{1,0:T(8,128)S(1)}, f32[168,128]{1,0:T(8,128)S(1)}, u32[]{:S(2)}, u32[]{:S(2)}) %collective-permute-start.4) | collective-permute-done | bytes 86048 | tf_op jit(solution)/shard_map/ppermute | solution.py:288
  31.9 0.0 collective-permute-start.12
  31.9 0.2 fusion.3
  32.1 0.1 copy.11
  32.3 0.2 fusion
  32.4 0.0 collective-permute-done.8.refs_9_
  32.4 0.0 collective-permute-done.14.refs_15_
  32.5 0.7 collective-permute-done.12.refs_13_
  33.2 2.2 %copy-done = bf16[64,128,256]{2,1,0:T(8,128)(2,1)S(1)} copy-done((bf16[64,128,256]{2,1,0:T(8,128)(2,1)S(1)}, bf16[64,128,256]{2,1,0:T(8,128)(2,1)}, u32[]{:S(2)}) %copy-start) | copy-done | bytes 4194328
  35.4 0.7 copy-done.5
  36.0 58.4 %field.1 = f32[256,4,512]{2,1,0:T(4,128)} custom-call(s32[64]{0:T(128)S(1)} %copy-done.5, s32[1]{0:T(128)} %bitcast.first, f32[168,128]{1,0:T(8,128)S(1)} %route.1.refs_0_.refs_16_, f32[168,128]{1,0:T(8,128)S(1)} %collective-permute-done.refs_1_.refs_17_, f32[168,128]{1,0:T(8,128)S(1)} %collective-permute-done.1.refs_2_.refs_18_, ...), custom_call_target="tpu_custom_call" | custom-call | tf_op jit(solution)/shard_map/field/pallas_call | solution.py:261
  (13 shorter events, 0.0 us)
Async XLA Ops:
  0.0 0.8 copy-start.1
  0.8 0.7 copy-start.2
  1.6 0.7 copy-start.3
  2.3 0.7 copy-start.4
  5.7 17.4 %collective-permute-start.7 = (f32[168,128]{1,0:T(8,128)S(1)}, f32[168,128]{1,0:T(8,128)S(1)}, u32[]{:S(2)}, u32[]{:S(2)}) collective-permute-start(f32[168,128]{1,0:T(8,128)S(1)} %route.1.refs_0_.refs_16_), channel_id=1, source_target_pairs={{0,1},{1,0},{2,3},{3,2},{4,5},{5,4},{6,7},{7,6},{8,9},{9,8},{10,11... | collective-permute-start | bytes 258056 | tf_op jit(solution)/shard_map/ppermute | solution.py:289
  6.2 17.5 %collective-permute-start.3 = (f32[168,128]{1,0:T(8,128)S(1)}, f32[168,128]{1,0:T(8,128)S(1)}, u32[]{:S(2)}, u32[]{:S(2)}) collective-permute-start(f32[168,128]{1,0:T(8,128)S(1)} %route.1.refs_0_.refs_16_), channel_id=1, source_target_pairs={{0,2},{2,0},{4,6},{6,4},{8,10},{10,8},{12,14},{14,12},{1,3},{3,1},... | collective-permute-start | bytes 258056 | tf_op jit(solution)/shard_map/ppermute | solution.py:288
  8.8 14.2 %collective-permute-start.2 = (f32[168,128]{1,0:T(8,128)S(1)}, f32[168,128]{1,0:T(8,128)S(1)}, u32[]{:S(2)}, u32[]{:S(2)}) collective-permute-start(f32[168,128]{1,0:T(8,128)S(1)} %route.1.refs_0_.refs_16_), channel_id=1, source_target_pairs={{0,12},{2,14},{4,0},{6,2},{8,4},{10,6},{12,8},{14,10},{1,13},{3,15... | collective-permute-start | bytes 258056 | tf_op jit(solution)/shard_map/ppermute | solution.py:287
  12.4 11.5 %collective-permute-start.1 = (f32[168,128]{1,0:T(8,128)S(1)}, f32[168,128]{1,0:T(8,128)S(1)}, u32[]{:S(2)}, u32[]{:S(2)}) collective-permute-start(f32[168,128]{1,0:T(8,128)S(1)} %route.1.refs_0_.refs_16_), channel_id=1, source_target_pairs={{0,8},{2,10},{4,12},{6,14},{8,0},{10,2},{12,4},{14,6},{1,9},{3,11}... | collective-permute-start | bytes 258056 | tf_op jit(solution)/shard_map/ppermute | solution.py:287
  12.4 8.7 %collective-permute-start.15 = (f32[4,64]{1,0:T(4,128)}, f32[4,64]{1,0:T(4,128)S(1)}, u32[]{:S(2)}, u32[]{:S(2)}) collective-permute-start(f32[4,64]{1,0:T(4,128)} %param.13), channel_id=1, source_target_pairs={{0,1},{1,0},{2,3},{3,2},{4,5},{5,4},{6,7},{7,6},{8,9},{9,8},{10,11... | collective-permute-start | bytes 3080 | tf_op jit(solution)/shard_map/ppermute | solution.py:290
  21.1 6.3 %collective-permute-start = (f32[168,128]{1,0:T(8,128)S(1)}, f32[168,128]{1,0:T(8,128)S(1)}, u32[]{:S(2)}, u32[]{:S(2)}) collective-permute-start(f32[168,128]{1,0:T(8,128)S(1)} %route.1.refs_0_.refs_16_), channel_id=1, source_target_pairs={{0,4},{2,6},{4,8},{6,10},{8,12},{10,14},{12,0},{14,2},{1,5},{3,7},... | collective-permute-start | bytes 258056 | tf_op jit(solution)/shard_map/ppermute | solution.py:287
  23.0 5.7 %collective-permute-start.10 = (f32[168,128]{1,0:T(8,128)S(1)}, f32[168,128]{1,0:T(8,128)S(1)}, u32[]{:S(2)}, u32[]{:S(2)}) collective-permute-start(f32[168,128]{1,0:T(8,128)S(1)} %collective-permute-done.2.refs_3_.refs_19_), channel_id=1, source_target_pairs={{0,1},{1,0},{2,3},{3,2},{4,5},{5,4},{6,7},{7,6},{8,9},{9,8},{10,11... | collective-permute-start | bytes 258056 | tf_op jit(solution)/shard_map/ppermute | solution.py:289
  23.1 6.1 %collective-permute-start.6 = (f32[168,128]{1,0:T(8,128)S(1)}, f32[168,128]{1,0:T(8,128)S(1)}, u32[]{:S(2)}, u32[]{:S(2)}) collective-permute-start(f32[168,128]{1,0:T(8,128)S(1)} %collective-permute-done.2.refs_3_.refs_19_), channel_id=1, source_target_pairs={{0,2},{2,0},{4,6},{6,4},{8,10},{10,8},{12,14},{14,12},{1,3},{3,1},... | collective-permute-start | bytes 258056 | tf_op jit(solution)/shard_map/ppermute | solution.py:288
  23.7 4.9 %collective-permute-start.11 = (f32[168,128]{1,0:T(8,128)S(1)}, f32[168,128]{1,0:T(8,128)S(1)}, u32[]{:S(2)}, u32[]{:S(2)}) collective-permute-start(f32[168,128]{1,0:T(8,128)S(1)} %collective-permute-done.3.refs_4_.refs_20_), channel_id=1, source_target_pairs={{0,1},{1,0},{2,3},{3,2},{4,5},{5,4},{6,7},{7,6},{8,9},{9,8},{10,11... | collective-permute-start | bytes 258056 | tf_op jit(solution)/shard_map/ppermute | solution.py:289
  23.9 6.5 %collective-permute-start.5 = (f32[168,128]{1,0:T(8,128)S(1)}, f32[168,128]{1,0:T(8,128)S(1)}, u32[]{:S(2)}, u32[]{:S(2)}) collective-permute-start(f32[168,128]{1,0:T(8,128)S(1)} %collective-permute-done.1.refs_2_.refs_18_), channel_id=1, source_target_pairs={{0,2},{2,0},{4,6},{6,4},{8,10},{10,8},{12,14},{14,12},{1,3},{3,1},... | collective-permute-start | bytes 258056 | tf_op jit(solution)/shard_map/ppermute | solution.py:288
  27.4 4.5 %collective-permute-start.4 = (f32[168,128]{1,0:T(8,128)S(1)}, f32[168,128]{1,0:T(8,128)S(1)}, u32[]{:S(2)}, u32[]{:S(2)}) collective-permute-start(f32[168,128]{1,0:T(8,128)S(1)} %collective-permute-done.refs_1_.refs_17_), channel_id=1, source_target_pairs={{0,2},{2,0},{4,6},{6,4},{8,10},{10,8},{12,14},{14,12},{1,3},{3,1},... | collective-permute-start | bytes 258056 | tf_op jit(solution)/shard_map/ppermute | solution.py:288
  28.6 3.8 %collective-permute-start.9 = (f32[168,128]{1,0:T(8,128)S(1)}, f32[168,128]{1,0:T(8,128)S(1)}, u32[]{:S(2)}, u32[]{:S(2)}) collective-permute-start(f32[168,128]{1,0:T(8,128)S(1)} %collective-permute-done.1.refs_2_.refs_18_), channel_id=1, source_target_pairs={{0,1},{1,0},{2,3},{3,2},{4,5},{5,4},{6,7},{7,6},{8,9},{9,8},{10,11... | collective-permute-start | bytes 258056 | tf_op jit(solution)/shard_map/ppermute | solution.py:289
  28.7 3.7 %collective-permute-start.8 = (f32[168,128]{1,0:T(8,128)S(1)}, f32[168,128]{1,0:T(8,128)S(1)}, u32[]{:S(2)}, u32[]{:S(2)}) collective-permute-start(f32[168,128]{1,0:T(8,128)S(1)} %collective-permute-done.refs_1_.refs_17_), channel_id=1, source_target_pairs={{0,1},{1,0},{2,3},{3,2},{4,5},{5,4},{6,7},{7,6},{8,9},{9,8},{10,11... | collective-permute-start | bytes 258056 | tf_op jit(solution)/shard_map/ppermute | solution.py:289
  29.2 3.2 %collective-permute-start.14 = (f32[168,128]{1,0:T(8,128)S(1)}, f32[168,128]{1,0:T(8,128)S(1)}, u32[]{:S(2)}, u32[]{:S(2)}) collective-permute-start(f32[168,128]{1,0:T(8,128)S(1)} %collective-permute-done.6.refs_7_.refs_23_), channel_id=1, source_target_pairs={{0,1},{1,0},{2,3},{3,2},{4,5},{5,4},{6,7},{7,6},{8,9},{9,8},{10,11... | collective-permute-start | bytes 258056 | tf_op jit(solution)/shard_map/ppermute | solution.py:289
  30.4 2.1 %collective-permute-start.13 = (f32[168,128]{1,0:T(8,128)S(1)}, f32[168,128]{1,0:T(8,128)S(1)}, u32[]{:S(2)}, u32[]{:S(2)}) collective-permute-start(f32[168,128]{1,0:T(8,128)S(1)} %collective-permute-done.5.refs_6_.refs_22_), channel_id=1, source_target_pairs={{0,1},{1,0},{2,3},{3,2},{4,5},{5,4},{6,7},{7,6},{8,9},{9,8},{10,11... | collective-permute-start | bytes 258056 | tf_op jit(solution)/shard_map/ppermute | solution.py:289
  31.9 1.3 %collective-permute-start.12 = (f32[168,128]{1,0:T(8,128)S(1)}, f32[168,128]{1,0:T(8,128)S(1)}, u32[]{:S(2)}, u32[]{:S(2)}) collective-permute-start(f32[168,128]{1,0:T(8,128)S(1)} %collective-permute-done.4.refs_5_.refs_21_), channel_id=1, source_target_pairs={{0,1},{1,0},{2,3},{3,2},{4,5},{5,4},{6,7},{7,6},{8,9},{9,8},{10,11... | collective-permute-start | bytes 258056 | tf_op jit(solution)/shard_map/ppermute | solution.py:289
  33.2 2.2 %copy-start = (bf16[64,128,256]{2,1,0:T(8,128)(2,1)S(1)}, bf16[64,128,256]{2,1,0:T(8,128)(2,1)}, u32[]{:S(2)}) copy-start(bf16[64,128,256]{2,1,0:T(8,128)(2,1)} %get-tuple-element.7.refs_24_) | copy-start | bytes 12582916
  35.4 0.7 copy-start.5

commit v2 on v1

v2 whole, which is shorter than its diff:
```python
import functools

import jax
import jax.numpy as jnp
from jax import lax
from jax.experimental import pallas as pl
from jax.experimental.pallas import tpu as pltpu
from jax.sharding import PartitionSpec as P

VB = 6
NX_DEV = 4
NY = 512
LANES = 128
HALF = 256
F32 = jnp.float32
BF16 = jnp.bfloat16


def nt_dot(a, b):
    return lax.dot_general(a, b, (((1,), (1,)), ((), ())), preferred_element_type=F32)


def nn_dot(a, b):
    return jnp.dot(a, b, preferred_element_type=F32)


def iota(shape, dim):
    return lax.broadcasted_iota(jnp.int32, shape, dim)


def route_kernel(inn, level, owner, local, pay, hot, pre, dest, left, right):
    nvar, nobs = inn.shape
    chunks = nobs // LANES
    levels = hot.shape[0] // chunks
    rows = iota((levels, LANES), 0)
    for c in range(chunks):
        hit = jnp.where(rows == level[c : c + 1, :], 1.0, 0.0)
        hot[c * levels : (c + 1) * levels, :] = hit.astype(BF16)
    before = iota((LANES, 2 * LANES), 0) < iota((LANES, 2 * LANES), 1)
    pre[...] = nn_dot(hot[...], jnp.where(before, 1.0, 0.0).astype(BF16))
    count = jnp.zeros((levels, LANES), F32)
    for c in range(chunks):
        count = count + pre[c * levels : (c + 1) * levels, LANES:]
    lower = iota((levels, levels), 1) < iota((levels, levels), 0)
    base = nn_dot(jnp.where(lower, 1.0, 0.0).astype(BF16), count.astype(BF16))
    lane = iota((levels, LANES), 1)
    starts = jnp.sum(jnp.where(lane == rows, base, 0.0), 0, keepdims=True)
    starts = jnp.where(iota((8, LANES), 1) < levels, starts, float(nobs))
    for c in range(chunks):
        part = pre[c * levels : (c + 1) * levels, :]
        slot = jnp.where(rows == level[c : c + 1, :], part[:, :LANES] + base, 0.0)
        dest[c : c + 1, :] = jnp.sum(slot, 0, keepdims=True).astype(jnp.int32)
        base = base + part[:, LANES:]
    place = owner[...] * (NX_DEV * NY) + local[...]
    rows_hi, rows_lo = iota((chunks, LANES), 0), iota((LANES, LANES), 0)
    for c in range(chunks):
        at = slice(c * LANES, (c + 1) * LANES)
        slot = dest[c : c + 1, :]
        mask = rows_hi == slot // LANES
        right[:, at] = jnp.where(rows_lo == slot % LANES, 1.0, 0.0).astype(BF16)
        pieces = []
        for v in range(nvar):
            value = inn[v : v + 1, at]
            high = value.astype(BF16).astype(F32)
            pieces += [high, value - high]
        spot = place[c : c + 1, :]
        pieces += [(spot // HALF).astype(F32), (spot % HALF).astype(F32)]
        for q, piece in enumerate(pieces):
            left[q * chunks : (q + 1) * chunks, at] = jnp.where(mask, piece, 0.0).astype(BF16)
    packed = nt_dot(left[...], right[...])
    for v in range(nvar):
        both = packed[2 * v * chunks : (2 * v + 1) * chunks] + packed[(2 * v + 1) * chunks : (2 * v + 2) * chunks]
        pay[pl.ds(v, chunks, stride=nvar), :] = both
    high, low = packed[2 * nvar * chunks : (2 * nvar + 1) * chunks], packed[(2 * nvar + 1) * chunks :]
    pay[nvar * chunks : (nvar + 1) * chunks, :] = high * float(HALF) + low
    pay[(nvar + 1) * chunks :, :] = starts


def route(innovations, owner, level, local, levels):
    nvar, nobs = innovations.shape
    chunks = nobs // LANES
    pieces = 2 * nvar + 2
    return pl.pallas_call(
        route_kernel,
        out_shape=jax.ShapeDtypeStruct(((nvar + 1) * chunks + 8, LANES), F32),
        scratch_shapes=[
            pltpu.VMEM((chunks * levels, LANES), BF16),
            pltpu.VMEM((chunks * levels, 2 * LANES), F32),
            pltpu.VMEM((chunks, LANES), jnp.int32),
            pltpu.VMEM((pieces * chunks, nobs), BF16),
            pltpu.VMEM((LANES, nobs), BF16),
        ],
        compiler_params=pltpu.CompilerParams(vmem_limit_bytes=32 << 20),
        name="route",
    )(innovations, level.reshape(chunks, LANES), owner.reshape(chunks, LANES), local.reshape(chunks, LANES))


def table_kernel(width, base, high, low):
    depth = high.shape[0]
    row, col = iota((LANES, LANES), 0), iota((LANES, LANES), 1)
    near = jnp.abs(row - col).astype(F32)
    far = jnp.where(col < LANES // 2, LANES - row, row + 1).astype(F32)
    for k in range(depth):
        rate = width[base[0] + pl.program_id(0) * depth + k].astype(F32)
        for at, dist in ((0, near), (LANES, far)):
            full = jnp.exp(-dist / rate)
            top = full.astype(BF16)
            high[k, :, at : at + LANES] = top
            low[k, :, at : at + LANES] = (full - top.astype(F32)).astype(BF16)


def tables(band_width, base, levels):
    depth = 8
    spec = pl.BlockSpec((depth, LANES, 2 * LANES), lambda i: (i, 0, 0))
    shape = jax.ShapeDtypeStruct((levels, LANES, 2 * LANES), BF16)
    return pl.pallas_call(
        table_kernel,
        grid=(levels // depth,),
        in_specs=[pl.BlockSpec(memory_space=pltpu.SMEM)] * 2,
        out_specs=(spec, spec),
        out_shape=(shape, shape),
        name="tables",
    )(band_width, base)


def mix_matrix(scale, sigma, weights, base, depth):
    nvar, levels = scale.shape
    level = base + jnp.arange(depth)
    dist = jnp.arange(levels)[:, None] - jnp.repeat(level, nvar)[None, :]
    own = jnp.tile(scale.T, (1, depth))
    other = lax.dynamic_slice_in_dim(scale, base, depth, 1).T.reshape(1, -1)
    gap = dist.astype(F32)
    corr = jnp.exp(-gap * gap / (2.0 * own * other))
    corr = jnp.where(jnp.abs(dist) <= VB, corr, F32(0.0))
    mix = sigma[:, :, None] * jnp.tile(weights, (1, depth))[:, None, :] * corr[None]
    mix = mix.reshape(-1, depth * nvar)
    high = lax.reduce_precision(mix, 8, 7)
    return high.astype(BF16), (mix - high).astype(BF16)


def gather_levels(sources, nvar, chunks, base, levels, own, oth, marks, vals, spots, queue, queue_spot, level_of, total):
    lane = iota((8, LANES), 1)
    sub = iota((8, LANES), 0)
    for s in range(sources):
        for c in range(0, chunks, 2):
            here, there = own[s][4 * c : 4 * c + 8, :], oth[s][4 * c : 4 * c + 8, :]
            vals[s, 8 * c : 8 * c + 8, :] = jnp.where(sub < 4, here, pltpu.roll(there, 4, 0))
            vals[s, 8 * c + 8 : 8 * c + 16, :] = jnp.where(sub < 4, pltpu.roll(here, 4, 0), there)
        vals[s, 8 * chunks :, :] = jnp.zeros((8, LANES), F32)
        spots[s, :chunks, :] = own[s][nvar * chunks : (nvar + 1) * chunks, :]
        spots[s, chunks:, :] = jnp.zeros((8, LANES), F32)
    nothing = jnp.zeros((8, LANES), F32)

    def rows(chunk):
        return pl.ds(pl.multiple_of(8 * chunk, 8), 8)

    def per_level(k, pair):
        lev = base + k
        held, held_spot = nothing, nothing
        end = jnp.int32(0)
        for s in range(sources):
            start = marks[s][0, lev].astype(jnp.int32)
            size = marks[s][0, lev + 1].astype(jnp.int32) - start
            c, off = jnp.minimum(start >> 7, chunks - 1), start & (LANES - 1)
            put = end & (LANES - 1)
            turn = (put - off) & (LANES - 1)
            value = jnp.where(lane >= off, vals[s, rows(c), :], vals[s, rows(c + 1), :])
            value = pltpu.roll(value, turn, 1)
            spot = jnp.where(lane[:1] >= off, spots[s, pl.ds(c, 1), :], spots[s, pl.ds(c + 1, 1), :])
            spot = pltpu.roll(jnp.broadcast_to(spot, (8, LANES)), turn, 1)
            fresh = (lane >= put) & (lane < put + size)
            held = jnp.where(fresh, value, held)
            held_spot = jnp.where(fresh, spot, held_spot)
            at = rows(2 * pair + (end >> 7))
            queue[at, :] = held
            queue_spot[at, :] = held_spot
            over = put + size - LANES
            late = lane < over
            held = jnp.where(over >= 0, jnp.where(late, value, 0.0), held)
            held_spot = jnp.where(over >= 0, jnp.where(late, spot, 0.0), held_spot)
            end = end + size
        at = 2 * pair + (end >> 7)
        queue[rows(at), :] = held
        queue_spot[rows(at), :] = held_spot
        queue[rows(at + 1), :] = nothing
        queue_spot[rows(at + 1), :] = nothing
        pairs = (end + 2 * LANES - 1) >> 8

        def note(p, carry):
            level_of[pair + p] = k
            return carry

        lax.fori_loop(0, pairs, note, 0)
        return pair + pairs

    pair = lax.fori_loop(0, levels, per_level, jnp.int32(0))
    for p in range(UNROLL):
        level_of[pair + p] = levels
        for h in range(2):
            queue[rows(2 * (pair + p) + h), :] = nothing
            queue_spot[rows(2 * (pair + p) + h), :] = nothing
    total[0] = pair


UNROLL = 4


def spread(wide, levels, base, width, first, queue, queue_spot, level_of, total, field):
    sub = iota((8, LANES), 0)
    col = first[0] + sub % 4
    reach = jnp.where(sub < 4, col, 2 * wide - col).astype(F32)
    tall = iota((HALF, LANES), 0).astype(F32).astype(BF16)
    one, zero = jnp.ones((HALF, LANES), BF16), jnp.zeros((HALF, LANES), BF16)

    def clear(k, carry):
        field[k] = jnp.zeros(field.shape[1:], F32)
        return carry

    lax.fori_loop(0, levels + 1, clear, 0)

    def group(g, carry):
        for p in range(UNROLL):
            pair = g * UNROLL + p
            k = level_of[pair]
            rate = width[base + jnp.minimum(k, levels - 1)].astype(F32)
            slope = -1.0 / jnp.full((8, LANES), rate, F32)
            lefts, rights = [], []
            for h in range(2):
                at = pl.ds(pl.multiple_of(8 * (2 * pair + h), 8), 8)
                value = queue[at, :]
                spot = queue_spot[at, :].astype(jnp.int32)
                xpos = (spot >> 9).astype(F32)
                side = ((spot >> 8) & 1).astype(F32)
                ypos = (spot & (HALF - 1)).astype(F32)
                gain = jnp.exp(jnp.abs(reach - xpos) * slope)
                gain = gain - pltpu.roll(gain, 4, 0)
                upper = jnp.concatenate([side, side], 0).astype(BF16)
                lower = jnp.concatenate([1.0 - side, 1.0 - side], 0).astype(BF16)
                tiles = []
                for x in range(NX_DEV):
                    term = value * jnp.broadcast_to(gain[x : x + 1, :], (8, LANES))
                    top = term.astype(BF16).astype(F32)
                    both = jnp.concatenate([top, term - top], 0).astype(BF16)
                    tiles += [both * lower, both * upper]
                lefts.append(jnp.concatenate(tiles, 0))
                mark = jnp.broadcast_to(ypos[:1], (HALF, LANES)).astype(BF16)
                rights.append(jnp.where(tall == mark, one, zero))
            done = nt_dot(jnp.concatenate(lefts, 1), jnp.concatenate(rights, 1))
            parts = [done[16 * i : 16 * i + 8] + done[16 * i + 8 : 16 * i + 16] for i in range(2 * NX_DEV)]
            field[k] = field[k] + jnp.concatenate(parts, 0)
        return carry

    lax.fori_loop(0, (total[0] + UNROLL - 1) // UNROLL, group, 0)


def filter_levels(levels, base, width, high, low, field, slab):
    lane = iota((8, LANES), 1)
    line = lane.astype(F32)

    def one_level(k):
        slope = -1.0 / jnp.full((8, LANES), width[base + k].astype(F32), F32)
        grid = field[k]
        blocks = []
        for i in range(2 * NX_DEV):
            blocks += [grid[8 * i : 8 * i + 8, :LANES], grid[8 * i : 8 * i + 8, LANES:]]
        grid = jnp.concatenate(blocks, 0)
        top = grid.astype(BF16)
        rest = (grid - top.astype(F32)).astype(BF16)
        mat = high[k]
        done = nn_dot(jnp.concatenate([top, rest], 1), jnp.concatenate([mat, mat], 0)) + nn_dot(top, low[k])
        rise = jnp.exp(line * slope)
        fall = jnp.exp((LANES - 1.0 - line) * slope)
        edge = jnp.exp((LANES - line) * slope)
        hop = jnp.exp(LANES * slope)
        for x in range(NX_DEV):
            ahead, behind, here = [], [], []
            for b in range(4):
                row = (4 * x + b) * 8
                here.append(done[row : row + 8, :LANES])
                moments = done[row : row + 8, LANES:]
                turned = pltpu.roll(moments, LANES // 2, 1)
                ahead.append(jnp.where(lane < LANES // 2, moments, turned))
                behind.append(jnp.where(lane < LANES // 2, turned, moments))
            run = ahead[0]
            for b in range(1, 4):
                here[b] = here[b] + rise * run
                run = ahead[b] + hop * run
            bound = edge * run
            run = behind[3]
            for b in (2, 1, 0):
                here[b] = here[b] + fall * run
                run = behind[b] + hop * run
            for b in (3, 2, 1, 0):
                slab[4 * x + b, pl.ds(pl.multiple_of(8 * k, 8), 8), :] = here[b] - bound
                bound = bound * hop

    def group(g, carry):
        for p in range(2):
            one_level(2 * g + p)
        return carry

    lax.fori_loop(0, levels // 2, group, 0)


def field_kernel(sources, wide, nvar, width, first, start, *refs):
    own, oth, marks = refs[:sources], refs[sources : 2 * sources], refs[2 * sources : 3 * sources]
    high, low, slab, vals, spots, queue, queue_spot, level_of, total, field = refs[3 * sources :]
    chunks = (own[0].shape[0] - 8) // (nvar + 1)
    levels = high.shape[0]
    base = start[0]
    gather_levels(
        sources, nvar, chunks, base, levels, own, oth, marks, vals, spots, queue, queue_spot, level_of, total
    )
    spread(wide, levels, base, width, first, queue, queue_spot, level_of, total, field)
    filter_levels(levels, base, width, high, low, field, slab)


def make_field(own, oth, band_width, first, base, high, low, nvar, levels, wide):
    sources = len(own)
    rows = own[0].shape[0]
    chunks = (rows - 8) // (nvar + 1)
    whole = pl.BlockSpec(memory_space=pltpu.VMEM)
    marks = pl.BlockSpec((8, LANES), lambda i: (rows // 8 - 1, 0), memory_space=pltpu.SMEM)
    smem = pl.BlockSpec(memory_space=pltpu.SMEM)
    pairs = levels * sources // 2 + UNROLL + 1
    return pl.pallas_call(
        functools.partial(field_kernel, sources, wide, nvar),
        grid=(1,),
        in_specs=[smem] * 3 + [whole] * (2 * sources) + [marks] * sources + [whole] * 2,
        out_specs=whole,
        out_shape=jax.ShapeDtypeStruct((4 * NX_DEV, 2 * nvar * levels, LANES), F32),
        scratch_shapes=[
            pltpu.VMEM((sources, 8 * chunks + 8, LANES), F32),
            pltpu.VMEM((sources, chunks + 8, LANES), F32),
            pltpu.VMEM((16 * pairs, LANES), F32),
            pltpu.VMEM((16 * pairs, LANES), F32),
            pltpu.SMEM((pairs,), jnp.int32),
            pltpu.SMEM((1,), jnp.int32),
            pltpu.VMEM((levels + 1, 16 * NX_DEV, HALF), F32),
        ],
        compiler_params=pltpu.CompilerParams(vmem_limit_bytes=48 << 20),
        name="field",
    )(band_width, first, base, *own, *oth, *own, high, low)


def mix_kernel(own, oth, own_high, own_low, oth_high, oth_low, out):
    for x in range(NX_DEV):
        for h in range(2):
            total = None
            for slab, high, low in ((own, own_high, own_low), (oth, oth_high, oth_low)):
                part = jnp.concatenate([slab[4 * x + 2 * h], slab[4 * x + 2 * h + 1]], 1)
                top = part.astype(BF16)
                rest = (part - top.astype(F32)).astype(BF16)
                term = nn_dot(high[...], top) + nn_dot(high[...], rest) + nn_dot(low[...], top)
                total = term if total is None else total + term
            for g in range(2):
                rows = pl.ds(8 * h + 4 * g + x, total.shape[0], stride=4 * NX_DEV)
                out[rows, :] = total[:, g * LANES : (g + 1) * LANES]


def mix(own, oth, own_mats, oth_mats):
    rows = own_mats[0].shape[0]
    return pl.pallas_call(
        mix_kernel,
        out_shape=jax.ShapeDtypeStruct((rows * NX_DEV * NY // LANES, LANES), F32),
        compiler_params=pltpu.CompilerParams(vmem_limit_bytes=32 << 20),
        name="mix",
    )(own, oth, *own_mats, *oth_mats)


def on_device(innovations, obs_owner, obs_local, obs_level, band_width, vert_scale, sigma, balance):
    groups = lax.axis_size("sub")
    nvar, _ = innovations.shape
    levels = band_width.shape[0]
    swap = [(0, 1), (1, 0)]
    unit = route(innovations, obs_owner, obs_level, obs_local, levels)
    own = [unit]
    for k in range(2, groups, 2):
        own.append(lax.ppermute(unit, "sub", [(i, (i + k) % groups) for i in range(groups)]))
    own += [lax.ppermute(held, "sub", [(i, i ^ 1) for i in range(groups)]) for held in own]
    oth = [lax.ppermute(held, "var", swap) for held in own]
    side = lax.axis_index("var").astype(jnp.int32)
    half = levels // 2
    base, last = half * side, half * (1 - side)
    theirs = lax.ppermute(vert_scale, "var", swap)
    weights = jnp.where(side == 0, balance, jnp.roll(balance, nvar, 1))
    own_mats = mix_matrix(jnp.concatenate([vert_scale, theirs], 0), sigma, weights, base, half)
    oth_mats = mix_matrix(jnp.concatenate([theirs, vert_scale], 0), sigma, jnp.roll(weights, nvar, 1), last, half)
    first = (lax.axis_index("sub") * NX_DEV).astype(jnp.int32).reshape(1)
    base = base.reshape(1)
    high, low = tables(band_width, base, half)
    slab = make_field(own, oth, band_width, first, base, high, low, nvar, half, NX_DEV * groups)
    out = mix(slab, lax.ppermute(slab, "var", swap), own_mats, oth_mats)
    out = out.reshape(nvar, levels, NY // LANES, NX_DEV, LANES)
    return jnp.swapaxes(out, 2, 3).reshape(nvar, levels, NX_DEV, NY)


def solution(mesh):
    in_specs = (
        P("var", ("member", "sub")),
        P(("member", "sub"), None),
        P(("member", "sub")),
        P(("member", "sub"), None),
        P(),
        P("var", None),
        P("var", None),
        P("var", None),
    )
    out_specs = P("var", None, ("member", "sub"), None)
    return jax.shard_map(on_device, mesh=mesh, in_specs=in_specs, out_specs=out_specs, check_vma=False)
```

time: 95 us -> 58.7 us (0.62)
  Pallas kernels: 67.2 us -> 29.2 us
  starting transfers between devices: 11.2 us -> 13.7 us
  waiting for transfers between devices: 5.42 us -> 7.89 us
  other arithmetic: 2.51 us -> 0.71 us
  local copies, waits for them, and re-layouts: 7.94 us -> 6.49 us
    pallas_call x1 -> x2, Pallas kernels: 58.4 us -> 22.9 us  [the longest x1 17.8 us: make_field(): pl.pallas_call(functools.partial(field_kernel, sources, wide, nvar), grid...]
    ppermute x1 -> x2, waiting for transfers between devices: 0.01 us -> 2.68 us  [the longest x1 2.67 us: on_device(): theirs = lax.ppermute(vert_scale, 'var', swap)]
    pallas_call x1, Pallas kernels: 6.16 us -> 3.55 us  [tables(): pl.pallas_call(table_kernel, grid=(levels // depth,), in_specs=[pl.BlockS...]
    ppermute x3, starting transfers between devices: 4.61 us -> 7.01 us  [on_device(): lax.ppermute(unit, 'sub', [(i, (i + k) % groups) for i in range(groups)])]
    ppermute x4, waiting for transfers between devices: 2.62 us -> 3.71 us  [on_device(): lax.ppermute(held, 'sub', [(i, i ^ 1) for i in range(groups)])]
    unnamed x12 -> x18, local copies, waits for them, and re-layouts: 5.83 us -> 5.24 us
  transfers between devices with their start and end apart: 16 -> 17, of which waited for: 4 -> 4; matrix products, arithmetic and copies ran while one was open for 5% -> 3% of each run, Pallas kernels for 7% -> 6%
where the time goes in v2:
time: 58.7 us; the launch traced here: 58.1 us
  Pallas kernels  29.2 us (50%)
  starting transfers between devices  13.7 us (23%)
  waiting for transfers between devices  7.89 us (13%)
  local copies, waits for them, and re-layouts  6.49 us (11%)
  other arithmetic  0.71 us (1%)
    pallas_call x1, Pallas kernels, make_field(): pl.pallas_call(functools.partial(field_kernel, sources, wide, nvar), grid...  17.8 us
    ppermute x3, starting transfers between devices, on_device(): lax.ppermute(unit, 'sub', [(i, (i + k) % groups) for i in range(groups)])  7.01 us
    unnamed x18, local copies, waits for them, and re-layouts  5.24 us
    pallas_call x1, Pallas kernels, mix(): pl.pallas_call(mix_kernel, out_shape=jax.ShapeDtypeStruct((rows * NX_DEV...  5.19 us
    ppermute x4, starting transfers between devices, on_device(): lax.ppermute(held, 'sub', [(i, i ^ 1) for i in range(groups)])  4.95 us
    ppermute x4, waiting for transfers between devices, on_device(): lax.ppermute(held, 'sub', [(i, i ^ 1) for i in range(groups)])  3.71 us
    pallas_call x1, Pallas kernels, tables(): pl.pallas_call(table_kernel, grid=(levels // depth,), in_specs=[pl.BlockS...  3.55 us
    ppermute x1, waiting for transfers between devices, on_device(): theirs = lax.ppermute(vert_scale, 'var', swap)  2.67 us
  transfers between devices with their start and end apart: 17, of which 4 were waited for; matrix products, arithmetic and copies ran while one was open for 3% of the time, Pallas kernels for 6%

profile of v2, /device:TPU:0, one launch (start us, length us, event | category | flops | bytes accessed | tf_op | source)
XLA Modules:
  0.0 58.1 jit_solution(13065808430852779663)
XLA Ops:
  0.0 0.8 %copy-done.1 = f32[4,4096]{1,0:T(4,128)S(1)} copy-done((f32[4,4096]{1,0:T(4,128)S(1)}, f32[4,4096]{1,0:T(4,128)}, u32[]{:S(2)}) %copy-start.1) | copy-done | bytes 65560
  0.8 0.7 %copy-done.2 = s32[4096,1]{0,1:T(1,128)S(1)} copy-done((s32[4096,1]{0,1:T(1,128)S(1)}, s32[4096,1]{0,1:T(1,128)}, u32[]{:S(2)}) %copy-start.2) | copy-done | bytes 16408
  1.6 0.7 %copy-done.3 = s32[4096,1]{0,1:T(1,128)S(1)} copy-done((s32[4096,1]{0,1:T(1,128)S(1)}, s32[4096,1]{0,1:T(1,128)}, u32[]{:S(2)}) %copy-start.3) | copy-done | bytes 16408
  2.3 0.7 %copy-done.4 = s32[4096]{0:T(1024)S(1)} copy-done((s32[4096]{0:T(1024)S(1)}, s32[4096]{0:T(1024)}, u32[]{:S(2)}) %copy-start.4) | copy-done | bytes 16408
  3.0 2.7 %route.1.refs_0_.refs_16_ = f32[168,128]{1,0:T(8,128)S(1)} custom-call(f32[4,4096]{1,0:T(4,128)S(1)} %copy-done.1, s32[32,128]{1,0:T(8,128)S(1)} %bitcast.54, s32[32,128]{1,0:T(8,128)S(1)} %bitcast.55, s32[32,128]{1,0:T(8,128)S(1)} %bitcast.56), custom_call_target="tpu_custom_call" | custom-call | tf_op jit(solution)/shard_map/route/pallas_call | solution.py:83
  5.7 3.1 %collective-permute-start = (f32[168,128]{1,0:T(8,128)S(1)}, f32[168,128]{1,0:T(8,128)S(1)}, u32[]{:S(2)}, u32[]{:S(2)}) collective-permute-start(f32[168,128]{1,0:T(8,128)S(1)} %route.1.refs_0_.refs_16_), channel_id=1, source_target_pairs={{0,4},{2,6},{4,8},{6,10},{8,12},{10,14},{12,0},{14,2},{1,5},{3,7},... | collective-permute-start | bytes 258056 | tf_op jit(solution)/shard_map/ppermute | solution.py:379
  8.7 2.6 %collective-permute-start.1 = (f32[168,128]{1,0:T(8,128)S(1)}, f32[168,128]{1,0:T(8,128)S(1)}, u32[]{:S(2)}, u32[]{:S(2)}) collective-permute-start(f32[168,128]{1,0:T(8,128)S(1)} %route.1.refs_0_.refs_16_), channel_id=1, source_target_pairs={{0,8},{2,10},{4,12},{6,14},{8,0},{10,2},{12,4},{14,6},{1,9},{3,11}... | collective-permute-start | bytes 258056 | tf_op jit(solution)/shard_map/ppermute | solution.py:379
  11.3 1.3 %collective-permute-start.2 = (f32[168,128]{1,0:T(8,128)S(1)}, f32[168,128]{1,0:T(8,128)S(1)}, u32[]{:S(2)}, u32[]{:S(2)}) collective-permute-start(f32[168,128]{1,0:T(8,128)S(1)} %route.1.refs_0_.refs_16_), channel_id=1, source_target_pairs={{0,12},{2,14},{4,0},{6,2},{8,4},{10,6},{12,8},{14,10},{1,13},{3,15... | collective-permute-start | bytes 258056 | tf_op jit(solution)/shard_map/ppermute | solution.py:379
  12.7 1.5 %collective-permute-start.3 = (f32[168,128]{1,0:T(8,128)S(1)}, f32[168,128]{1,0:T(8,128)S(1)}, u32[]{:S(2)}, u32[]{:S(2)}) collective-permute-start(f32[168,128]{1,0:T(8,128)S(1)} %route.1.refs_0_.refs_16_), channel_id=1, source_target_pairs={{0,2},{2,0},{4,6},{6,4},{8,10},{10,8},{12,14},{14,12},{1,3},{3,1},... | collective-permute-start | bytes 258056 | tf_op jit(solution)/shard_map/ppermute | solution.py:380
  14.2 1.4 %collective-permute-start.4 = (f32[168,128]{1,0:T(8,128)S(1)}, f32[168,128]{1,0:T(8,128)S(1)}, u32[]{:S(2)}, u32[]{:S(2)}) collective-permute-start(f32[168,128]{1,0:T(8,128)S(1)} %collective-permute-done.refs_1_.refs_17_), channel_id=1, source_target_pairs={{0,2},{2,0},{4,6},{6,4},{8,10},{10,8},{12,14},{14,12},{1,3},{3,1},... | collective-permute-start | bytes 258056 | tf_op jit(solution)/shard_map/ppermute | solution.py:380
  15.6 1.5 %collective-permute-done.1.refs_2_.refs_18_ = f32[168,128]{1,0:T(8,128)S(1)} collective-permute-done((f32[168,128]{1,0:T(8,128)S(1)}, f32[168,128]{1,0:T(8,128)S(1)}, u32[]{:S(2)}, u32[]{:S(2)}) %collective-permute-start.1) | collective-permute-done | bytes 86048 | tf_op jit(solution)/shard_map/ppermute | solution.py:379
  17.1 1.6 %collective-permute-start.5 = (f32[168,128]{1,0:T(8,128)S(1)}, f32[168,128]{1,0:T(8,128)S(1)}, u32[]{:S(2)}, u32[]{:S(2)}) collective-permute-start(f32[168,128]{1,0:T(8,128)S(1)} %collective-permute-done.1.refs_2_.refs_18_), channel_id=1, source_target_pairs={{0,2},{2,0},{4,6},{6,4},{8,10},{10,8},{12,14},{14,12},{1,3},{3,1},... | collective-permute-start | bytes 258056 | tf_op jit(solution)/shard_map/ppermute | solution.py:380
  18.7 0.5 collective-permute-start.6
  19.1 0.5 collective-permute-start.8
  19.7 0.1 collective-permute-start.9
  19.7 2.7 %collective-permute-done.5.refs_6_.refs_22_ = f32[168,128]{1,0:T(8,128)S(1)} collective-permute-done((f32[168,128]{1,0:T(8,128)S(1)}, f32[168,128]{1,0:T(8,128)S(1)}, u32[]{:S(2)}, u32[]{:S(2)}) %collective-permute-start.5) | collective-permute-done | bytes 86048 | tf_op jit(solution)/shard_map/ppermute | solution.py:380
  22.4 1.0 %collective-permute-done.6.refs_7_.refs_23_ = f32[168,128]{1,0:T(8,128)S(1)} collective-permute-done((f32[168,128]{1,0:T(8,128)S(1)}, f32[168,128]{1,0:T(8,128)S(1)}, u32[]{:S(2)}, u32[]{:S(2)}) %collective-permute-start.6) | collective-permute-done | bytes 86048 | tf_op jit(solution)/shard_map/ppermute | solution.py:380
  23.4 0.5 collective-permute-start.13
  23.9 0.1 collective-permute-start.14
  24.0 3.6 %tables.1 = (bf16[32,128,256]{2,1,0:T(8,128)(2,1)}, bf16[32,128,256]{2,1,0:T(8,128)(2,1)}) custom-call(s32[64]{0:T(128)} %width.3, s32[1]{0:T(128)} %bitcast.1.base.start), custom_call_target="tpu_custom_call" | custom-call | tf_op jit(solution)/shard_map/tables/pallas_call | solution.py:116
  27.6 1.6 %copy-done = bf16[32,128,256]{2,1,0:T(8,128)(2,1)S(1)} copy-done((bf16[32,128,256]{2,1,0:T(8,128)(2,1)S(1)}, bf16[32,128,256]{2,1,0:T(8,128)(2,1)}, u32[]{:S(2)}) %copy-start) | copy-done | bytes 2097176
  29.2 0.7 %copy-done.5 = s32[64]{0:T(128)S(1)} copy-done((s32[64]{0:T(128)S(1)}, s32[64]{0:T(128)}, u32[]{:S(2)}) %copy-start.5) | copy-done | bytes 280
  29.9 17.8 %field.1.own = f32[16,256,128]{2,1,0:T(8,128)S(1)} custom-call(s32[64]{0:T(128)S(1)} %copy-done.5, s32[1]{0:T(128)} %bitcast.first, s32[1]{0:T(128)} %bitcast.1.base.start, f32[168,128]{1,0:T(8,128)S(1)} %route.1.refs_0_.refs_16_, f32[168,128]{1,0:T(8,128)S(1)} %collective-permute-done.refs_1_.refs_17_, ...), custom_call_target="tpu_custom_call" | custom-call | tf_op jit(solution)/shard_map/field/pallas_call | solution.py:326
  47.6 0.5 collective-permute-start.15
  48.1 0.1 collective-permute-start.16
  48.2 0.1 fusion.11
  48.3 0.1 maximum_select_fusion
  48.4 0.1 fusion.10
  48.5 0.1 pad_maximum_fusion.2
  48.5 0.1 broadcast_in_dim.9
  48.6 0.1 sub.48
  48.7 0.1 broadcast_in_dim.19
  48.8 0.1 sub.54
  48.9 0.1 tile.39
  49.0 0.1 tile.17
  49.1 0.1 mul.119
  49.2 2.7 %collective-permute-done.16 = f32[4,64]{1,0:T(4,128)S(1)} collective-permute-done((f32[4,64]{1,0:T(4,128)S(1)}, f32[4,64]{1,0:T(4,128)S(1)}, u32[]{:S(2)}, u32[]{:S(2)}) %collective-permute-start.16) | collective-permute-done | bytes 1056 | tf_op jit(solution)/shard_map/ppermute | solution.py:385
  51.9 0.1 multiply_bitcast_fusion.1
  51.9 0.1 copy.12
  52.0 0.1 mul.128
  52.1 0.1 multiply_bitcast_fusion
  52.2 0.1 copy.14
  52.3 0.1 mul.141
  52.4 0.2 fusion.4
  52.6 0.1 copy.13
  52.7 0.1 copy.15
  52.8 0.2 fusion.1
  52.9 5.2 %mix.1 = f32[4096,128]{1,0:T(8,128)} custom-call(f32[16,256,128]{2,1,0:T(8,128)S(1)} %field.1.own, f32[16,256,128]{2,1,0:T(8,128)} %collective-permute-done.15.oth, bf16[256,256]{1,0:T(8,128)(2,1)S(1)} %get-tuple-element.21.own_high, bf16[256,256]{1,0:T(8,128)(2,1)S(1)} %get-tuple-element.22.own_low, bf16[256,256]{1,0:T(8,128)(2,1)S(1)} %get-tuple-element.10.oth_high, ...), custom_call_target="tpu_custom_call" | custom-call | tf_op jit(solution)/shard_map/mix/pallas_call | solution.py:363
  (34 shorter events, 0.1 us)
Async XLA Ops:
  0.0 0.8 %copy-start.1 = (f32[4,4096]{1,0:T(4,128)S(1)}, f32[4,4096]{1,0:T(4,128)}, u32[]{:S(2)}) copy-start(f32[4,4096]{1,0:T(4,128)} %inn.1) | copy-start | bytes 196612
  0.8 0.7 %copy-start.2 = (s32[4096,1]{0,1:T(1,128)S(1)}, s32[4096,1]{0,1:T(1,128)}, u32[]{:S(2)}) copy-start(s32[4096,1]{0,1:T(1,128)} %param.11) | copy-start | bytes 49156
  1.6 0.7 %copy-start.3 = (s32[4096,1]{0,1:T(1,128)S(1)}, s32[4096,1]{0,1:T(1,128)}, u32[]{:S(2)}) copy-start(s32[4096,1]{0,1:T(1,128)} %param.9) | copy-start | bytes 49156
  2.3 0.7 %copy-start.4 = (s32[4096]{0:T(1024)S(1)}, s32[4096]{0:T(1024)}, u32[]{:S(2)}) copy-start(s32[4096]{0:T(1024)} %param.10) | copy-start | bytes 49156
  5.7 8.5 %collective-permute-start = (f32[168,128]{1,0:T(8,128)S(1)}, f32[168,128]{1,0:T(8,128)S(1)}, u32[]{:S(2)}, u32[]{:S(2)}) collective-permute-start(f32[168,128]{1,0:T(8,128)S(1)} %route.1.refs_0_.refs_16_), channel_id=1, source_target_pairs={{0,4},{2,6},{4,8},{6,10},{8,12},{10,14},{12,0},{14,2},{1,5},{3,7},... | collective-permute-start | bytes 258056 | tf_op jit(solution)/shard_map/ppermute | solution.py:379
  8.7 8.4 %collective-permute-start.1 = (f32[168,128]{1,0:T(8,128)S(1)}, f32[168,128]{1,0:T(8,128)S(1)}, u32[]{:S(2)}, u32[]{:S(2)}) collective-permute-start(f32[168,128]{1,0:T(8,128)S(1)} %route.1.refs_0_.refs_16_), channel_id=1, source_target_pairs={{0,8},{2,10},{4,12},{6,14},{8,0},{10,2},{12,4},{14,6},{1,9},{3,11}... | collective-permute-start | bytes 258056 | tf_op jit(solution)/shard_map/ppermute | solution.py:379
  11.3 7.3 %collective-permute-start.2 = (f32[168,128]{1,0:T(8,128)S(1)}, f32[168,128]{1,0:T(8,128)S(1)}, u32[]{:S(2)}, u32[]{:S(2)}) collective-permute-start(f32[168,128]{1,0:T(8,128)S(1)} %route.1.refs_0_.refs_16_), channel_id=1, source_target_pairs={{0,12},{2,14},{4,0},{6,2},{8,4},{10,6},{12,8},{14,10},{1,13},{3,15... | collective-permute-start | bytes 258056 | tf_op jit(solution)/shard_map/ppermute | solution.py:379
  12.7 6.4 %collective-permute-start.3 = (f32[168,128]{1,0:T(8,128)S(1)}, f32[168,128]{1,0:T(8,128)S(1)}, u32[]{:S(2)}, u32[]{:S(2)}) collective-permute-start(f32[168,128]{1,0:T(8,128)S(1)} %route.1.refs_0_.refs_16_), channel_id=1, source_target_pairs={{0,2},{2,0},{4,6},{6,4},{8,10},{10,8},{12,14},{14,12},{1,3},{3,1},... | collective-permute-start | bytes 258056 | tf_op jit(solution)/shard_map/ppermute | solution.py:380
  14.2 4.9 %collective-permute-start.7 = (f32[168,128]{1,0:T(8,128)S(1)}, f32[168,128]{1,0:T(8,128)S(1)}, u32[]{:S(2)}, u32[]{:S(2)}) collective-permute-start(f32[168,128]{1,0:T(8,128)S(1)} %route.1.refs_0_.refs_16_), channel_id=1, source_target_pairs={{0,1},{1,0},{2,3},{3,2},{4,5},{5,4},{6,7},{7,6},{8,9},{9,8},{10,11... | collective-permute-start | bytes 258056 | tf_op jit(solution)/shard_map/ppermute | solution.py:381
  14.2 5.4 %collective-permute-start.4 = (f32[168,128]{1,0:T(8,128)S(1)}, f32[168,128]{1,0:T(8,128)S(1)}, u32[]{:S(2)}, u32[]{:S(2)}) collective-permute-start(f32[168,128]{1,0:T(8,128)S(1)} %collective-permute-done.refs_1_.refs_17_), channel_id=1, source_target_pairs={{0,2},{2,0},{4,6},{6,4},{8,10},{10,8},{12,14},{14,12},{1,3},{3,1},... | collective-permute-start | bytes 258056 | tf_op jit(solution)/shard_map/ppermute | solution.py:380
  17.1 5.3 %collective-permute-start.5 = (f32[168,128]{1,0:T(8,128)S(1)}, f32[168,128]{1,0:T(8,128)S(1)}, u32[]{:S(2)}, u32[]{:S(2)}) collective-permute-start(f32[168,128]{1,0:T(8,128)S(1)} %collective-permute-done.1.refs_2_.refs_18_), channel_id=1, source_target_pairs={{0,2},{2,0},{4,6},{6,4},{8,10},{10,8},{12,14},{14,12},{1,3},{3,1},... | collective-permute-start | bytes 258056 | tf_op jit(solution)/shard_map/ppermute | solution.py:380
  18.7 4.8 %collective-permute-start.6 = (f32[168,128]{1,0:T(8,128)S(1)}, f32[168,128]{1,0:T(8,128)S(1)}, u32[]{:S(2)}, u32[]{:S(2)}) collective-permute-start(f32[168,128]{1,0:T(8,128)S(1)} %collective-permute-done.2.refs_3_.refs_19_), channel_id=1, source_target_pairs={{0,2},{2,0},{4,6},{6,4},{8,10},{10,8},{12,14},{14,12},{1,3},{3,1},... | collective-permute-start | bytes 258056 | tf_op jit(solution)/shard_map/ppermute | solution.py:380
  19.1 4.3 %collective-permute-start.10 = (f32[168,128]{1,0:T(8,128)S(1)}, f32[168,128]{1,0:T(8,128)S(1)}, u32[]{:S(2)}, u32[]{:S(2)}) collective-permute-start(f32[168,128]{1,0:T(8,128)S(1)} %collective-permute-done.2.refs_3_.refs_19_), channel_id=1, source_target_pairs={{0,1},{1,0},{2,3},{3,2},{4,5},{5,4},{6,7},{7,6},{8,9},{9,8},{10,11... | collective-permute-start | bytes 258056 | tf_op jit(solution)/shard_map/ppermute | solution.py:381
  19.1 4.8 %collective-permute-start.8 = (f32[168,128]{1,0:T(8,128)S(1)}, f32[168,128]{1,0:T(8,128)S(1)}, u32[]{:S(2)}, u32[]{:S(2)}) collective-permute-start(f32[168,128]{1,0:T(8,128)S(1)} %collective-permute-done.refs_1_.refs_17_), channel_id=1, source_target_pairs={{0,1},{1,0},{2,3},{3,2},{4,5},{5,4},{6,7},{7,6},{8,9},{9,8},{10,11... | collective-permute-start | bytes 258056 | tf_op jit(solution)/shard_map/ppermute | solution.py:381
  19.7 7.9 %collective-permute-start.9 = (f32[168,128]{1,0:T(8,128)S(1)}, f32[168,128]{1,0:T(8,128)S(1)}, u32[]{:S(2)}, u32[]{:S(2)}) collective-permute-start(f32[168,128]{1,0:T(8,128)S(1)} %collective-permute-done.1.refs_2_.refs_18_), channel_id=1, source_target_pairs={{0,1},{1,0},{2,3},{3,2},{4,5},{5,4},{6,7},{7,6},{8,9},{9,8},{10,11... | collective-permute-start | bytes 258056 | tf_op jit(solution)/shard_map/ppermute | solution.py:381
  22.4 5.2 %collective-permute-start.11 = (f32[168,128]{1,0:T(8,128)S(1)}, f32[168,128]{1,0:T(8,128)S(1)}, u32[]{:S(2)}, u32[]{:S(2)}) collective-permute-start(f32[168,128]{1,0:T(8,128)S(1)} %collective-permute-done.3.refs_4_.refs_20_), channel_id=1, source_target_pairs={{0,1},{1,0},{2,3},{3,2},{4,5},{5,4},{6,7},{7,6},{8,9},{9,8},{10,11... | collective-permute-start | bytes 258056 | tf_op jit(solution)/shard_map/ppermute | solution.py:381
  23.4 4.2 %collective-permute-start.12 = (f32[168,128]{1,0:T(8,128)S(1)}, f32[168,128]{1,0:T(8,128)S(1)}, u32[]{:S(2)}, u32[]{:S(2)}) collective-permute-start(f32[168,128]{1,0:T(8,128)S(1)} %collective-permute-done.4.refs_5_.refs_21_), channel_id=1, source_target_pairs={{0,1},{1,0},{2,3},{3,2},{4,5},{5,4},{6,7},{7,6},{8,9},{9,8},{10,11... | collective-permute-start | bytes 258056 | tf_op jit(solution)/shard_map/ppermute | solution.py:381
  23.4 4.2 %collective-permute-start.13 = (f32[168,128]{1,0:T(8,128)S(1)}, f32[168,128]{1,0:T(8,128)S(1)}, u32[]{:S(2)}, u32[]{:S(2)}) collective-permute-start(f32[168,128]{1,0:T(8,128)S(1)} %collective-permute-done.5.refs_6_.refs_22_), channel_id=1, source_target_pairs={{0,1},{1,0},{2,3},{3,2},{4,5},{5,4},{6,7},{7,6},{8,9},{9,8},{10,11... | collective-permute-start | bytes 258056 | tf_op jit(solution)/shard_map/ppermute | solution.py:381
  23.9 3.7 %collective-permute-start.14 = (f32[168,128]{1,0:T(8,128)S(1)}, f32[168,128]{1,0:T(8,128)S(1)}, u32[]{:S(2)}, u32[]{:S(2)}) collective-permute-start(f32[168,128]{1,0:T(8,128)S(1)} %collective-permute-done.6.refs_7_.refs_23_), channel_id=1, source_target_pairs={{0,1},{1,0},{2,3},{3,2},{4,5},{5,4},{6,7},{7,6},{8,9},{9,8},{10,11... | collective-permute-start | bytes 258056 | tf_op jit(solution)/shard_map/ppermute | solution.py:381
  27.6 1.6 %copy-start = (bf16[32,128,256]{2,1,0:T(8,128)(2,1)S(1)}, bf16[32,128,256]{2,1,0:T(8,128)(2,1)}, u32[]{:S(2)}) copy-start(bf16[32,128,256]{2,1,0:T(8,128)(2,1)} %get-tuple-element.7.refs_24_) | copy-start | bytes 6291460
  29.2 0.7 %copy-start.5 = (s32[64]{0:T(128)S(1)}, s32[64]{0:T(128)}, u32[]{:S(2)}) copy-start(s32[64]{0:T(128)} %width.3) | copy-start | bytes 772
  29.9 18.3 %copy-start.7 = (f32[4,64]{1,0:T(4,128)S(1)}, f32[4,64]{1,0:T(4,128)}, u32[]{:S(2)}) copy-start(f32[4,64]{1,0:T(4,128)} %param.13) | copy-start | bytes 3076
  29.9 18.4 %copy-start.6 = (f32[4,8]{1,0:T(4,128)S(1)}, f32[4,8]{1,0:T(4,128)}, u32[]{:S(2)}) copy-start(f32[4,8]{1,0:T(4,128)} %param.15) | copy-start | bytes 388
  29.9 19.2 %copy-start.8 = (f32[4,64]{1,0:T(4,128)S(1)}, f32[4,64]{1,0:T(4,128)}, u32[]{:S(2)}) copy-start(f32[4,64]{1,0:T(4,128)} %param.14) | copy-start | bytes 3076
  47.6 5.3 %collective-permute-start.15 = (f32[16,256,128]{2,1,0:T(8,128)S(1)}, f32[16,256,128]{2,1,0:T(8,128)}, u32[]{:S(2)}, u32[]{:S(2)}) collective-permute-start(f32[16,256,128]{2,1,0:T(8,128)S(1)} %field.1.own), channel_id=1, source_target_pairs={{0,1},{1,0},{2,3},{3,2},{4,5},{5,4},{6,7},{7,6},{8,9},{9,8},{10,11... | collective-permute-start | bytes 6291464 | tf_op jit(solution)/shard_map/ppermute | solution.py:393
  48.1 3.7 %collective-permute-start.16 = (f32[4,64]{1,0:T(4,128)S(1)}, f32[4,64]{1,0:T(4,128)S(1)}, u32[]{:S(2)}, u32[]{:S(2)}) collective-permute-start(f32[4,64]{1,0:T(4,128)S(1)} %copy-done.7), channel_id=1, source_target_pairs={{0,1},{1,0},{2,3},{3,2},{4,5},{5,4},{6,7},{7,6},{8,9},{9,8},{10,11... | collective-permute-start | bytes 3080 | tf_op jit(solution)/shard_map/ppermute | solution.py:385

commit v3 on v2

--- a/solution.py
+++ b/solution.py
@@ -28,7 +28,13 @@
     return lax.broadcasted_iota(jnp.int32, shape, dim)
 
 
-def route_kernel(inn, level, owner, local, pay, hot, pre, dest, left, right):
+def route_kernel(inn_ref, level_ref, owner_ref, local_ref, pay, inn, level, owner, local, sems, hot, pre, dest, left, right):
+    pairs = ((level_ref, level), (inn_ref, inn), (owner_ref, owner), (local_ref, local))
+    copies = [pltpu.make_async_copy(src, dst, sems.at[k]) for k, (src, dst) in enumerate(pairs)]
+    for copy in copies:
+        copy.start()
+    for copy in copies:
+        copy.wait()
     nvar, nobs = inn.shape
     chunks = nobs // LANES
     levels = hot.shape[0] // chunks
@@ -83,14 +89,20 @@
     return pl.pallas_call(
         route_kernel,
         out_shape=jax.ShapeDtypeStruct(((nvar + 1) * chunks + 8, LANES), F32),
+        in_specs=[pl.BlockSpec(memory_space=pltpu.HBM)] * 4,
         scratch_shapes=[
+            pltpu.VMEM((nvar, nobs), F32),
+            pltpu.VMEM((chunks, LANES), jnp.int32),
+            pltpu.VMEM((chunks, LANES), jnp.int32),
+            pltpu.VMEM((chunks, LANES), jnp.int32),
+            pltpu.SemaphoreType.DMA((4,)),
             pltpu.VMEM((chunks * levels, LANES), BF16),
             pltpu.VMEM((chunks * levels, 2 * LANES), F32),
             pltpu.VMEM((chunks, LANES), jnp.int32),
             pltpu.VMEM((pieces * chunks, nobs), BF16),
             pltpu.VMEM((LANES, nobs), BF16),
         ],
-        compiler_params=pltpu.CompilerParams(vmem_limit_bytes=32 << 20),
+        compiler_params=pltpu.CompilerParams(vmem_limit_bytes=60 << 20),
         name="route",
     )(innovations, level.reshape(chunks, LANES), owner.reshape(chunks, LANES), local.reshape(chunks, LANES))
 
@@ -119,6 +131,7 @@
         in_specs=[pl.BlockSpec(memory_space=pltpu.SMEM)] * 2,
         out_specs=(spec, spec),
         out_shape=(shape, shape),
+        cost_estimate=pl.CostEstimate(flops=1 << 24, bytes_accessed=8 << 20, transcendentals=1 << 20),
         name="tables",
     )(band_width, base)
 
@@ -143,11 +156,11 @@
     sub = iota((8, LANES), 0)
     for s in range(sources):
         for c in range(0, chunks, 2):
-            here, there = own[s][4 * c : 4 * c + 8, :], oth[s][4 * c : 4 * c + 8, :]
+            here, there = own[s, 4 * c : 4 * c + 8, :], oth[s, 4 * c : 4 * c + 8, :]
             vals[s, 8 * c : 8 * c + 8, :] = jnp.where(sub < 4, here, pltpu.roll(there, 4, 0))
             vals[s, 8 * c + 8 : 8 * c + 16, :] = jnp.where(sub < 4, pltpu.roll(here, 4, 0), there)
         vals[s, 8 * chunks :, :] = jnp.zeros((8, LANES), F32)
-        spots[s, :chunks, :] = own[s][nvar * chunks : (nvar + 1) * chunks, :]
+        spots[s, :chunks, :] = own[s, nvar * chunks : (nvar + 1) * chunks, :]
         spots[s, chunks:, :] = jnp.zeros((8, LANES), F32)
     nothing = jnp.zeros((8, LANES), F32)
 
@@ -193,7 +206,10 @@
         lax.fori_loop(0, pairs, note, 0)
         return pair + pairs
 
-    pair = lax.fori_loop(0, levels, per_level, jnp.int32(0))
+    def two_levels(k, pair):
+        return per_level(2 * k + 1, per_level(2 * k, pair))
+
+    pair = lax.fori_loop(0, levels // 2, two_levels, jnp.int32(0))
     for p in range(UNROLL):
         level_of[pair + p] = levels
         for h in range(2):
@@ -202,7 +218,7 @@
     total[0] = pair
 
 
-UNROLL = 4
+UNROLL = 8
 
 
 def spread(wide, levels, base, width, first, queue, queue_spot, level_of, total, field):
@@ -295,41 +311,51 @@
                 bound = bound * hop
 
     def group(g, carry):
-        for p in range(2):
-            one_level(2 * g + p)
+        for p in range(4):
+            one_level(4 * g + p)
         return carry
 
-    lax.fori_loop(0, levels // 2, group, 0)
+    lax.fori_loop(0, levels // 4, group, 0)
 
 
 def field_kernel(sources, wide, nvar, width, first, start, *refs):
-    own, oth, marks = refs[:sources], refs[sources : 2 * sources], refs[2 * sources : 3 * sources]
-    high, low, slab, vals, spots, queue, queue_spot, level_of, total, field = refs[3 * sources :]
-    chunks = (own[0].shape[0] - 8) // (nvar + 1)
+    own, oth, *marks = refs[: 2 + sources]
+    far_high, far_low, slab, high, low, sems, vals, spots, queue, queue_spot, level_of, total, field = refs[2 + sources :]
+    chunks = (own.shape[1] - 8) // (nvar + 1)
     levels = high.shape[0]
+    copies = [pltpu.make_async_copy(far_high, high, sems.at[0]), pltpu.make_async_copy(far_low, low, sems.at[1])]
+    for copy in copies:
+        copy.start()
     base = start[0]
     gather_levels(
         sources, nvar, chunks, base, levels, own, oth, marks, vals, spots, queue, queue_spot, level_of, total
     )
     spread(wide, levels, base, width, first, queue, queue_spot, level_of, total, field)
+    for copy in copies:
+        copy.wait()
     filter_levels(levels, base, width, high, low, field, slab)
 
 
 def make_field(own, oth, band_width, first, base, high, low, nvar, levels, wide):
-    sources = len(own)
-    rows = own[0].shape[0]
+    sources, rows, _ = own.shape
     chunks = (rows - 8) // (nvar + 1)
     whole = pl.BlockSpec(memory_space=pltpu.VMEM)
-    marks = pl.BlockSpec((8, LANES), lambda i: (rows // 8 - 1, 0), memory_space=pltpu.SMEM)
+    marks = [
+        pl.BlockSpec((None, 8, LANES), functools.partial(lambda s, i: (s, rows // 8 - 1, 0), s), memory_space=pltpu.SMEM)
+        for s in range(sources)
+    ]
     smem = pl.BlockSpec(memory_space=pltpu.SMEM)
     pairs = levels * sources // 2 + UNROLL + 1
     return pl.pallas_call(
         functools.partial(field_kernel, sources, wide, nvar),
         grid=(1,),
-        in_specs=[smem] * 3 + [whole] * (2 * sources) + [marks] * sources + [whole] * 2,
+        in_specs=[smem] * 3 + [whole] * 2 + marks + [pl.BlockSpec(memory_space=pltpu.HBM)] * 2,
         out_specs=whole,
         out_shape=jax.ShapeDtypeStruct((4 * NX_DEV, 2 * nvar * levels, LANES), F32),
         scratch_shapes=[
+            pltpu.VMEM(high.shape, BF16),
+            pltpu.VMEM(low.shape, BF16),
+            pltpu.SemaphoreType.DMA((2,)),
             pltpu.VMEM((sources, 8 * chunks + 8, LANES), F32),
             pltpu.VMEM((sources, chunks + 8, LANES), F32),
             pltpu.VMEM((16 * pairs, LANES), F32),
@@ -338,34 +364,49 @@
             pltpu.SMEM((1,), jnp.int32),
             pltpu.VMEM((levels + 1, 16 * NX_DEV, HALF), F32),
         ],
-        compiler_params=pltpu.CompilerParams(vmem_limit_bytes=48 << 20),
+        compiler_params=pltpu.CompilerParams(vmem_limit_bytes=56 << 20),
         name="field",
-    )(band_width, first, base, *own, *oth, *own, high, low)
-
-
-def mix_kernel(own, oth, own_high, own_low, oth_high, oth_low, out):
-    for x in range(NX_DEV):
-        for h in range(2):
-            total = None
-            for slab, high, low in ((own, own_high, own_low), (oth, oth_high, oth_low)):
-                part = jnp.concatenate([slab[4 * x + 2 * h], slab[4 * x + 2 * h + 1]], 1)
-                top = part.astype(BF16)
-                rest = (part - top.astype(F32)).astype(BF16)
-                term = nn_dot(high[...], top) + nn_dot(high[...], rest) + nn_dot(low[...], top)
-                total = term if total is None else total + term
+    )(band_width, first, base, own, oth, *([own] * sources), high, low)
+
+
+def mix_kernel(slab, high, low, *refs):
+    out = refs[-1]
+    x = pl.program_id(0)
+    for h in range(2):
+        part = jnp.concatenate([slab[2 * h], slab[2 * h + 1]], 1)
+        top = part.astype(BF16)
+        rest = (part - top.astype(F32)).astype(BF16)
+        term = nn_dot(high[...], top) + nn_dot(high[...], rest) + nn_dot(low[...], top)
+        if len(refs) == 1:
+            out[0, :, h * HALF : (h + 1) * HALF] = term
+        else:
+            term = term + refs[0][0, :, h * HALF : (h + 1) * HALF]
             for g in range(2):
-                rows = pl.ds(8 * h + 4 * g + x, total.shape[0], stride=4 * NX_DEV)
-                out[rows, :] = total[:, g * LANES : (g + 1) * LANES]
-
-
-def mix(own, oth, own_mats, oth_mats):
-    rows = own_mats[0].shape[0]
+                rows = pl.ds(8 * h + 4 * g + x, term.shape[0], stride=4 * NX_DEV)
+                out[rows, :] = term[:, g * LANES : (g + 1) * LANES]
+
+
+def mix(slab, mats, *before):
+    rows, depth = mats[0].shape
+    strip = pl.BlockSpec((4, depth, LANES), lambda i: (i, 0, 0))
+    matrix = pl.BlockSpec((rows, depth), lambda i: (0, 0))
+    partial = pl.BlockSpec((1, rows, NY), lambda i: (i, 0, 0))
+    if before:
+        shape = (rows * NX_DEV * NY // LANES, LANES)
+        out_spec = pl.BlockSpec(shape, lambda i: (0, 0))
+    else:
+        shape = (NX_DEV, rows, NY)
+        out_spec = partial
     return pl.pallas_call(
         mix_kernel,
-        out_shape=jax.ShapeDtypeStruct((rows * NX_DEV * NY // LANES, LANES), F32),
+        grid=(NX_DEV,),
+        in_specs=[strip, matrix, matrix] + [partial] * len(before),
+        out_specs=out_spec,
+        out_shape=jax.ShapeDtypeStruct(shape, F32),
         compiler_params=pltpu.CompilerParams(vmem_limit_bytes=32 << 20),
+        cost_estimate=pl.CostEstimate(flops=1 << 30, bytes_accessed=6 << 20, transcendentals=0),
         name="mix",
-    )(own, oth, *own_mats, *oth_mats)
+    )(slab, *mats, *before)
 
 
 def on_device(innovations, obs_owner, obs_local, obs_level, band_width, vert_scale, sigma, balance):
@@ -374,11 +415,6 @@
     levels = band_width.shape[0]
     swap = [(0, 1), (1, 0)]
     unit = route(innovations, obs_owner, obs_level, obs_local, levels)
-    own = [unit]
-    for k in range(2, groups, 2):
-        own.append(lax.ppermute(unit, "sub", [(i, (i + k) % groups) for i in range(groups)]))
-    own += [lax.ppermute(held, "sub", [(i, i ^ 1) for i in range(groups)]) for held in own]
-    oth = [lax.ppermute(held, "var", swap) for held in own]
     side = lax.axis_index("var").astype(jnp.int32)
     half = levels // 2
     base, last = half * side, half * (1 - side)
@@ -389,8 +425,17 @@
     first = (lax.axis_index("sub") * NX_DEV).astype(jnp.int32).reshape(1)
     base = base.reshape(1)
     high, low = tables(band_width, base, half)
+    own = [unit]
+    for k in range(2, groups, 2):
+        own.append(lax.ppermute(unit, "sub", [(i, (i + k) % groups) for i in range(groups)]))
+    own[-1], high, low = lax.optimization_barrier((own[-1], high, low))
+    own += [lax.ppermute(held, "sub", [(i, i ^ 1) for i in range(groups)]) for held in own]
+    own[-1], own_mats, oth_mats = lax.optimization_barrier((own[-1], own_mats, oth_mats))
+    own = jnp.stack(own)
+    oth = lax.ppermute(own, "var", swap)
     slab = make_field(own, oth, band_width, first, base, high, low, nvar, half, NX_DEV * groups)
-    out = mix(slab, lax.ppermute(slab, "var", swap), own_mats, oth_mats)
+    swapped = lax.ppermute(slab, "var", swap)
+    out = mix(swapped, oth_mats, mix(slab, own_mats))
     out = out.reshape(nvar, levels, NY // LANES, NX_DEV, LANES)
     return jnp.swapaxes(out, 2, 3).reshape(nvar, levels, NX_DEV, NY)
 

time: 58.7 us -> 55.4 us (0.944)
  starting transfers between devices: 13.7 us -> 10.5 us
  Pallas kernels: 29.2 us -> 28.3 us
  waiting for transfers between devices: 7.89 us -> 8.58 us
  other arithmetic: 0.71 us -> 1.39 us
    ppermute x9 -> x2, waiting for transfers between devices: 0.02 us -> 3.3 us  [the longest x1 2.13 us: on_device(): oth = lax.ppermute(own, 'var', swap)]
    ppermute x1, waiting for transfers between devices: 2.67 us -> 0.01 us  [on_device(): theirs = lax.ppermute(vert_scale, 'var', swap)]
    ppermute x3, starting transfers between devices: 7.01 us -> 4.61 us  [on_device(): lax.ppermute(unit, 'sub', [(i, (i + k) % groups) for i in range(groups)])]
    pallas_call x1, Pallas kernels: 17.8 us -> 15.7 us  [make_field(): pl.pallas_call(functools.partial(field_kernel, sources, wide, nvar), grid...]
    unnamed x18 -> x15, local copies, waits for them, and re-layouts: 5.24 us -> 3.41 us
    pallas_call x1, Pallas kernels: 2.67 us -> 4.25 us  [route(): pl.pallas_call(route_kernel, out_shape=jax.ShapeDtypeStruct(((nvar + 1) *...]
    ppermute x4, waiting for transfers between devices: 3.71 us -> 5.27 us  [on_device(): lax.ppermute(held, 'sub', [(i, i ^ 1) for i in range(groups)])]
    ppermute x9 -> x2, starting transfers between devices: 1.67 us -> 0.14 us  [the longest x1 0.07 us: on_device(): oth = lax.ppermute(own, 'var', swap)]
  transfers between devices with their start and end apart: 17 -> 10, of which waited for: 4 -> 3; matrix products, arithmetic and copies ran while one was open for 3% -> 9% of each run, Pallas kernels for 6% -> 9%
where the time goes in v3:
time: 55.4 us; the launch traced here: 55.1 us
  Pallas kernels  28.3 us (51%)
  starting transfers between devices  10.5 us (19%)
  waiting for transfers between devices  8.58 us (15%)
  local copies, waits for them, and re-layouts  6.11 us (11%)
  other arithmetic  1.39 us (3%)
    pallas_call x1, Pallas kernels, make_field(): pl.pallas_call(functools.partial(field_kernel, sources, wide, nvar), grid...  15.7 us
    ppermute x4, starting transfers between devices, on_device(): lax.ppermute(held, 'sub', [(i, i ^ 1) for i in range(groups)])  5.7 us
    ppermute x4, waiting for transfers between devices, on_device(): lax.ppermute(held, 'sub', [(i, i ^ 1) for i in range(groups)])  5.27 us
    pallas_call x2, Pallas kernels, mix(): pl.pallas_call(mix_kernel, grid=(NX_DEV,), in_specs=[strip, matrix, matri...  4.84 us
    ppermute x3, starting transfers between devices, on_device(): lax.ppermute(unit, 'sub', [(i, (i + k) % groups) for i in range(groups)])  4.61 us
    pallas_call x1, Pallas kernels, route(): pl.pallas_call(route_kernel, out_shape=jax.ShapeDtypeStruct(((nvar + 1) *...  4.25 us
    pallas_call x1, Pallas kernels, tables(): pl.pallas_call(table_kernel, grid=(levels // depth,), in_specs=[pl.BlockS...  3.59 us
    unnamed x15, local copies, waits for them, and re-layouts  3.41 us
  transfers between devices with their start and end apart: 10, of which 3 were waited for; matrix products, arithmetic and copies ran while one was open for 9% of the time, Pallas kernels for 9%

profile of v3, /device:TPU:0, one launch (start us, length us, event | category | flops | bytes accessed | tf_op | source)
XLA Modules:
  0.0 55.1 jit_solution(10667894449828980370)
XLA Ops:
  0.0 4.2 %route.1 = f32[168,128]{1,0:T(8,128)} custom-call(f32[4,4096]{1,0:T(4,128)} %inn_ref.1, s32[32,128]{1,0:T(8,128)} %bitcast.70, s32[32,128]{1,0:T(8,128)} %bitcast.71, s32[32,128]{1,0:T(8,128)} %bitcast.72), custom_call_target="tpu_custom_call" | custom-call | tf_op jit(solution)/shard_map/route/pallas_call | solution.py:89
  4.3 3.0 %collective-permute-start.3 = (f32[168,128]{1,0:T(8,128)}, f32[168,128]{1,0:T(8,128)S(1)}, u32[]{:S(2)}, u32[]{:S(2)}) collective-permute-start(f32[168,128]{1,0:T(8,128)} %route.1), channel_id=1, source_target_pairs={{0,2},{2,0},{4,6},{6,4},{8,10},{10,8},{12,14},{14,12},{1,3},{3,1},... | collective-permute-start | bytes 258056 | tf_op jit(solution)/shard_map/ppermute | solution.py:432
  7.3 3.6 %collective-permute-start.2 = (f32[168,128]{1,0:T(8,128)}, f32[168,128]{1,0:T(8,128)S(1)}, u32[]{:S(2)}, u32[]{:S(2)}) collective-permute-start(f32[168,128]{1,0:T(8,128)} %route.1), channel_id=1, source_target_pairs={{0,12},{2,14},{4,0},{6,2},{8,4},{10,6},{12,8},{14,10},{1,13},{3,15... | collective-permute-start | bytes 258056 | tf_op jit(solution)/shard_map/ppermute | solution.py:430
  10.9 0.0 collective-permute-start.1
  10.9 1.0 %collective-permute-start = (f32[168,128]{1,0:T(8,128)}, f32[168,128]{1,0:T(8,128)S(1)}, u32[]{:S(2)}, u32[]{:S(2)}) collective-permute-start(f32[168,128]{1,0:T(8,128)} %route.1), channel_id=1, source_target_pairs={{0,4},{2,6},{4,8},{6,10},{8,12},{10,14},{12,0},{14,2},{1,5},{3,7},... | collective-permute-start | bytes 258056 | tf_op jit(solution)/shard_map/ppermute | solution.py:430
  11.9 0.0 collective-permute-start.7
  11.9 0.9 %bitcast_dynamic-update-slice_fusion.7 = f32[8,168,128]{2,1,0:T(8,128)S(1)} fusion(f32[168,128]{1,0:T(8,128)} %route.1), kind=kLoop, calls=%fused_computation.29 | loop fusion | bytes 172032
  12.8 0.8 %mul.119 = f32[256]{0:T(256)S(1)} reshape(f32[4,64]{1,0:T(4,128)} %param.14) | data formatting | bytes 2048 | tf_op jit(solution)/shard_map/mul | solution.py:148
  13.6 0.8 %fusion.11 = (f32[4,4]{1,0:T(4,128)S(1)}, f32[4,4]{1,0:T(4,128)S(1)}) fusion(f32[4,8]{1,0:T(4,128)} %param.15), kind=kLoop, calls=%fused_computation.41 | loop fusion | bytes 256 | tf_op jit(solution)/shard_map/jit(_roll_static)/slice | solution.py:422
  14.4 0.8 %maximum_select_fusion = f32[4,8]{1,0:T(4,128)S(1)} fusion(f32[4,8]{1,0:T(4,128)} %param.15, f32[4,4]{1,0:T(4,128)S(1)} %get-tuple-element.36, f32[4,4]{1,0:T(4,128)S(1)} %get-tuple-element.35, pred[]{:T(512)S(6)} %eq.3), kind=kLoop, calls=%fused_computation.34 | loop fusion | flops 64 | bytes 385 | tf_op jit(solution)/shard_map/jit(_where)/select_n | solution.py:422
  15.2 0.1 fusion.10
  15.3 0.1 broadcast_in_dim.9
  15.3 0.1 sub.48
  15.4 0.1 broadcast_in_dim.19
  15.5 0.1 sub.54
  15.6 0.1 pad_maximum_fusion.2
  15.7 0.1 tile.39
  15.8 0.1 tile.17
  15.9 3.6 %tables.1 = (bf16[32,128,256]{2,1,0:T(8,128)(2,1)}, bf16[32,128,256]{2,1,0:T(8,128)(2,1)}) custom-call(s32[64]{0:T(128)} %width.3, s32[1]{0:T(128)} %bitcast.1.base.start), custom_call_target="tpu_custom_call" | custom-call | flops 16777216 | bytes 8388608 | tf_op jit(solution)/shard_map/tables/pallas_call | solution.py:128
  19.5 0.0 collective-permute-done.7
  19.5 0.1 multiply_bitcast_fusion.1
  19.6 0.1 copy.12
  19.6 0.1 mul.128
  19.7 0.1 multiply_bitcast_fusion
  19.8 0.1 copy.14
  19.9 0.1 mul.141
  20.0 0.2 fusion.4
  20.2 0.1 copy.13
  20.3 0.1 copy.15
  20.4 0.2 fusion.1
  20.6 0.0 collective-permute-done.2
  20.6 0.6 %collective-permute-start.6 = (f32[168,128]{1,0:T(8,128)S(1)}, f32[168,128]{1,0:T(8,128)S(1)}, u32[]{:S(2)}, u32[]{:S(2)}) collective-permute-start(f32[168,128]{1,0:T(8,128)S(1)} %collective-permute-done.2), channel_id=1, source_target_pairs={{0,2},{2,0},{4,6},{6,4},{8,10},{10,8},{12,14},{14,12},{1,3},{3,1},... | collective-permute-start | bytes 258056 | tf_op jit(solution)/shard_map/ppermute | solution.py:432
  21.1 0.0 collective-permute-done
  21.2 0.0 collective-permute-done.1
  21.2 1.6 %collective-permute-start.5 = (f32[168,128]{1,0:T(8,128)S(1)}, f32[168,128]{1,0:T(8,128)S(1)}, u32[]{:S(2)}, u32[]{:S(2)}) collective-permute-start(f32[168,128]{1,0:T(8,128)S(1)} %collective-permute-done.1), channel_id=1, source_target_pairs={{0,2},{2,0},{4,6},{6,4},{8,10},{10,8},{12,14},{14,12},{1,3},{3,1},... | collective-permute-start | bytes 258056 | tf_op jit(solution)/shard_map/ppermute | solution.py:432
  22.8 0.5 collective-permute-start.4
  23.3 0.0 collective-permute-done.3
  23.3 5.3 %collective-permute-done.4 = f32[168,128]{1,0:T(8,128)S(1)} collective-permute-done((f32[168,128]{1,0:T(8,128)S(1)}, f32[168,128]{1,0:T(8,128)S(1)}, u32[]{:S(2)}, u32[]{:S(2)}) %collective-permute-start.4) | collective-permute-done | bytes 86048 | tf_op jit(solution)/shard_map/ppermute | solution.py:432
  28.6 0.0 collective-permute-done.5
  28.6 0.1 collective-permute-start.8
  28.7 2.1 %collective-permute-done.8.refs_1_ = f32[8,168,128]{2,1,0:T(8,128)S(1)} collective-permute-done((f32[8,168,128]{2,1,0:T(8,128)S(1)}, f32[8,168,128]{2,1,0:T(8,128)S(1)}, u32[]{:S(2)}, u32[]{:S(2)}) %collective-permute-start.8) | collective-permute-done | bytes 688160 | tf_op jit(solution)/shard_map/ppermute | solution.py:435
  30.8 0.9 %copy-done.2 = f32[8,168,128]{2,1,0:T(8,128)} copy-done((f32[8,168,128]{2,1,0:T(8,128)}, f32[8,168,128]{2,1,0:T(8,128)S(1)}, u32[]{:S(2)}) %copy-start.2) | copy-done | bytes 688152
  31.7 15.7 %field.1.slab = f32[16,256,128]{2,1,0:T(8,128)} custom-call(s32[64]{0:T(128)} %width.3, s32[1]{0:T(128)} %bitcast.first, s32[1]{0:T(128)} %bitcast.1.base.start, f32[8,168,128]{2,1,0:T(8,128)} %copy-done.1, f32[8,168,128]{2,1,0:T(8,128)} %copy-done.2, f32[8,168,128]{2,1,0:T(8,128)} %copy-done.1, f32[8,168,128]{2,1,0:T(8,128)} %copy-done.1, ...), custom_call_target="tpu_custom_call" | custom-call | tf_op jit(solution)/shard_map/field/pallas_call | solution.py:349
  47.4 0.1 collective-permute-start.9
  47.5 1.6 %copy-done = f32[16,256,128]{2,1,0:T(8,128)S(1)} copy-done((f32[16,256,128]{2,1,0:T(8,128)S(1)}, f32[16,256,128]{2,1,0:T(8,128)}, u32[]{:S(2)}) %copy-start) | copy-done | bytes 2097176
  49.0 1.6 %mix.2.refs_0_ = f32[4,256,512]{2,1,0:T(8,128)S(1)} custom-call(f32[16,256,128]{2,1,0:T(8,128)S(1)} %copy-done, bf16[256,256]{1,0:T(8,128)(2,1)S(1)} %get-tuple-element.23.high, bf16[256,256]{1,0:T(8,128)(2,1)S(1)} %get-tuple-element.24.low), custom_call_target="tpu_custom_call" | custom-call | flops 1073741824 | bytes 6291456 | tf_op jit(solution)/shard_map/mix/pallas_call | solution.py:400
  50.6 1.2 %collective-permute-done.9.slab = f32[16,256,128]{2,1,0:T(8,128)S(1)} collective-permute-done((f32[16,256,128]{2,1,0:T(8,128)}, f32[16,256,128]{2,1,0:T(8,128)S(1)}, u32[]{:S(2)}, u32[]{:S(2)}) %collective-permute-start.9) | collective-permute-done | bytes 2097184 | tf_op jit(solution)/shard_map/ppermute | solution.py:437
  51.8 3.3 %mix.3 = f32[4096,128]{1,0:T(8,128)} custom-call(f32[16,256,128]{2,1,0:T(8,128)S(1)} %collective-permute-done.9.slab, bf16[256,256]{1,0:T(8,128)(2,1)S(1)} %get-tuple-element.21.high, bf16[256,256]{1,0:T(8,128)(2,1)S(1)} %get-tuple-element.22.low, f32[4,256,512]{2,1,0:T(8,128)S(1)} %mix.2.refs_0_), custom_call_target="tpu_custom_call" | custom-call | flops 1073741824 | bytes 6291456 | tf_op jit(solution)/shard_map/mix/pallas_call | solution.py:400
  (19 shorter events, 0.1 us)
Async XLA Ops:
  0.0 19.5 %copy-start.3 = (f32[4,64]{1,0:T(4,128)S(1)}, f32[4,64]{1,0:T(4,128)}, u32[]{:S(2)}) copy-start(f32[4,64]{1,0:T(4,128)} %param.13) | copy-start | bytes 3076
  4.3 19.0 %collective-permute-start.3 = (f32[168,128]{1,0:T(8,128)}, f32[168,128]{1,0:T(8,128)S(1)}, u32[]{:S(2)}, u32[]{:S(2)}) collective-permute-start(f32[168,128]{1,0:T(8,128)} %route.1), channel_id=1, source_target_pairs={{0,2},{2,0},{4,6},{6,4},{8,10},{10,8},{12,14},{14,12},{1,3},{3,1},... | collective-permute-start | bytes 258056 | tf_op jit(solution)/shard_map/ppermute | solution.py:432
  7.3 13.3 %collective-permute-start.2 = (f32[168,128]{1,0:T(8,128)}, f32[168,128]{1,0:T(8,128)S(1)}, u32[]{:S(2)}, u32[]{:S(2)}) collective-permute-start(f32[168,128]{1,0:T(8,128)} %route.1), channel_id=1, source_target_pairs={{0,12},{2,14},{4,0},{6,2},{8,4},{10,6},{12,8},{14,10},{1,13},{3,15... | collective-permute-start | bytes 258056 | tf_op jit(solution)/shard_map/ppermute | solution.py:430
  10.9 10.3 %collective-permute-start.1 = (f32[168,128]{1,0:T(8,128)}, f32[168,128]{1,0:T(8,128)S(1)}, u32[]{:S(2)}, u32[]{:S(2)}) collective-permute-start(f32[168,128]{1,0:T(8,128)} %route.1), channel_id=1, source_target_pairs={{0,8},{2,10},{4,12},{6,14},{8,0},{10,2},{12,4},{14,6},{1,9},{3,11}... | collective-permute-start | bytes 258056 | tf_op jit(solution)/shard_map/ppermute | solution.py:430
  10.9 10.2 %collective-permute-start = (f32[168,128]{1,0:T(8,128)}, f32[168,128]{1,0:T(8,128)S(1)}, u32[]{:S(2)}, u32[]{:S(2)}) collective-permute-start(f32[168,128]{1,0:T(8,128)} %route.1), channel_id=1, source_target_pairs={{0,4},{2,6},{4,8},{6,10},{8,12},{10,14},{12,0},{14,2},{1,5},{3,7},... | collective-permute-start | bytes 258056 | tf_op jit(solution)/shard_map/ppermute | solution.py:430
  11.9 7.6 %collective-permute-start.7 = (f32[4,64]{1,0:T(4,128)}, f32[4,64]{1,0:T(4,128)S(1)}, u32[]{:S(2)}, u32[]{:S(2)}) collective-permute-start(f32[4,64]{1,0:T(4,128)} %param.13), channel_id=1, source_target_pairs={{0,1},{1,0},{2,3},{3,2},{4,5},{5,4},{6,7},{7,6},{8,9},{9,8},{10,11... | collective-permute-start | bytes 3080 | tf_op jit(solution)/shard_map/ppermute | solution.py:421
  20.6 8.0 %collective-permute-start.6 = (f32[168,128]{1,0:T(8,128)S(1)}, f32[168,128]{1,0:T(8,128)S(1)}, u32[]{:S(2)}, u32[]{:S(2)}) collective-permute-start(f32[168,128]{1,0:T(8,128)S(1)} %collective-permute-done.2), channel_id=1, source_target_pairs={{0,2},{2,0},{4,6},{6,4},{8,10},{10,8},{12,14},{14,12},{1,3},{3,1},... | collective-permute-start | bytes 258056 | tf_op jit(solution)/shard_map/ppermute | solution.py:432
  21.2 7.4 %collective-permute-start.5 = (f32[168,128]{1,0:T(8,128)S(1)}, f32[168,128]{1,0:T(8,128)S(1)}, u32[]{:S(2)}, u32[]{:S(2)}) collective-permute-start(f32[168,128]{1,0:T(8,128)S(1)} %collective-permute-done.1), channel_id=1, source_target_pairs={{0,2},{2,0},{4,6},{6,4},{8,10},{10,8},{12,14},{14,12},{1,3},{3,1},... | collective-permute-start | bytes 258056 | tf_op jit(solution)/shard_map/ppermute | solution.py:432
  22.8 5.8 %collective-permute-start.4 = (f32[168,128]{1,0:T(8,128)S(1)}, f32[168,128]{1,0:T(8,128)S(1)}, u32[]{:S(2)}, u32[]{:S(2)}) collective-permute-start(f32[168,128]{1,0:T(8,128)S(1)} %collective-permute-done), channel_id=1, source_target_pairs={{0,2},{2,0},{4,6},{6,4},{8,10},{10,8},{12,14},{14,12},{1,3},{3,1},... | collective-permute-start | bytes 258056 | tf_op jit(solution)/shard_map/ppermute | solution.py:432
  28.6 2.2 %copy-start.1 = (f32[8,168,128]{2,1,0:T(8,128)}, f32[8,168,128]{2,1,0:T(8,128)S(1)}, u32[]{:S(2)}) copy-start(f32[8,168,128]{2,1,0:T(8,128)S(1)} %bitcast_dynamic-update-slice_fusion.refs_0_.refs_2_.refs_3_.refs_4_.refs_5_.refs_6_.refs_7_.refs_8_.refs_9_) | copy-start | bytes 2064388
  28.6 2.2 %collective-permute-start.8 = (f32[8,168,128]{2,1,0:T(8,128)S(1)}, f32[8,168,128]{2,1,0:T(8,128)S(1)}, u32[]{:S(2)}, u32[]{:S(2)}) collective-permute-start(f32[8,168,128]{2,1,0:T(8,128)S(1)} %bitcast_dynamic-update-slice_fusion.refs_0_.refs_2_.refs_3_.refs_4_.refs_5_.refs_6_.refs_7_.refs_8_.refs_9_), channel_id=1, source_target_pairs={{0,1},{1,0},{2,3},{3,2},{4,5},{5,4},{6,7},{7,6},{8,9},{9,8},{10,11... | collective-permute-start | bytes 2064392 | tf_op jit(solution)/shard_map/ppermute | solution.py:435
  30.8 0.9 %copy-start.2 = (f32[8,168,128]{2,1,0:T(8,128)}, f32[8,168,128]{2,1,0:T(8,128)S(1)}, u32[]{:S(2)}) copy-start(f32[8,168,128]{2,1,0:T(8,128)S(1)} %collective-permute-done.8.refs_1_) | copy-start | bytes 2064388
  47.4 4.4 %collective-permute-start.9 = (f32[16,256,128]{2,1,0:T(8,128)}, f32[16,256,128]{2,1,0:T(8,128)S(1)}, u32[]{:S(2)}, u32[]{:S(2)}) collective-permute-start(f32[16,256,128]{2,1,0:T(8,128)} %field.1.slab), channel_id=1, source_target_pairs={{0,1},{1,0},{2,3},{3,2},{4,5},{5,4},{6,7},{7,6},{8,9},{9,8},{10,11... | collective-permute-start | bytes 6291464 | tf_op jit(solution)/shard_map/ppermute | solution.py:437
  47.4 1.6 %copy-start = (f32[16,256,128]{2,1,0:T(8,128)S(1)}, f32[16,256,128]{2,1,0:T(8,128)}, u32[]{:S(2)}) copy-start(f32[16,256,128]{2,1,0:T(8,128)} %field.1.slab) | copy-start | bytes 6291460

commit v4 on v3

--- a/solution.py
+++ b/solution.py
@@ -63,7 +63,7 @@
         at = slice(c * LANES, (c + 1) * LANES)
         slot = dest[c : c + 1, :]
         mask = rows_hi == slot // LANES
-        right[:, at] = jnp.where(rows_lo == slot % LANES, 1.0, 0.0).astype(BF16)
+        right[c] = jnp.where(rows_lo == slot % LANES, 1.0, 0.0).astype(BF16)
         pieces = []
         for v in range(nvar):
             value = inn[v : v + 1, at]
@@ -72,8 +72,11 @@
         spot = place[c : c + 1, :]
         pieces += [(spot // HALF).astype(F32), (spot % HALF).astype(F32)]
         for q, piece in enumerate(pieces):
-            left[q * chunks : (q + 1) * chunks, at] = jnp.where(mask, piece, 0.0).astype(BF16)
-    packed = nt_dot(left[...], right[...])
+            left[c, q * chunks : (q + 1) * chunks, :] = jnp.where(mask, piece, 0.0).astype(BF16)
+    packed = nt_dot(
+        jnp.concatenate([left[c] for c in range(chunks)], 1),
+        jnp.concatenate([right[c] for c in range(chunks)], 1),
+    )
     for v in range(nvar):
         both = packed[2 * v * chunks : (2 * v + 1) * chunks] + packed[(2 * v + 1) * chunks : (2 * v + 2) * chunks]
         pay[pl.ds(v, chunks, stride=nvar), :] = both
@@ -99,16 +102,16 @@
             pltpu.VMEM((chunks * levels, LANES), BF16),
             pltpu.VMEM((chunks * levels, 2 * LANES), F32),
             pltpu.VMEM((chunks, LANES), jnp.int32),
-            pltpu.VMEM((pieces * chunks, nobs), BF16),
-            pltpu.VMEM((LANES, nobs), BF16),
+            pltpu.VMEM((chunks, pieces * chunks, LANES), BF16),
+            pltpu.VMEM((chunks, LANES, LANES), BF16),
         ],
         compiler_params=pltpu.CompilerParams(vmem_limit_bytes=60 << 20),
         name="route",
     )(innovations, level.reshape(chunks, LANES), owner.reshape(chunks, LANES), local.reshape(chunks, LANES))
 
 
-def table_kernel(width, base, high, low):
-    depth = high.shape[0]
+def table_kernel(width, base, table):
+    depth = table.shape[0]
     row, col = iota((LANES, LANES), 0), iota((LANES, LANES), 1)
     near = jnp.abs(row - col).astype(F32)
     far = jnp.where(col < LANES // 2, LANES - row, row + 1).astype(F32)
@@ -117,20 +120,20 @@
         for at, dist in ((0, near), (LANES, far)):
             full = jnp.exp(-dist / rate)
             top = full.astype(BF16)
-            high[k, :, at : at + LANES] = top
-            low[k, :, at : at + LANES] = (full - top.astype(F32)).astype(BF16)
+            table[k, :LANES, at : at + LANES] = top
+            table[k, LANES:, at : at + LANES] = (full - top.astype(F32)).astype(BF16)
 
 
 def tables(band_width, base, levels):
     depth = 8
-    spec = pl.BlockSpec((depth, LANES, 2 * LANES), lambda i: (i, 0, 0))
-    shape = jax.ShapeDtypeStruct((levels, LANES, 2 * LANES), BF16)
+    spec = pl.BlockSpec((depth, 2 * LANES, 2 * LANES), lambda i: (i, 0, 0))
+    shape = jax.ShapeDtypeStruct((levels, 2 * LANES, 2 * LANES), BF16)
     return pl.pallas_call(
         table_kernel,
         grid=(levels // depth,),
         in_specs=[pl.BlockSpec(memory_space=pltpu.SMEM)] * 2,
-        out_specs=(spec, spec),
-        out_shape=(shape, shape),
+        out_specs=spec,
+        out_shape=shape,
         cost_estimate=pl.CostEstimate(flops=1 << 24, bytes_accessed=8 << 20, transcendentals=1 << 20),
         name="tables",
     )(band_width, base)
@@ -151,77 +154,101 @@
     return high.astype(BF16), (mix - high).astype(BF16)
 
 
-def gather_levels(sources, nvar, chunks, base, levels, own, oth, marks, vals, spots, queue, queue_spot, level_of, total):
+CUES = 8
+
+
+def make_cues(sources, starts_row, chunks, base, levels, own, cue):
+    end = jnp.zeros((1, LANES), jnp.int32)
+    for s in range(sources):
+        start = own[s, starts_row : starts_row + 1, :]
+        size = (pltpu.roll(start, LANES - 1, 1) - start).astype(jnp.int32)
+        start = start.astype(jnp.int32)
+        off, put = start & (LANES - 1), end & (LANES - 1)
+        row = 8 * jnp.minimum(start >> 7, chunks - 1)
+        for j, item in enumerate((row, off, put, put + size, (put - off) & (LANES - 1), 8 * (end >> 7))):
+            cue[CUES * s + j : CUES * s + j + 1, :] = item
+        end = end + size
+    lane = iota((1, LANES), 1)
+    pairs = jnp.where((lane >= base) & (lane < base + levels), (end + 2 * LANES - 1) >> 8, 0).astype(F32)
+    earlier = jnp.where(iota((LANES, LANES), 0) < iota((LANES, LANES), 1), 1.0, 0.0).astype(BF16)
+    before = nn_dot(jnp.broadcast_to(pairs, (8, LANES)).astype(BF16), earlier)[:1]
+    count = jnp.sum(pairs, 1, keepdims=True)
+    last = CUES * sources
+    cue[last : last + 1, :] = before.astype(jnp.int32)
+    cue[last + 1 : last + 2, :] = 8 * (end >> 7)
+    cue[last + 2 : last + 3, :] = jnp.broadcast_to(count, (1, LANES)).astype(jnp.int32)
+
+
+def gather_levels(sources, nvar, chunks, base, levels, own, oth, cue, scalar_cue, sem, vals, spots, queue, queue_spot, level_of):
     lane = iota((8, LANES), 1)
     sub = iota((8, LANES), 0)
+    make_cues(sources, (nvar + 1) * chunks, chunks, base, levels, own, cue)
+    copy = pltpu.make_async_copy(cue, scalar_cue, sem)
+    copy.start()
     for s in range(sources):
         for c in range(0, chunks, 2):
             here, there = own[s, 4 * c : 4 * c + 8, :], oth[s, 4 * c : 4 * c + 8, :]
             vals[s, 8 * c : 8 * c + 8, :] = jnp.where(sub < 4, here, pltpu.roll(there, 4, 0))
             vals[s, 8 * c + 8 : 8 * c + 16, :] = jnp.where(sub < 4, pltpu.roll(here, 4, 0), there)
         vals[s, 8 * chunks :, :] = jnp.zeros((8, LANES), F32)
-        spots[s, :chunks, :] = own[s, nvar * chunks : (nvar + 1) * chunks, :]
-        spots[s, chunks:, :] = jnp.zeros((8, LANES), F32)
+        for c in range(chunks):
+            spot = own[s, nvar * chunks + c : nvar * chunks + c + 1, :]
+            spots[s, 8 * c : 8 * c + 8, :] = jnp.broadcast_to(spot, (8, LANES))
+        spots[s, 8 * chunks :, :] = jnp.zeros((8, LANES), F32)
+    copy.wait()
     nothing = jnp.zeros((8, LANES), F32)
-
-    def rows(chunk):
-        return pl.ds(pl.multiple_of(8 * chunk, 8), 8)
-
-    def per_level(k, pair):
+    last = CUES * sources
+
+    def rows(start):
+        return pl.ds(pl.multiple_of(start, 8), 8)
+
+    def per_level(k):
         lev = base + k
         held, held_spot = nothing, nothing
-        end = jnp.int32(0)
+        pair = scalar_cue[last, lev]
         for s in range(sources):
-            start = marks[s][0, lev].astype(jnp.int32)
-            size = marks[s][0, lev + 1].astype(jnp.int32) - start
-            c, off = jnp.minimum(start >> 7, chunks - 1), start & (LANES - 1)
-            put = end & (LANES - 1)
-            turn = (put - off) & (LANES - 1)
-            value = jnp.where(lane >= off, vals[s, rows(c), :], vals[s, rows(c + 1), :])
+            row, off, put, stop, turn, at = (scalar_cue[CUES * s + j, lev] for j in range(6))
+            first = lane >= off
+            value = jnp.where(first, vals[s, rows(row), :], vals[s, rows(row + 8), :])
             value = pltpu.roll(value, turn, 1)
-            spot = jnp.where(lane[:1] >= off, spots[s, pl.ds(c, 1), :], spots[s, pl.ds(c + 1, 1), :])
-            spot = pltpu.roll(jnp.broadcast_to(spot, (8, LANES)), turn, 1)
-            fresh = (lane >= put) & (lane < put + size)
+            spot = jnp.where(first, spots[s, rows(row), :], spots[s, rows(row + 8), :])
+            spot = pltpu.roll(spot, turn, 1)
+            fresh = (lane >= put) & (lane < stop)
             held = jnp.where(fresh, value, held)
             held_spot = jnp.where(fresh, spot, held_spot)
-            at = rows(2 * pair + (end >> 7))
-            queue[at, :] = held
-            queue_spot[at, :] = held_spot
-            over = put + size - LANES
-            late = lane < over
-            held = jnp.where(over >= 0, jnp.where(late, value, 0.0), held)
-            held_spot = jnp.where(over >= 0, jnp.where(late, spot, 0.0), held_spot)
-            end = end + size
-        at = 2 * pair + (end >> 7)
+            queue[rows(16 * pair + at), :] = held
+            queue_spot[rows(16 * pair + at), :] = held_spot
+            late = lane < stop - LANES
+            over = jnp.broadcast_to(stop, (8, LANES)) >= LANES
+            held = jnp.where(over, jnp.where(late, value, 0.0), held)
+            held_spot = jnp.where(over, jnp.where(late, spot, 0.0), held_spot)
+        at = 16 * pair + scalar_cue[last + 1, lev]
         queue[rows(at), :] = held
         queue_spot[rows(at), :] = held_spot
-        queue[rows(at + 1), :] = nothing
-        queue_spot[rows(at + 1), :] = nothing
-        pairs = (end + 2 * LANES - 1) >> 8
-
-        def note(p, carry):
+        queue[rows(at + 8), :] = nothing
+        queue_spot[rows(at + 8), :] = nothing
+        for p in range(sources // 2):
             level_of[pair + p] = k
-            return carry
-
-        lax.fori_loop(0, pairs, note, 0)
-        return pair + pairs
-
-    def two_levels(k, pair):
-        return per_level(2 * k + 1, per_level(2 * k, pair))
-
-    pair = lax.fori_loop(0, levels // 2, two_levels, jnp.int32(0))
+
+    def group(g, carry):
+        for p in range(2):
+            per_level(2 * g + p)
+        return carry
+
+    lax.fori_loop(0, levels // 2, group, 0)
+    pair = scalar_cue[last + 2, 0]
     for p in range(UNROLL):
         level_of[pair + p] = levels
         for h in range(2):
-            queue[rows(2 * (pair + p) + h), :] = nothing
-            queue_spot[rows(2 * (pair + p) + h), :] = nothing
-    total[0] = pair
+            queue[rows(16 * (pair + p) + 8 * h), :] = nothing
+            queue_spot[rows(16 * (pair + p) + 8 * h), :] = nothing
+    return pair
 
 
 UNROLL = 8
 
 
-def spread(wide, levels, base, width, first, queue, queue_spot, level_of, total, field):
+def spread(wide, levels, base, width, first, queue, queue_spot, level_of, count, field):
     sub = iota((8, LANES), 0)
     col = first[0] + sub % 4
     reach = jnp.where(sub < 4, col, 2 * wide - col).astype(F32)
@@ -266,10 +293,10 @@
             field[k] = field[k] + jnp.concatenate(parts, 0)
         return carry
 
-    lax.fori_loop(0, (total[0] + UNROLL - 1) // UNROLL, group, 0)
-
-
-def filter_levels(levels, base, width, high, low, field, slab):
+    lax.fori_loop(0, (count + UNROLL - 1) // UNROLL, group, 0)
+
+
+def filter_levels(levels, base, width, table, field, slab):
     lane = iota((8, LANES), 1)
     line = lane.astype(F32)
 
@@ -282,8 +309,8 @@
         grid = jnp.concatenate(blocks, 0)
         top = grid.astype(BF16)
         rest = (grid - top.astype(F32)).astype(BF16)
-        mat = high[k]
-        done = nn_dot(jnp.concatenate([top, rest], 1), jnp.concatenate([mat, mat], 0)) + nn_dot(top, low[k])
+        mat = table[k, :LANES, :]
+        done = nn_dot(jnp.concatenate([top, rest], 1), jnp.concatenate([mat, mat], 0)) + nn_dot(top, table[k, LANES:, :])
         rise = jnp.exp(line * slope)
         fall = jnp.exp((LANES - 1.0 - line) * slope)
         edge = jnp.exp((LANES - line) * slope)
@@ -307,7 +334,7 @@
                 here[b] = here[b] + fall * run
                 run = behind[b] + hop * run
             for b in (3, 2, 1, 0):
-                slab[4 * x + b, pl.ds(pl.multiple_of(8 * k, 8), 8), :] = here[b] - bound
+                slab[x, b, pl.ds(pl.multiple_of(8 * k, 8), 8), :] = here[b] - bound
                 bound = bound * hop
 
     def group(g, carry):
@@ -318,92 +345,86 @@
     lax.fori_loop(0, levels // 4, group, 0)
 
 
-def field_kernel(sources, wide, nvar, width, first, start, *refs):
-    own, oth, *marks = refs[: 2 + sources]
-    far_high, far_low, slab, high, low, sems, vals, spots, queue, queue_spot, level_of, total, field = refs[2 + sources :]
+def field_kernel(sources, wide, nvar, width, first, start, own, oth, far_table, slab, *scratch):
+    table, table_sem, cue, scalar_cue, sem, vals, spots, queue, queue_spot, level_of, field = scratch
     chunks = (own.shape[1] - 8) // (nvar + 1)
-    levels = high.shape[0]
-    copies = [pltpu.make_async_copy(far_high, high, sems.at[0]), pltpu.make_async_copy(far_low, low, sems.at[1])]
-    for copy in copies:
-        copy.start()
+    levels = table.shape[0]
     base = start[0]
-    gather_levels(
-        sources, nvar, chunks, base, levels, own, oth, marks, vals, spots, queue, queue_spot, level_of, total
+    fetch = pltpu.make_async_copy(far_table, table, table_sem)
+    fetch.start()
+    count = gather_levels(
+        sources, nvar, chunks, base, levels, own, oth, cue, scalar_cue, sem, vals, spots, queue, queue_spot, level_of
     )
-    spread(wide, levels, base, width, first, queue, queue_spot, level_of, total, field)
-    for copy in copies:
-        copy.wait()
-    filter_levels(levels, base, width, high, low, field, slab)
-
-
-def make_field(own, oth, band_width, first, base, high, low, nvar, levels, wide):
+    spread(wide, levels, base, width, first, queue, queue_spot, level_of, count, field)
+    fetch.wait()
+    filter_levels(levels, base, width, table, field, slab)
+
+
+def make_field(own, oth, band_width, first, base, table, nvar, levels, wide):
     sources, rows, _ = own.shape
     chunks = (rows - 8) // (nvar + 1)
     whole = pl.BlockSpec(memory_space=pltpu.VMEM)
-    marks = [
-        pl.BlockSpec((None, 8, LANES), functools.partial(lambda s, i: (s, rows // 8 - 1, 0), s), memory_space=pltpu.SMEM)
-        for s in range(sources)
-    ]
     smem = pl.BlockSpec(memory_space=pltpu.SMEM)
     pairs = levels * sources // 2 + UNROLL + 1
     return pl.pallas_call(
         functools.partial(field_kernel, sources, wide, nvar),
-        grid=(1,),
-        in_specs=[smem] * 3 + [whole] * 2 + marks + [pl.BlockSpec(memory_space=pltpu.HBM)] * 2,
+        in_specs=[smem] * 3 + [whole] * 2 + [pl.BlockSpec(memory_space=pltpu.HBM)],
         out_specs=whole,
-        out_shape=jax.ShapeDtypeStruct((4 * NX_DEV, 2 * nvar * levels, LANES), F32),
+        out_shape=jax.ShapeDtypeStruct((NX_DEV, 4, 2 * nvar * levels, LANES), F32),
         scratch_shapes=[
-            pltpu.VMEM(high.shape, BF16),
-            pltpu.VMEM(low.shape, BF16),
-            pltpu.SemaphoreType.DMA((2,)),
+            pltpu.VMEM(table.shape, BF16),
+            pltpu.SemaphoreType.DMA,
+            pltpu.VMEM((CUES * sources + 8, LANES), jnp.int32),
+            pltpu.SMEM((CUES * sources + 8, LANES), jnp.int32),
+            pltpu.SemaphoreType.DMA,
             pltpu.VMEM((sources, 8 * chunks + 8, LANES), F32),
-            pltpu.VMEM((sources, chunks + 8, LANES), F32),
+            pltpu.VMEM((sources, 8 * chunks + 8, LANES), F32),
             pltpu.VMEM((16 * pairs, LANES), F32),
             pltpu.VMEM((16 * pairs, LANES), F32),
-            pltpu.SMEM((pairs,), jnp.int32),
-            pltpu.SMEM((1,), jnp.int32),
+            pltpu.SMEM((pairs + sources,), jnp.int32),
             pltpu.VMEM((levels + 1, 16 * NX_DEV, HALF), F32),
         ],
-        compiler_params=pltpu.CompilerParams(vmem_limit_bytes=56 << 20),
+        compiler_params=pltpu.CompilerParams(vmem_limit_bytes=50 << 20),
         name="field",
-    )(band_width, first, base, own, oth, *([own] * sources), high, low)
+    )(band_width, first, base, own, oth, table)
 
 
 def mix_kernel(slab, high, low, *refs):
     out = refs[-1]
-    x = pl.program_id(0)
-    for h in range(2):
-        part = jnp.concatenate([slab[2 * h], slab[2 * h + 1]], 1)
+    rows = high.shape[0]
+    for x in range(NX_DEV):
+        part = jnp.concatenate([slab[x, 0], slab[x, 1]], 1)
         top = part.astype(BF16)
         rest = (part - top.astype(F32)).astype(BF16)
-        term = nn_dot(high[...], top) + nn_dot(high[...], rest) + nn_dot(low[...], top)
+        term = nn_dot(jnp.concatenate([high[...], low[...]], 0), top)
+        term = term[:rows] + term[rows:] + nn_dot(high[...], rest)
         if len(refs) == 1:
-            out[0, :, h * HALF : (h + 1) * HALF] = term
+            out[0, x] = term
         else:
-            term = term + refs[0][0, :, h * HALF : (h + 1) * HALF]
+            term = term + refs[0][0, x]
+            flat = out.reshape(8 * term.shape[0], LANES)
             for g in range(2):
-                rows = pl.ds(8 * h + 4 * g + x, term.shape[0], stride=4 * NX_DEV)
-                out[rows, :] = term[:, g * LANES : (g + 1) * LANES]
+                flat[pl.ds(4 * g + x, term.shape[0], stride=8), :] = term[:, g * LANES : (g + 1) * LANES]
 
 
 def mix(slab, mats, *before):
     rows, depth = mats[0].shape
-    strip = pl.BlockSpec((4, depth, LANES), lambda i: (i, 0, 0))
+    strip = pl.BlockSpec((NX_DEV, 2, depth, LANES), lambda i: (0, i, 0, 0))
     matrix = pl.BlockSpec((rows, depth), lambda i: (0, 0))
-    partial = pl.BlockSpec((1, rows, NY), lambda i: (i, 0, 0))
+    partial = pl.BlockSpec((1, NX_DEV, rows, HALF), lambda i: (i, 0, 0, 0))
     if before:
-        shape = (rows * NX_DEV * NY // LANES, LANES)
-        out_spec = pl.BlockSpec(shape, lambda i: (0, 0))
+        shape = (rows, 16, LANES)
+        out_spec = pl.BlockSpec((rows, 8, LANES), lambda i: (0, i, 0))
     else:
-        shape = (NX_DEV, rows, NY)
+        shape = (2, NX_DEV, rows, HALF)
         out_spec = partial
     return pl.pallas_call(
         mix_kernel,
-        grid=(NX_DEV,),
+        grid=(2,),
         in_specs=[strip, matrix, matrix] + [partial] * len(before),
         out_specs=out_spec,
         out_shape=jax.ShapeDtypeStruct(shape, F32),
-        compiler_params=pltpu.CompilerParams(vmem_limit_bytes=32 << 20),
+        compiler_params=pltpu.CompilerParams(vmem_limit_bytes=16 << 20),
         cost_estimate=pl.CostEstimate(flops=1 << 30, bytes_accessed=6 << 20, transcendentals=0),
         name="mix",
     )(slab, *mats, *before)
@@ -424,16 +445,17 @@
     oth_mats = mix_matrix(jnp.concatenate([theirs, vert_scale], 0), sigma, jnp.roll(weights, nvar, 1), last, half)
     first = (lax.axis_index("sub") * NX_DEV).astype(jnp.int32).reshape(1)
     base = base.reshape(1)
-    high, low = tables(band_width, base, half)
     own = [unit]
     for k in range(2, groups, 2):
         own.append(lax.ppermute(unit, "sub", [(i, (i + k) % groups) for i in range(groups)]))
-    own[-1], high, low = lax.optimization_barrier((own[-1], high, low))
+    far = len(own) // 2
+    own[far], own_mats, oth_mats, when = lax.optimization_barrier((own[far], own_mats, oth_mats, base))
+    table = tables(band_width, when, half)
     own += [lax.ppermute(held, "sub", [(i, i ^ 1) for i in range(groups)]) for held in own]
-    own[-1], own_mats, oth_mats = lax.optimization_barrier((own[-1], own_mats, oth_mats))
+    own[-1], table = lax.optimization_barrier((own[-1], table))
     own = jnp.stack(own)
     oth = lax.ppermute(own, "var", swap)
-    slab = make_field(own, oth, band_width, first, base, high, low, nvar, half, NX_DEV * groups)
+    slab = make_field(own, oth, band_width, first, base, table, nvar, half, NX_DEV * groups)
     swapped = lax.ppermute(slab, "var", swap)
     out = mix(swapped, oth_mats, mix(slab, own_mats))
     out = out.reshape(nvar, levels, NY // LANES, NX_DEV, LANES)

time: 55.4 us -> 47.6 us (0.86)
  Pallas kernels: 28.3 us -> 23.7 us
  local copies, waits for them, and re-layouts: 6.11 us -> 3.67 us
  waiting for transfers between devices: 8.58 us -> 6.81 us
  other arithmetic: 1.39 us -> 2.15 us
    pallas_call x3, Pallas kernels: 20.5 us -> 16.1 us  [the longest x1 12.3 us: make_field(): pl.pallas_call(functools.partial(field_kernel, sources, wide, nvar), in_s...]
    ppermute x4, waiting for transfers between devices: 5.27 us -> 1.19 us  [on_device(): lax.ppermute(held, 'sub', [(i, i ^ 1) for i in range(groups)])]
    unnamed x15 -> x9, local copies, waits for them, and re-layouts: 3.41 us -> 0.98 us
    ppermute x1, waiting for transfers between devices: 1.17 us -> 2.69 us  [on_device(): swapped = lax.ppermute(slab, 'var', swap)]
    ppermute x3, waiting for transfers between devices: 0.01 us -> 0.8 us  [on_device(): lax.ppermute(unit, 'sub', [(i, (i + k) % groups) for i in range(groups)])]
    transpose x1, other arithmetic: 0.01 us -> 0.77 us  [mix_matrix(): own = jnp.tile(scale.T, (1, depth))]
  transfers between devices with their start and end apart: 10 -> 10, of which waited for: 3 -> 5; matrix products, arithmetic and copies ran while one was open for 9% -> 12% of each run, Pallas kernels for 9% -> 11%
where the time goes in v4:
time: 47.6 us; the launch traced here: 47 us
  Pallas kernels  23.7 us (50%)
  starting transfers between devices  10.5 us (22%)
  waiting for transfers between devices  6.81 us (14%)
  local copies, waits for them, and re-layouts  3.67 us (8%)
  other arithmetic  2.15 us (5%)
    pallas_call x1, Pallas kernels, make_field(): pl.pallas_call(functools.partial(field_kernel, sources, wide, nvar), in_s...  12.3 us
    ppermute x4, starting transfers between devices, on_device(): lax.ppermute(held, 'sub', [(i, i ^ 1) for i in range(groups)])  5.66 us
    ppermute x3, starting transfers between devices, on_device(): lax.ppermute(unit, 'sub', [(i, (i + k) % groups) for i in range(groups)])  4.61 us
    pallas_call x1, Pallas kernels, route(): pl.pallas_call(route_kernel, out_shape=jax.ShapeDtypeStruct(((nvar + 1) *...  3.95 us
    pallas_call x2, Pallas kernels, mix(): pl.pallas_call(mix_kernel, grid=(2,), in_specs=[strip, matrix, matrix] +...  3.74 us
    pallas_call x1, Pallas kernels, tables(): pl.pallas_call(table_kernel, grid=(levels // depth,), in_specs=[pl.BlockS...  3.65 us
    ppermute x1, waiting for transfers between devices, on_device(): swapped = lax.ppermute(slab, 'var', swap)  2.69 us
    ppermute x1, waiting for transfers between devices, on_device(): oth = lax.ppermute(own, 'var', swap)  2.13 us
  transfers between devices with their start and end apart: 10, of which 5 were waited for; matrix products, arithmetic and copies ran while one was open for 12% of the time, Pallas kernels for 11%

profile of v4, /device:TPU:0, one launch (start us, length us, event | category | flops | bytes accessed | tf_op | source)
XLA Modules:
  0.0 47.0 jit_solution(11968068465569547417)
XLA Ops:
  0.0 3.9 %route.1 = f32[168,128]{1,0:T(8,128)} custom-call(f32[4,4096]{1,0:T(4,128)} %inn_ref.1, s32[32,128]{1,0:T(8,128)} %bitcast.70, s32[32,128]{1,0:T(8,128)} %bitcast.71, s32[32,128]{1,0:T(8,128)} %bitcast.72), custom_call_target="tpu_custom_call" | custom-call | tf_op jit(solution)/shard_map/route/pallas_call | solution.py:92
  4.0 3.0 %collective-permute-start.4 = (f32[168,128]{1,0:T(8,128)}, f32[168,128]{1,0:T(8,128)S(1)}, u32[]{:S(2)}, u32[]{:S(2)}) collective-permute-start(f32[168,128]{1,0:T(8,128)} %route.1), channel_id=1, source_target_pairs={{0,2},{2,0},{4,6},{6,4},{8,10},{10,8},{12,14},{14,12},{1,3},{3,1},... | collective-permute-start | bytes 258056 | tf_op jit(solution)/shard_map/ppermute | solution.py:454
  7.0 3.6 %collective-permute-start.3 = (f32[168,128]{1,0:T(8,128)}, f32[168,128]{1,0:T(8,128)S(1)}, u32[]{:S(2)}, u32[]{:S(2)}) collective-permute-start(f32[168,128]{1,0:T(8,128)} %route.1), channel_id=1, source_target_pairs={{0,12},{2,14},{4,0},{6,2},{8,4},{10,6},{12,8},{14,10},{1,13},{3,15... | collective-permute-start | bytes 258056 | tf_op jit(solution)/shard_map/ppermute | solution.py:450
  10.6 0.0 collective-permute-start.1
  10.6 1.0 %collective-permute-start = (f32[168,128]{1,0:T(8,128)}, f32[168,128]{1,0:T(8,128)S(1)}, u32[]{:S(2)}, u32[]{:S(2)}) collective-permute-start(f32[168,128]{1,0:T(8,128)} %route.1), channel_id=1, source_target_pairs={{0,4},{2,6},{4,8},{6,10},{8,12},{10,14},{12,0},{14,2},{1,5},{3,7},... | collective-permute-start | bytes 258056 | tf_op jit(solution)/shard_map/ppermute | solution.py:450
  11.6 0.0 collective-permute-start.2
  11.6 0.9 %bitcast_dynamic-update-slice_fusion.7 = f32[8,168,128]{2,1,0:T(8,128)S(1)} fusion(f32[168,128]{1,0:T(8,128)} %route.1), kind=kLoop, calls=%fused_computation.29 | loop fusion | bytes 172032
  12.5 0.8 %fusion.11 = (f32[4,4]{1,0:T(4,128)S(1)}, f32[4,4]{1,0:T(4,128)S(1)}) fusion(f32[4,8]{1,0:T(4,128)} %param.15), kind=kLoop, calls=%fused_computation.41 | loop fusion | bytes 256 | tf_op jit(solution)/shard_map/jit(_roll_static)/slice | solution.py:443
  13.4 0.8 %maximum_select_fusion = f32[4,8]{1,0:T(4,128)S(1)} fusion(f32[4,8]{1,0:T(4,128)} %param.15, f32[4,4]{1,0:T(4,128)S(1)} %get-tuple-element.32, f32[4,4]{1,0:T(4,128)S(1)} %get-tuple-element.31, pred[]{:T(512)S(6)} %eq.3), kind=kLoop, calls=%fused_computation.34 | loop fusion | flops 64 | bytes 385 | tf_op jit(solution)/shard_map/jit(_where)/select_n | solution.py:443
  14.1 0.1 fusion.10
  14.2 0.1 pad_maximum_fusion.2
  14.3 0.8 %mul.119 = f32[256]{0:T(256)S(1)} reshape(f32[4,64]{1,0:T(4,128)} %param.14) | data formatting | bytes 2048 | tf_op jit(solution)/shard_map/mul | solution.py:151
  15.0 0.1 broadcast_in_dim.9
  15.1 0.1 sub.48
  15.2 0.1 broadcast_in_dim.19
  15.3 0.1 sub.54
  15.4 0.1 tile.39
  15.5 0.1 tile.17
  15.6 0.8 %fusion.8 = (f32[64,8]{0,1:T(8,128)S(1)}, f32[64,8]{0,1:T(8,128)S(1)}, f32[8,64]{1,0:T(8,128)S(1)}, f32[8,64]{1,0:T(8,128)S(1)}) fusion(f32[4,64]{1,0:T(4,128)} %param.13, f32[4,64]{1,0:T(4,128)S(1)} %collective-permute-done.2), kind=kLoop, calls=%fused_computation.38 | loop fusion | flops 1024 | bytes 10240 | tf_op jit(solution)/shard_map/transpose | solution.py:146
  16.4 0.1 multiply_bitcast_fusion.1
  16.4 0.1 copy.12
  16.5 0.1 mul.128
  16.6 0.1 multiply_bitcast_fusion
  16.7 0.1 copy.14
  16.8 0.1 mul.141
  16.9 0.2 fusion.4
  17.1 0.1 copy.13
  17.2 0.1 copy.15
  17.3 0.2 fusion.1
  17.4 0.8 %collective-permute-done.1 = f32[168,128]{1,0:T(8,128)S(1)} collective-permute-done((f32[168,128]{1,0:T(8,128)}, f32[168,128]{1,0:T(8,128)S(1)}, u32[]{:S(2)}, u32[]{:S(2)}) %collective-permute-start.1) | collective-permute-done | bytes 86048 | tf_op jit(solution)/shard_map/ppermute | solution.py:450
  18.2 0.5 %collective-permute-start.6 = (f32[168,128]{1,0:T(8,128)S(1)}, f32[168,128]{1,0:T(8,128)S(1)}, u32[]{:S(2)}, u32[]{:S(2)}) collective-permute-start(f32[168,128]{1,0:T(8,128)S(1)} %collective-permute-done.1), channel_id=1, source_target_pairs={{0,2},{2,0},{4,6},{6,4},{8,10},{10,8},{12,14},{14,12},{1,3},{3,1},... | collective-permute-start | bytes 258056 | tf_op jit(solution)/shard_map/ppermute | solution.py:454
  18.7 0.0 collective-permute-done
  18.8 1.6 %collective-permute-start.5 = (f32[168,128]{1,0:T(8,128)S(1)}, f32[168,128]{1,0:T(8,128)S(1)}, u32[]{:S(2)}, u32[]{:S(2)}) collective-permute-start(f32[168,128]{1,0:T(8,128)S(1)} %collective-permute-done), channel_id=1, source_target_pairs={{0,2},{2,0},{4,6},{6,4},{8,10},{10,8},{12,14},{14,12},{1,3},{3,1},... | collective-permute-start | bytes 258056 | tf_op jit(solution)/shard_map/ppermute | solution.py:454
  20.3 0.0 collective-permute-done.3
  20.4 0.5 %collective-permute-start.7 = (f32[168,128]{1,0:T(8,128)S(1)}, f32[168,128]{1,0:T(8,128)S(1)}, u32[]{:S(2)}, u32[]{:S(2)}) collective-permute-start(f32[168,128]{1,0:T(8,128)S(1)} %collective-permute-done.3), channel_id=1, source_target_pairs={{0,2},{2,0},{4,6},{6,4},{8,10},{10,8},{12,14},{14,12},{1,3},{3,1},... | collective-permute-start | bytes 258056 | tf_op jit(solution)/shard_map/ppermute | solution.py:454
  20.9 0.0 collective-permute-done.4
  20.9 0.0 copy-start
  20.9 3.7 %tables.1.far_table = bf16[32,256,256]{2,1,0:T(8,128)(2,1)} custom-call(s32[64]{0:T(128)} %width.3, s32[1]{0:T(128)} %bitcast.1.base.start), custom_call_target="tpu_custom_call" | custom-call | flops 16777216 | bytes 8388608 | tf_op jit(solution)/shard_map/tables/pallas_call | solution.py:131
  24.6 0.3 collective-permute-done.5
  24.9 0.9 %collective-permute-done.7 = f32[168,128]{1,0:T(8,128)S(1)} collective-permute-done((f32[168,128]{1,0:T(8,128)S(1)}, f32[168,128]{1,0:T(8,128)S(1)}, u32[]{:S(2)}, u32[]{:S(2)}) %collective-permute-start.7) | collective-permute-done | bytes 86048 | tf_op jit(solution)/shard_map/ppermute | solution.py:454
  25.8 0.0 collective-permute-done.6
  25.8 0.1 collective-permute-start.8
  25.9 2.1 %collective-permute-done.8.oth = f32[8,168,128]{2,1,0:T(8,128)S(1)} collective-permute-done((f32[8,168,128]{2,1,0:T(8,128)S(1)}, f32[8,168,128]{2,1,0:T(8,128)S(1)}, u32[]{:S(2)}, u32[]{:S(2)}) %collective-permute-start.8) | collective-permute-done | bytes 688160 | tf_op jit(solution)/shard_map/ppermute | solution.py:457
  28.0 12.3 %field.1.slab = f32[4,4,256,128]{3,2,1,0:T(8,128)S(1)} custom-call(s32[64]{0:T(128)S(1)} %copy-done, s32[1]{0:T(128)} %bitcast.first, s32[1]{0:T(128)} %bitcast.1.base.start, f32[8,168,128]{2,1,0:T(8,128)S(1)} %bitcast_dynamic-update-slice_fusion.own, f32[8,168,128]{2,1,0:T(8,128)S(1)} %collective-permute-done.8.oth, bf16[32,256,256]{2,1,0:T(8,128)(2,1)} %tables.1.far_table), custom_call_target="tpu_custom_call" | custom-call | tf_op jit(solution)/shard_map/field/pallas_call | solution.py:369
  40.4 0.2 collective-permute-start.9
  40.6 1.3 %mix.2.refs_0_ = f32[2,4,256,256]{3,2,1,0:T(8,128)S(1)} custom-call(f32[4,4,256,128]{3,2,1,0:T(8,128)S(1)} %field.1.slab, bf16[256,256]{1,0:T(8,128)(2,1)S(1)} %get-tuple-element.19.high, bf16[256,256]{1,0:T(8,128)(2,1)S(1)} %get-tuple-element.20.low), custom_call_target="tpu_custom_call" | custom-call | flops 1073741824 | bytes 6291456 | tf_op jit(solution)/shard_map/mix/pallas_call | solution.py:421
  41.9 2.7 %collective-permute-done.9.slab = f32[4,4,256,128]{3,2,1,0:T(8,128)S(1)} collective-permute-done((f32[4,4,256,128]{3,2,1,0:T(8,128)S(1)}, f32[4,4,256,128]{3,2,1,0:T(8,128)S(1)}, u32[]{:S(2)}, u32[]{:S(2)}) %collective-permute-start.9) | collective-permute-done | bytes 2097184 | tf_op jit(solution)/shard_map/ppermute | solution.py:459
  44.6 2.4 %mix.3 = f32[256,16,128]{2,1,0:T(8,128)} custom-call(f32[4,4,256,128]{3,2,1,0:T(8,128)S(1)} %collective-permute-done.9.slab, bf16[256,256]{1,0:T(8,128)(2,1)S(1)} %get-tuple-element.17.high, bf16[256,256]{1,0:T(8,128)(2,1)S(1)} %get-tuple-element.18.low, f32[2,4,256,256]{3,2,1,0:T(8,128)S(1)} %mix.2.refs_0_), custom_call_target="tpu_custom_call" | custom-call | flops 1073741824 | bytes 6291456 | tf_op jit(solution)/shard_map/mix/pallas_call | solution.py:421
  (13 shorter events, 0.1 us)
Async XLA Ops:
  4.0 16.9 %collective-permute-start.4 = (f32[168,128]{1,0:T(8,128)}, f32[168,128]{1,0:T(8,128)S(1)}, u32[]{:S(2)}, u32[]{:S(2)}) collective-permute-start(f32[168,128]{1,0:T(8,128)} %route.1), channel_id=1, source_target_pairs={{0,2},{2,0},{4,6},{6,4},{8,10},{10,8},{12,14},{14,12},{1,3},{3,1},... | collective-permute-start | bytes 258056 | tf_op jit(solution)/shard_map/ppermute | solution.py:454
  7.0 13.4 %collective-permute-start.3 = (f32[168,128]{1,0:T(8,128)}, f32[168,128]{1,0:T(8,128)S(1)}, u32[]{:S(2)}, u32[]{:S(2)}) collective-permute-start(f32[168,128]{1,0:T(8,128)} %route.1), channel_id=1, source_target_pairs={{0,12},{2,14},{4,0},{6,2},{8,4},{10,6},{12,8},{14,10},{1,13},{3,15... | collective-permute-start | bytes 258056 | tf_op jit(solution)/shard_map/ppermute | solution.py:450
  10.6 7.6 %collective-permute-start.1 = (f32[168,128]{1,0:T(8,128)}, f32[168,128]{1,0:T(8,128)S(1)}, u32[]{:S(2)}, u32[]{:S(2)}) collective-permute-start(f32[168,128]{1,0:T(8,128)} %route.1), channel_id=1, source_target_pairs={{0,8},{2,10},{4,12},{6,14},{8,0},{10,2},{12,4},{14,6},{1,9},{3,11}... | collective-permute-start | bytes 258056 | tf_op jit(solution)/shard_map/ppermute | solution.py:450
  10.6 8.1 %collective-permute-start = (f32[168,128]{1,0:T(8,128)}, f32[168,128]{1,0:T(8,128)S(1)}, u32[]{:S(2)}, u32[]{:S(2)}) collective-permute-start(f32[168,128]{1,0:T(8,128)} %route.1), channel_id=1, source_target_pairs={{0,4},{2,6},{4,8},{6,10},{8,12},{10,14},{12,0},{14,2},{1,5},{3,7},... | collective-permute-start | bytes 258056 | tf_op jit(solution)/shard_map/ppermute | solution.py:450
  11.6 4.0 %collective-permute-start.2 = (f32[4,64]{1,0:T(4,128)}, f32[4,64]{1,0:T(4,128)S(1)}, u32[]{:S(2)}, u32[]{:S(2)}) collective-permute-start(f32[4,64]{1,0:T(4,128)} %param.13), channel_id=1, source_target_pairs={{0,1},{1,0},{2,3},{3,2},{4,5},{5,4},{6,7},{7,6},{8,9},{9,8},{10,11... | collective-permute-start | bytes 3080 | tf_op jit(solution)/shard_map/ppermute | solution.py:442
  18.2 7.6 %collective-permute-start.6 = (f32[168,128]{1,0:T(8,128)S(1)}, f32[168,128]{1,0:T(8,128)S(1)}, u32[]{:S(2)}, u32[]{:S(2)}) collective-permute-start(f32[168,128]{1,0:T(8,128)S(1)} %collective-permute-done.1), channel_id=1, source_target_pairs={{0,2},{2,0},{4,6},{6,4},{8,10},{10,8},{12,14},{14,12},{1,3},{3,1},... | collective-permute-start | bytes 258056 | tf_op jit(solution)/shard_map/ppermute | solution.py:454
  18.8 6.1 %collective-permute-start.5 = (f32[168,128]{1,0:T(8,128)S(1)}, f32[168,128]{1,0:T(8,128)S(1)}, u32[]{:S(2)}, u32[]{:S(2)}) collective-permute-start(f32[168,128]{1,0:T(8,128)S(1)} %collective-permute-done), channel_id=1, source_target_pairs={{0,2},{2,0},{4,6},{6,4},{8,10},{10,8},{12,14},{14,12},{1,3},{3,1},... | collective-permute-start | bytes 258056 | tf_op jit(solution)/shard_map/ppermute | solution.py:454
  20.4 5.4 %collective-permute-start.7 = (f32[168,128]{1,0:T(8,128)S(1)}, f32[168,128]{1,0:T(8,128)S(1)}, u32[]{:S(2)}, u32[]{:S(2)}) collective-permute-start(f32[168,128]{1,0:T(8,128)S(1)} %collective-permute-done.3), channel_id=1, source_target_pairs={{0,2},{2,0},{4,6},{6,4},{8,10},{10,8},{12,14},{14,12},{1,3},{3,1},... | collective-permute-start | bytes 258056 | tf_op jit(solution)/shard_map/ppermute | solution.py:454
  20.9 7.1 %copy-start = (s32[64]{0:T(128)S(1)}, s32[64]{0:T(128)}, u32[]{:S(2)}) copy-start(s32[64]{0:T(128)} %width.3) | copy-start | bytes 772
  25.8 2.2 %collective-permute-start.8 = (f32[8,168,128]{2,1,0:T(8,128)S(1)}, f32[8,168,128]{2,1,0:T(8,128)S(1)}, u32[]{:S(2)}, u32[]{:S(2)}) collective-permute-start(f32[8,168,128]{2,1,0:T(8,128)S(1)} %bitcast_dynamic-update-slice_fusion.own), channel_id=1, source_target_pairs={{0,1},{1,0},{2,3},{3,2},{4,5},{5,4},{6,7},{7,6},{8,9},{9,8},{10,11... | collective-permute-start | bytes 2064392 | tf_op jit(solution)/shard_map/ppermute | solution.py:457
  40.4 4.2 %collective-permute-start.9 = (f32[4,4,256,128]{3,2,1,0:T(8,128)S(1)}, f32[4,4,256,128]{3,2,1,0:T(8,128)S(1)}, u32[]{:S(2)}, u32[]{:S(2)}) collective-permute-start(f32[4,4,256,128]{3,2,1,0:T(8,128)S(1)} %field.1.slab), channel_id=1, source_target_pairs={{0,1},{1,0},{2,3},{3,2},{4,5},{5,4},{6,7},{7,6},{8,9},{9,8},{10,11... | collective-permute-start | bytes 6291464 | tf_op jit(solution)/shard_map/ppermute | solution.py:459

commit v5 on v4

--- a/solution.py
+++ b/solution.py
@@ -154,79 +154,84 @@
     return high.astype(BF16), (mix - high).astype(BF16)
 
 
-CUES = 8
+CUES = 4
 
 
 def make_cues(sources, starts_row, chunks, base, levels, own, cue):
     end = jnp.zeros((1, LANES), jnp.int32)
+    goals = []
     for s in range(sources):
         start = own[s, starts_row : starts_row + 1, :]
         size = (pltpu.roll(start, LANES - 1, 1) - start).astype(jnp.int32)
         start = start.astype(jnp.int32)
         off, put = start & (LANES - 1), end & (LANES - 1)
-        row = 8 * jnp.minimum(start >> 7, chunks - 1)
-        for j, item in enumerate((row, off, put, put + size, (put - off) & (LANES - 1), 8 * (end >> 7))):
+        row = 16 * jnp.minimum(start >> 7, chunks - 1)
+        for j, item in enumerate((row, (put - off) & (LANES - 1), off + (put << 7) + ((put + size) << 14))):
             cue[CUES * s + j : CUES * s + j + 1, :] = item
+        goals.append(16 * (end >> 7))
         end = end + size
     lane = iota((1, LANES), 1)
     pairs = jnp.where((lane >= base) & (lane < base + levels), (end + 2 * LANES - 1) >> 8, 0).astype(F32)
     earlier = jnp.where(iota((LANES, LANES), 0) < iota((LANES, LANES), 1), 1.0, 0.0).astype(BF16)
-    before = nn_dot(jnp.broadcast_to(pairs, (8, LANES)).astype(BF16), earlier)[:1]
+    before = nn_dot(jnp.broadcast_to(pairs, (8, LANES)).astype(BF16), earlier)[:1].astype(jnp.int32)
     count = jnp.sum(pairs, 1, keepdims=True)
+    for s, goal in enumerate(goals):
+        cue[CUES * s + 3 : CUES * s + 4, :] = 32 * before + goal
     last = CUES * sources
-    cue[last : last + 1, :] = before.astype(jnp.int32)
-    cue[last + 1 : last + 2, :] = 8 * (end >> 7)
+    cue[last : last + 1, :] = before
+    cue[last + 1 : last + 2, :] = 32 * before + 16 * (end >> 7)
     cue[last + 2 : last + 3, :] = jnp.broadcast_to(count, (1, LANES)).astype(jnp.int32)
 
 
-def gather_levels(sources, nvar, chunks, base, levels, own, oth, cue, scalar_cue, sem, vals, spots, queue, queue_spot, level_of):
+def gather_levels(sources, nvar, chunks, base, levels, own, oth, cue, scalar_cue, sem, store, queue, level_of):
     lane = iota((8, LANES), 1)
     sub = iota((8, LANES), 0)
     make_cues(sources, (nvar + 1) * chunks, chunks, base, levels, own, cue)
     copy = pltpu.make_async_copy(cue, scalar_cue, sem)
     copy.start()
+    nothing = jnp.zeros((8, LANES), F32)
     for s in range(sources):
         for c in range(0, chunks, 2):
             here, there = own[s, 4 * c : 4 * c + 8, :], oth[s, 4 * c : 4 * c + 8, :]
-            vals[s, 8 * c : 8 * c + 8, :] = jnp.where(sub < 4, here, pltpu.roll(there, 4, 0))
-            vals[s, 8 * c + 8 : 8 * c + 16, :] = jnp.where(sub < 4, pltpu.roll(here, 4, 0), there)
-        vals[s, 8 * chunks :, :] = jnp.zeros((8, LANES), F32)
+            store[s, 16 * c : 16 * c + 8, :] = jnp.where(sub < 4, here, pltpu.roll(there, 4, 0))
+            store[s, 16 * c + 16 : 16 * c + 24, :] = jnp.where(sub < 4, pltpu.roll(here, 4, 0), there)
         for c in range(chunks):
             spot = own[s, nvar * chunks + c : nvar * chunks + c + 1, :]
-            spots[s, 8 * c : 8 * c + 8, :] = jnp.broadcast_to(spot, (8, LANES))
-        spots[s, 8 * chunks :, :] = jnp.zeros((8, LANES), F32)
+            store[s, 16 * c + 8 : 16 * c + 16, :] = jnp.broadcast_to(spot, (8, LANES))
+        store[s, 16 * chunks :, :] = jnp.zeros((16, LANES), F32)
     copy.wait()
-    nothing = jnp.zeros((8, LANES), F32)
     last = CUES * sources
 
-    def rows(start):
-        return pl.ds(pl.multiple_of(start, 8), 8)
+    def tile(start, at):
+        return pl.ds(pl.multiple_of(start, 16) + at, 8)
 
     def per_level(k):
         lev = base + k
         held, held_spot = nothing, nothing
-        pair = scalar_cue[last, lev]
         for s in range(sources):
-            row, off, put, stop, turn, at = (scalar_cue[CUES * s + j, lev] for j in range(6))
-            first = lane >= off
-            value = jnp.where(first, vals[s, rows(row), :], vals[s, rows(row + 8), :])
+            row, turn, word, at = (scalar_cue[CUES * s + j, lev] for j in range(4))
+            word = jnp.full((8, LANES), word, jnp.int32)
+            put, stop = (word >> 7) & (LANES - 1), word >> 14
+            first = lane >= (word & (LANES - 1))
+            value = jnp.where(first, store[s, tile(row, 0), :], store[s, tile(row, 16), :])
             value = pltpu.roll(value, turn, 1)
-            spot = jnp.where(first, spots[s, rows(row), :], spots[s, rows(row + 8), :])
+            spot = jnp.where(first, store[s, tile(row, 8), :], store[s, tile(row, 24), :])
             spot = pltpu.roll(spot, turn, 1)
             fresh = (lane >= put) & (lane < stop)
             held = jnp.where(fresh, value, held)
             held_spot = jnp.where(fresh, spot, held_spot)
-            queue[rows(16 * pair + at), :] = held
-            queue_spot[rows(16 * pair + at), :] = held_spot
+            queue[tile(at, 0), :] = held
+            queue[tile(at, 8), :] = held_spot
             late = lane < stop - LANES
-            over = jnp.broadcast_to(stop, (8, LANES)) >= LANES
+            over = stop >= LANES
             held = jnp.where(over, jnp.where(late, value, 0.0), held)
             held_spot = jnp.where(over, jnp.where(late, spot, 0.0), held_spot)
-        at = 16 * pair + scalar_cue[last + 1, lev]
-        queue[rows(at), :] = held
-        queue_spot[rows(at), :] = held_spot
-        queue[rows(at + 8), :] = nothing
-        queue_spot[rows(at + 8), :] = nothing
+        at = scalar_cue[last + 1, lev]
+        queue[tile(at, 0), :] = held
+        queue[tile(at, 8), :] = held_spot
+        queue[tile(at, 16), :] = nothing
+        queue[tile(at, 24), :] = nothing
+        pair = scalar_cue[last, lev]
         for p in range(sources // 2):
             level_of[pair + p] = k
 
@@ -239,21 +244,22 @@
     pair = scalar_cue[last + 2, 0]
     for p in range(UNROLL):
         level_of[pair + p] = levels
-        for h in range(2):
-            queue[rows(16 * (pair + p) + 8 * h), :] = nothing
-            queue_spot[rows(16 * (pair + p) + 8 * h), :] = nothing
+        for at in range(0, 32, 8):
+            queue[tile(32 * (pair + p), at), :] = nothing
     return pair
 
 
-UNROLL = 8
-
-
-def spread(wide, levels, base, width, first, queue, queue_spot, level_of, count, field):
+UNROLL = 16
+REST = 4
+
+
+def spread(wide, levels, base, width, first, queue, level_of, count, field):
     sub = iota((8, LANES), 0)
     col = first[0] + sub % 4
     reach = jnp.where(sub < 4, col, 2 * wide - col).astype(F32)
     tall = iota((HALF, LANES), 0).astype(F32).astype(BF16)
     one, zero = jnp.ones((HALF, LANES), BF16), jnp.zeros((HALF, LANES), BF16)
+    none = jnp.zeros((16, LANES), BF16)
 
     def clear(k, carry):
         field[k] = jnp.zeros(field.shape[1:], F32)
@@ -261,39 +267,55 @@
 
     lax.fori_loop(0, levels + 1, clear, 0)
 
-    def group(g, carry):
-        for p in range(UNROLL):
-            pair = g * UNROLL + p
+    def group(first_pair, size):
+        for p in range(size):
+            parts_of_y = 2 if p % 2 == 0 else 4
+            length = NY // parts_of_y
+            shift = length.bit_length() - 1
+            pair = first_pair + p
             k = level_of[pair]
             rate = width[base + jnp.minimum(k, levels - 1)].astype(F32)
             slope = -1.0 / jnp.full((8, LANES), rate, F32)
             lefts, rights = [], []
             for h in range(2):
-                at = pl.ds(pl.multiple_of(8 * (2 * pair + h), 8), 8)
-                value = queue[at, :]
-                spot = queue_spot[at, :].astype(jnp.int32)
+                start = pl.multiple_of(32 * pair + 16 * h, 16)
+                value = queue[pl.ds(start, 8), :]
+                spot = queue[pl.ds(start + 8, 8), :].astype(jnp.int32)
                 xpos = (spot >> 9).astype(F32)
-                side = ((spot >> 8) & 1).astype(F32)
-                ypos = (spot & (HALF - 1)).astype(F32)
+                section = ((spot >> shift) & (parts_of_y - 1)).astype(F32)
+                ypos = (spot & (length - 1)).astype(F32)
                 gain = jnp.exp(jnp.abs(reach - xpos) * slope)
                 gain = gain - pltpu.roll(gain, 4, 0)
-                upper = jnp.concatenate([side, side], 0).astype(BF16)
-                lower = jnp.concatenate([1.0 - side, 1.0 - side], 0).astype(BF16)
+                section = jnp.concatenate([section, section], 0).astype(BF16)
+                inside = [section == jnp.full((16, LANES), q, BF16) for q in range(parts_of_y)]
                 tiles = []
                 for x in range(NX_DEV):
                     term = value * jnp.broadcast_to(gain[x : x + 1, :], (8, LANES))
                     top = term.astype(BF16).astype(F32)
                     both = jnp.concatenate([top, term - top], 0).astype(BF16)
-                    tiles += [both * lower, both * upper]
+                    tiles += [jnp.where(inside[q], both, none) for q in range(parts_of_y)]
                 lefts.append(jnp.concatenate(tiles, 0))
-                mark = jnp.broadcast_to(ypos[:1], (HALF, LANES)).astype(BF16)
-                rights.append(jnp.where(tall == mark, one, zero))
+                mark = jnp.broadcast_to(ypos[:1], (length, LANES)).astype(BF16)
+                rights.append(jnp.where(tall[:length] == mark, one[:length], zero[:length]))
             done = nt_dot(jnp.concatenate(lefts, 1), jnp.concatenate(rights, 1))
-            parts = [done[16 * i : 16 * i + 8] + done[16 * i + 8 : 16 * i + 16] for i in range(2 * NX_DEV)]
+            parts = []
+            for i in range(parts_of_y * NX_DEV):
+                total = done[16 * i : 16 * i + 8] + done[16 * i + 8 : 16 * i + 16]
+                parts += [total[:, at : at + LANES] for at in range(0, length, LANES)]
             field[k] = field[k] + jnp.concatenate(parts, 0)
+
+    def long_group(g, carry):
+        group(g * UNROLL, UNROLL)
         return carry
 
-    lax.fori_loop(0, (count + UNROLL - 1) // UNROLL, group, 0)
+    def short_group(g, carry):
+        group(done_pairs + g * REST, REST)
+        return carry
+
+    groups = count >> 4
+    done_pairs = groups * UNROLL
+    lax.fori_loop(0, groups, long_group, 0)
+    lax.fori_loop(0, (count - done_pairs + REST - 1) >> 2, short_group, 0)
 
 
 def filter_levels(levels, base, width, table, field, slab):
@@ -303,10 +325,6 @@
     def one_level(k):
         slope = -1.0 / jnp.full((8, LANES), width[base + k].astype(F32), F32)
         grid = field[k]
-        blocks = []
-        for i in range(2 * NX_DEV):
-            blocks += [grid[8 * i : 8 * i + 8, :LANES], grid[8 * i : 8 * i + 8, LANES:]]
-        grid = jnp.concatenate(blocks, 0)
         top = grid.astype(BF16)
         rest = (grid - top.astype(F32)).astype(BF16)
         mat = table[k, :LANES, :]
@@ -346,16 +364,16 @@
 
 
 def field_kernel(sources, wide, nvar, width, first, start, own, oth, far_table, slab, *scratch):
-    table, table_sem, cue, scalar_cue, sem, vals, spots, queue, queue_spot, level_of, field = scratch
+    table, table_sem, cue, scalar_cue, sem, store, queue, level_of, field = scratch
     chunks = (own.shape[1] - 8) // (nvar + 1)
     levels = table.shape[0]
     base = start[0]
     fetch = pltpu.make_async_copy(far_table, table, table_sem)
     fetch.start()
     count = gather_levels(
-        sources, nvar, chunks, base, levels, own, oth, cue, scalar_cue, sem, vals, spots, queue, queue_spot, level_of
+        sources, nvar, chunks, base, levels, own, oth, cue, scalar_cue, sem, store, queue, level_of
     )
-    spread(wide, levels, base, width, first, queue, queue_spot, level_of, count, field)
+    spread(wide, levels, base, width, first, queue, level_of, count, field)
     fetch.wait()
     filter_levels(levels, base, width, table, field, slab)
 
@@ -377,12 +395,10 @@
             pltpu.VMEM((CUES * sources + 8, LANES), jnp.int32),
             pltpu.SMEM((CUES * sources + 8, LANES), jnp.int32),
             pltpu.SemaphoreType.DMA,
-            pltpu.VMEM((sources, 8 * chunks + 8, LANES), F32),
-            pltpu.VMEM((sources, 8 * chunks + 8, LANES), F32),
-            pltpu.VMEM((16 * pairs, LANES), F32),
-            pltpu.VMEM((16 * pairs, LANES), F32),
+            pltpu.VMEM((sources, 16 * chunks + 16, LANES), F32),
+            pltpu.VMEM((32 * pairs, LANES), F32),
             pltpu.SMEM((pairs + sources,), jnp.int32),
-            pltpu.VMEM((levels + 1, 16 * NX_DEV, HALF), F32),
+            pltpu.VMEM((levels + 1, 32 * NX_DEV, LANES), F32),
         ],
         compiler_params=pltpu.CompilerParams(vmem_limit_bytes=50 << 20),
         name="field",

time: 47.6 us -> 45.6 us (0.958)
  Pallas kernels: 23.7 us -> 21.9 us
    pallas_call x1, Pallas kernels: 12.3 us -> 10.5 us  [make_field(): pl.pallas_call(functools.partial(field_kernel, sources, wide, nvar), in_s...]
  transfers between devices with their start and end apart: 10 -> 10, of which waited for: 5 -> 5; matrix products, arithmetic and copies ran while one was open for 12% -> 13% of each run, Pallas kernels for 11% -> 11%
where the time goes in v5:
time: 45.6 us; the launch traced here: 45.2 us
  Pallas kernels  21.9 us (48%)
  starting transfers between devices  10.4 us (23%)
  waiting for transfers between devices  6.91 us (15%)
  local copies, waits for them, and re-layouts  3.67 us (8%)
  other arithmetic  2.15 us (5%)
    pallas_call x1, Pallas kernels, make_field(): pl.pallas_call(functools.partial(field_kernel, sources, wide, nvar), in_s...  10.5 us
    ppermute x4, starting transfers between devices, on_device(): lax.ppermute(held, 'sub', [(i, i ^ 1) for i in range(groups)])  5.66 us
    ppermute x3, starting transfers between devices, on_device(): lax.ppermute(unit, 'sub', [(i, (i + k) % groups) for i in range(groups)])  4.61 us
    pallas_call x1, Pallas kernels, route(): pl.pallas_call(route_kernel, out_shape=jax.ShapeDtypeStruct(((nvar + 1) *...  3.95 us
    pallas_call x2, Pallas kernels, mix(): pl.pallas_call(mix_kernel, grid=(2,), in_specs=[strip, matrix, matrix] +...  3.75 us
    pallas_call x1, Pallas kernels, tables(): pl.pallas_call(table_kernel, grid=(levels // depth,), in_specs=[pl.BlockS...  3.65 us
    ppermute x1, waiting for transfers between devices, on_device(): swapped = lax.ppermute(slab, 'var', swap)  2.79 us
    ppermute x1, waiting for transfers between devices, on_device(): oth = lax.ppermute(own, 'var', swap)  2.13 us
  transfers between devices with their start and end apart: 10, of which 5 were waited for; matrix products, arithmetic and copies ran while one was open for 13% of the time, Pallas kernels for 11%

profile of v5, /device:TPU:0, one launch (start us, length us, event | category | flops | bytes accessed | tf_op | source)
XLA Modules:
  0.0 45.2 jit_solution(7449784744531079909)
XLA Ops:
  0.0 3.9 %route.1 = f32[168,128]{1,0:T(8,128)} custom-call(f32[4,4096]{1,0:T(4,128)} %inn_ref.1, s32[32,128]{1,0:T(8,128)} %bitcast.70, s32[32,128]{1,0:T(8,128)} %bitcast.71, s32[32,128]{1,0:T(8,128)} %bitcast.72), custom_call_target="tpu_custom_call" | custom-call | tf_op jit(solution)/shard_map/route/pallas_call | solution.py:92
  4.0 3.0 %collective-permute-start.4 = (f32[168,128]{1,0:T(8,128)}, f32[168,128]{1,0:T(8,128)S(1)}, u32[]{:S(2)}, u32[]{:S(2)}) collective-permute-start(f32[168,128]{1,0:T(8,128)} %route.1), channel_id=1, source_target_pairs={{0,2},{2,0},{4,6},{6,4},{8,10},{10,8},{12,14},{14,12},{1,3},{3,1},... | collective-permute-start | bytes 258056 | tf_op jit(solution)/shard_map/ppermute | solution.py:470
  7.0 3.6 %collective-permute-start.3 = (f32[168,128]{1,0:T(8,128)}, f32[168,128]{1,0:T(8,128)S(1)}, u32[]{:S(2)}, u32[]{:S(2)}) collective-permute-start(f32[168,128]{1,0:T(8,128)} %route.1), channel_id=1, source_target_pairs={{0,12},{2,14},{4,0},{6,2},{8,4},{10,6},{12,8},{14,10},{1,13},{3,15... | collective-permute-start | bytes 258056 | tf_op jit(solution)/shard_map/ppermute | solution.py:466
  10.6 0.0 collective-permute-start.1
  10.6 1.0 %collective-permute-start = (f32[168,128]{1,0:T(8,128)}, f32[168,128]{1,0:T(8,128)S(1)}, u32[]{:S(2)}, u32[]{:S(2)}) collective-permute-start(f32[168,128]{1,0:T(8,128)} %route.1), channel_id=1, source_target_pairs={{0,4},{2,6},{4,8},{6,10},{8,12},{10,14},{12,0},{14,2},{1,5},{3,7},... | collective-permute-start | bytes 258056 | tf_op jit(solution)/shard_map/ppermute | solution.py:466
  11.6 0.0 collective-permute-start.2
  11.6 0.9 %bitcast_dynamic-update-slice_fusion.7 = f32[8,168,128]{2,1,0:T(8,128)S(1)} fusion(f32[168,128]{1,0:T(8,128)} %route.1), kind=kLoop, calls=%fused_computation.29 | loop fusion | bytes 172032
  12.5 0.8 %fusion.11 = (f32[4,4]{1,0:T(4,128)S(1)}, f32[4,4]{1,0:T(4,128)S(1)}) fusion(f32[4,8]{1,0:T(4,128)} %param.15), kind=kLoop, calls=%fused_computation.41 | loop fusion | bytes 256 | tf_op jit(solution)/shard_map/jit(_roll_static)/slice | solution.py:459
  13.4 0.8 %maximum_select_fusion = f32[4,8]{1,0:T(4,128)S(1)} fusion(f32[4,8]{1,0:T(4,128)} %param.15, f32[4,4]{1,0:T(4,128)S(1)} %get-tuple-element.32, f32[4,4]{1,0:T(4,128)S(1)} %get-tuple-element.31, pred[]{:T(512)S(6)} %eq.3), kind=kLoop, calls=%fused_computation.34 | loop fusion | flops 64 | bytes 385 | tf_op jit(solution)/shard_map/jit(_where)/select_n | solution.py:459
  14.1 0.1 fusion.10
  14.2 0.1 pad_maximum_fusion.2
  14.3 0.8 %mul.119 = f32[256]{0:T(256)S(1)} reshape(f32[4,64]{1,0:T(4,128)} %param.14) | data formatting | bytes 2048 | tf_op jit(solution)/shard_map/mul | solution.py:151
  15.0 0.1 broadcast_in_dim.9
  15.1 0.1 sub.48
  15.2 0.1 broadcast_in_dim.19
  15.3 0.1 sub.54
  15.4 0.1 tile.39
  15.5 0.1 tile.17
  15.6 0.0 collective-permute-done.2
  15.6 0.8 %fusion.8 = (f32[64,8]{0,1:T(8,128)S(1)}, f32[64,8]{0,1:T(8,128)S(1)}, f32[8,64]{1,0:T(8,128)S(1)}, f32[8,64]{1,0:T(8,128)S(1)}) fusion(f32[4,64]{1,0:T(4,128)} %param.13, f32[4,64]{1,0:T(4,128)S(1)} %collective-permute-done.2), kind=kLoop, calls=%fused_computation.38 | loop fusion | flops 1024 | bytes 10240 | tf_op jit(solution)/shard_map/transpose | solution.py:146
  16.4 0.1 multiply_bitcast_fusion.1
  16.4 0.1 copy.12
  16.5 0.1 mul.128
  16.6 0.1 multiply_bitcast_fusion
  16.7 0.1 copy.14
  16.8 0.1 mul.141
  16.9 0.2 fusion.4
  17.1 0.1 copy.13
  17.2 0.1 copy.15
  17.3 0.2 fusion.1
  17.4 0.8 %collective-permute-done.1 = f32[168,128]{1,0:T(8,128)S(1)} collective-permute-done((f32[168,128]{1,0:T(8,128)}, f32[168,128]{1,0:T(8,128)S(1)}, u32[]{:S(2)}, u32[]{:S(2)}) %collective-permute-start.1) | collective-permute-done | bytes 86048 | tf_op jit(solution)/shard_map/ppermute | solution.py:466
  18.2 0.5 %collective-permute-start.6 = (f32[168,128]{1,0:T(8,128)S(1)}, f32[168,128]{1,0:T(8,128)S(1)}, u32[]{:S(2)}, u32[]{:S(2)}) collective-permute-start(f32[168,128]{1,0:T(8,128)S(1)} %collective-permute-done.1), channel_id=1, source_target_pairs={{0,2},{2,0},{4,6},{6,4},{8,10},{10,8},{12,14},{14,12},{1,3},{3,1},... | collective-permute-start | bytes 258056 | tf_op jit(solution)/shard_map/ppermute | solution.py:470
  18.7 0.0 collective-permute-done
  18.8 1.6 %collective-permute-start.5 = (f32[168,128]{1,0:T(8,128)S(1)}, f32[168,128]{1,0:T(8,128)S(1)}, u32[]{:S(2)}, u32[]{:S(2)}) collective-permute-start(f32[168,128]{1,0:T(8,128)S(1)} %collective-permute-done), channel_id=1, source_target_pairs={{0,2},{2,0},{4,6},{6,4},{8,10},{10,8},{12,14},{14,12},{1,3},{3,1},... | collective-permute-start | bytes 258056 | tf_op jit(solution)/shard_map/ppermute | solution.py:470
  20.3 0.0 collective-permute-done.3
  20.4 0.5 %collective-permute-start.7 = (f32[168,128]{1,0:T(8,128)S(1)}, f32[168,128]{1,0:T(8,128)S(1)}, u32[]{:S(2)}, u32[]{:S(2)}) collective-permute-start(f32[168,128]{1,0:T(8,128)S(1)} %collective-permute-done.3), channel_id=1, source_target_pairs={{0,2},{2,0},{4,6},{6,4},{8,10},{10,8},{12,14},{14,12},{1,3},{3,1},... | collective-permute-start | bytes 258056 | tf_op jit(solution)/shard_map/ppermute | solution.py:470
  20.9 0.0 copy-start
  20.9 3.7 %tables.1.far_table = bf16[32,256,256]{2,1,0:T(8,128)(2,1)} custom-call(s32[64]{0:T(128)} %width.3, s32[1]{0:T(128)} %bitcast.1.base.start), custom_call_target="tpu_custom_call" | custom-call | flops 16777216 | bytes 8388608 | tf_op jit(solution)/shard_map/tables/pallas_call | solution.py:131
  24.6 0.3 collective-permute-done.5
  24.9 0.9 %collective-permute-done.7 = f32[168,128]{1,0:T(8,128)S(1)} collective-permute-done((f32[168,128]{1,0:T(8,128)S(1)}, f32[168,128]{1,0:T(8,128)S(1)}, u32[]{:S(2)}, u32[]{:S(2)}) %collective-permute-start.7) | collective-permute-done | bytes 86048 | tf_op jit(solution)/shard_map/ppermute | solution.py:470
  25.8 0.0 collective-permute-done.6
  25.8 0.1 collective-permute-start.8
  25.9 2.1 %collective-permute-done.8.oth = f32[8,168,128]{2,1,0:T(8,128)S(1)} collective-permute-done((f32[8,168,128]{2,1,0:T(8,128)S(1)}, f32[8,168,128]{2,1,0:T(8,128)S(1)}, u32[]{:S(2)}, u32[]{:S(2)}) %collective-permute-start.8) | collective-permute-done | bytes 688160 | tf_op jit(solution)/shard_map/ppermute | solution.py:473
  28.0 10.5 %field.1.slab = f32[4,4,256,128]{3,2,1,0:T(8,128)S(1)} custom-call(s32[64]{0:T(128)S(1)} %copy-done, s32[1]{0:T(128)} %bitcast.first, s32[1]{0:T(128)} %bitcast.1.base.start, f32[8,168,128]{2,1,0:T(8,128)S(1)} %bitcast_dynamic-update-slice_fusion.own, f32[8,168,128]{2,1,0:T(8,128)S(1)} %collective-permute-done.8.oth, bf16[32,256,256]{2,1,0:T(8,128)(2,1)} %tables.1.far_table), custom_call_target="tpu_custom_call" | custom-call | tf_op jit(solution)/shard_map/field/pallas_call | solution.py:387
  38.5 0.1 collective-permute-start.9
  38.6 1.3 %mix.2.refs_0_ = f32[2,4,256,256]{3,2,1,0:T(8,128)S(1)} custom-call(f32[4,4,256,128]{3,2,1,0:T(8,128)S(1)} %field.1.slab, bf16[256,256]{1,0:T(8,128)(2,1)S(1)} %get-tuple-element.19.high, bf16[256,256]{1,0:T(8,128)(2,1)S(1)} %get-tuple-element.20.low), custom_call_target="tpu_custom_call" | custom-call | flops 1073741824 | bytes 6291456 | tf_op jit(solution)/shard_map/mix/pallas_call | solution.py:437
  40.0 2.8 %collective-permute-done.9.slab = f32[4,4,256,128]{3,2,1,0:T(8,128)S(1)} collective-permute-done((f32[4,4,256,128]{3,2,1,0:T(8,128)S(1)}, f32[4,4,256,128]{3,2,1,0:T(8,128)S(1)}, u32[]{:S(2)}, u32[]{:S(2)}) %collective-permute-start.9) | collective-permute-done | bytes 2097184 | tf_op jit(solution)/shard_map/ppermute | solution.py:475
  42.8 2.4 %mix.3 = f32[256,16,128]{2,1,0:T(8,128)} custom-call(f32[4,4,256,128]{3,2,1,0:T(8,128)S(1)} %collective-permute-done.9.slab, bf16[256,256]{1,0:T(8,128)(2,1)S(1)} %get-tuple-element.17.high, bf16[256,256]{1,0:T(8,128)(2,1)S(1)} %get-tuple-element.18.low, f32[2,4,256,256]{3,2,1,0:T(8,128)S(1)} %mix.2.refs_0_), custom_call_target="tpu_custom_call" | custom-call | flops 1073741824 | bytes 6291456 | tf_op jit(solution)/shard_map/mix/pallas_call | solution.py:437
  (13 shorter events, 0.1 us)
Async XLA Ops:
  4.0 16.9 %collective-permute-start.4 = (f32[168,128]{1,0:T(8,128)}, f32[168,128]{1,0:T(8,128)S(1)}, u32[]{:S(2)}, u32[]{:S(2)}) collective-permute-start(f32[168,128]{1,0:T(8,128)} %route.1), channel_id=1, source_target_pairs={{0,2},{2,0},{4,6},{6,4},{8,10},{10,8},{12,14},{14,12},{1,3},{3,1},... | collective-permute-start | bytes 258056 | tf_op jit(solution)/shard_map/ppermute | solution.py:470
  7.0 13.4 %collective-permute-start.3 = (f32[168,128]{1,0:T(8,128)}, f32[168,128]{1,0:T(8,128)S(1)}, u32[]{:S(2)}, u32[]{:S(2)}) collective-permute-start(f32[168,128]{1,0:T(8,128)} %route.1), channel_id=1, source_target_pairs={{0,12},{2,14},{4,0},{6,2},{8,4},{10,6},{12,8},{14,10},{1,13},{3,15... | collective-permute-start | bytes 258056 | tf_op jit(solution)/shard_map/ppermute | solution.py:466
  10.6 7.6 %collective-permute-start.1 = (f32[168,128]{1,0:T(8,128)}, f32[168,128]{1,0:T(8,128)S(1)}, u32[]{:S(2)}, u32[]{:S(2)}) collective-permute-start(f32[168,128]{1,0:T(8,128)} %route.1), channel_id=1, source_target_pairs={{0,8},{2,10},{4,12},{6,14},{8,0},{10,2},{12,4},{14,6},{1,9},{3,11}... | collective-permute-start | bytes 258056 | tf_op jit(solution)/shard_map/ppermute | solution.py:466
  10.6 8.1 %collective-permute-start = (f32[168,128]{1,0:T(8,128)}, f32[168,128]{1,0:T(8,128)S(1)}, u32[]{:S(2)}, u32[]{:S(2)}) collective-permute-start(f32[168,128]{1,0:T(8,128)} %route.1), channel_id=1, source_target_pairs={{0,4},{2,6},{4,8},{6,10},{8,12},{10,14},{12,0},{14,2},{1,5},{3,7},... | collective-permute-start | bytes 258056 | tf_op jit(solution)/shard_map/ppermute | solution.py:466
  11.6 4.0 %collective-permute-start.2 = (f32[4,64]{1,0:T(4,128)}, f32[4,64]{1,0:T(4,128)S(1)}, u32[]{:S(2)}, u32[]{:S(2)}) collective-permute-start(f32[4,64]{1,0:T(4,128)} %param.13), channel_id=1, source_target_pairs={{0,1},{1,0},{2,3},{3,2},{4,5},{5,4},{6,7},{7,6},{8,9},{9,8},{10,11... | collective-permute-start | bytes 3080 | tf_op jit(solution)/shard_map/ppermute | solution.py:458
  18.2 7.6 %collective-permute-start.6 = (f32[168,128]{1,0:T(8,128)S(1)}, f32[168,128]{1,0:T(8,128)S(1)}, u32[]{:S(2)}, u32[]{:S(2)}) collective-permute-start(f32[168,128]{1,0:T(8,128)S(1)} %collective-permute-done.1), channel_id=1, source_target_pairs={{0,2},{2,0},{4,6},{6,4},{8,10},{10,8},{12,14},{14,12},{1,3},{3,1},... | collective-permute-start | bytes 258056 | tf_op jit(solution)/shard_map/ppermute | solution.py:470
  18.8 6.1 %collective-permute-start.5 = (f32[168,128]{1,0:T(8,128)S(1)}, f32[168,128]{1,0:T(8,128)S(1)}, u32[]{:S(2)}, u32[]{:S(2)}) collective-permute-start(f32[168,128]{1,0:T(8,128)S(1)} %collective-permute-done), channel_id=1, source_target_pairs={{0,2},{2,0},{4,6},{6,4},{8,10},{10,8},{12,14},{14,12},{1,3},{3,1},... | collective-permute-start | bytes 258056 | tf_op jit(solution)/shard_map/ppermute | solution.py:470
  20.4 5.4 %collective-permute-start.7 = (f32[168,128]{1,0:T(8,128)S(1)}, f32[168,128]{1,0:T(8,128)S(1)}, u32[]{:S(2)}, u32[]{:S(2)}) collective-permute-start(f32[168,128]{1,0:T(8,128)S(1)} %collective-permute-done.3), channel_id=1, source_target_pairs={{0,2},{2,0},{4,6},{6,4},{8,10},{10,8},{12,14},{14,12},{1,3},{3,1},... | collective-permute-start | bytes 258056 | tf_op jit(solution)/shard_map/ppermute | solution.py:470
  20.9 7.1 %copy-start = (s32[64]{0:T(128)S(1)}, s32[64]{0:T(128)}, u32[]{:S(2)}) copy-start(s32[64]{0:T(128)} %width.3) | copy-start | bytes 772
  25.8 2.2 %collective-permute-start.8 = (f32[8,168,128]{2,1,0:T(8,128)S(1)}, f32[8,168,128]{2,1,0:T(8,128)S(1)}, u32[]{:S(2)}, u32[]{:S(2)}) collective-permute-start(f32[8,168,128]{2,1,0:T(8,128)S(1)} %bitcast_dynamic-update-slice_fusion.own), channel_id=1, source_target_pairs={{0,1},{1,0},{2,3},{3,2},{4,5},{5,4},{6,7},{7,6},{8,9},{9,8},{10,11... | collective-permute-start | bytes 2064392 | tf_op jit(solution)/shard_map/ppermute | solution.py:473
  38.5 4.2 %collective-permute-start.9 = (f32[4,4,256,128]{3,2,1,0:T(8,128)S(1)}, f32[4,4,256,128]{3,2,1,0:T(8,128)S(1)}, u32[]{:S(2)}, u32[]{:S(2)}) collective-permute-start(f32[4,4,256,128]{3,2,1,0:T(8,128)S(1)} %field.1.slab), channel_id=1, source_target_pairs={{0,1},{1,0},{2,3},{3,2},{4,5},{5,4},{6,7},{7,6},{8,9},{9,8},{10,11... | collective-permute-start | bytes 6291464 | tf_op jit(solution)/shard_map/ppermute | solution.py:475

commit v6 on v5

--- a/solution.py
+++ b/solution.py
@@ -139,19 +139,52 @@
     )(band_width, base)
 
 
-def mix_matrix(scale, sigma, weights, base, depth):
+def pick(table, chosen):
+    return lax.dot_general(
+        table, chosen, (((0,), (0,)), ((), ())), precision=lax.Precision.HIGHEST, preferred_element_type=F32
+    )
+
+
+def matrix_kernel(side, scale, theirs, sigma, balance, *outs):
     nvar, levels = scale.shape
-    level = base + jnp.arange(depth)
-    dist = jnp.arange(levels)[:, None] - jnp.repeat(level, nvar)[None, :]
-    own = jnp.tile(scale.T, (1, depth))
-    other = lax.dynamic_slice_in_dim(scale, base, depth, 1).T.reshape(1, -1)
-    gap = dist.astype(F32)
-    corr = jnp.exp(-gap * gap / (2.0 * own * other))
-    corr = jnp.where(jnp.abs(dist) <= VB, corr, F32(0.0))
-    mix = sigma[:, :, None] * jnp.tile(weights, (1, depth))[:, None, :] * corr[None]
-    mix = mix.reshape(-1, depth * nvar)
-    high = lax.reduce_precision(mix, 8, 7)
-    return high.astype(BF16), (mix - high).astype(BF16)
+    both = 2 * nvar
+    cols = outs[0].shape[1]
+    depth = cols // both
+    for k in range(2):
+        here = (side[0] + k) % 2
+        scales = (scale, theirs) if k == 0 else (theirs, scale)
+        unit = iota((nvar, cols), 1) % both
+        pairs = [(held[...], jnp.where(unit == iota((nvar, cols), 0) + nvar * j, 1.0, 0.0)) for j, held in enumerate(scales)]
+        own = sum(pick(held, chosen) for held, chosen in pairs)
+        gap = iota((levels, cols), 0) - depth * here - iota((levels, cols), 1) // both
+        other = jnp.sum(jnp.where(gap == 0, own, 0.0), 0, keepdims=True)
+        dist = gap.astype(F32)
+        corr = jnp.where(jnp.abs(gap) <= VB, jnp.exp(-dist * dist / (2.0 * own * other)), 0.0)
+        order = (iota((both, cols), 1) + nvar * here) % both
+        chosen = jnp.where(order == iota((both, cols), 0), 1.0, 0.0)
+        weight = jnp.dot(balance[...], chosen, precision=lax.Precision.HIGHEST, preferred_element_type=F32)
+        for v in range(nvar):
+            spread_out = jnp.where(iota((nvar, cols), 0) == v, 1.0, 0.0)
+            full = pick(sigma[...], spread_out) * weight[v : v + 1, :] * corr
+            top = full.astype(BF16)
+            rows = slice(v * levels, (v + 1) * levels)
+            outs[2 * k][rows, :] = top
+            outs[2 * k + 1][rows, :] = (full - top.astype(F32)).astype(BF16)
+
+
+def mix_matrices(side, scale, theirs, sigma, balance):
+    nvar, levels = scale.shape
+    shape = jax.ShapeDtypeStruct((nvar * levels, nvar * levels), BF16)
+    whole = pl.BlockSpec(memory_space=pltpu.VMEM)
+    outs = pl.pallas_call(
+        matrix_kernel,
+        in_specs=[pl.BlockSpec(memory_space=pltpu.SMEM)] + [whole] * 4,
+        out_specs=(whole,) * 4,
+        out_shape=(shape,) * 4,
+        compiler_params=pltpu.CompilerParams(vmem_limit_bytes=12 << 20),
+        name="matrices",
+    )(side, scale, theirs, sigma, balance)
+    return outs[:2], outs[2:]
 
 
 CUES = 4
@@ -318,13 +351,13 @@
     lax.fori_loop(0, (count - done_pairs + REST - 1) >> 2, short_group, 0)
 
 
-def filter_levels(levels, base, width, table, field, slab):
+def filter_levels(skip, levels, base, width, table, field, slab):
     lane = iota((8, LANES), 1)
     line = lane.astype(F32)
 
     def one_level(k):
-        slope = -1.0 / jnp.full((8, LANES), width[base + k].astype(F32), F32)
-        grid = field[k]
+        slope = -1.0 / jnp.full((8, LANES), width[base + skip + k].astype(F32), F32)
+        grid = field[skip + k]
         top = grid.astype(BF16)
         rest = (grid - top.astype(F32)).astype(BF16)
         mat = table[k, :LANES, :]
@@ -363,19 +396,27 @@
     lax.fori_loop(0, levels // 4, group, 0)
 
 
-def field_kernel(sources, wide, nvar, width, first, start, own, oth, far_table, slab, *scratch):
-    table, table_sem, cue, scalar_cue, sem, store, queue, level_of, field = scratch
+def field_kernel(sources, wide, nvar, width, first, start, own, oth, far_table, slab, field, table_rest, *scratch):
+    table, table_sems, cue, scalar_cue, sem, store, queue, level_of = scratch
     chunks = (own.shape[1] - 8) // (nvar + 1)
-    levels = table.shape[0]
+    levels, part = far_table.shape[0], table.shape[0]
     base = start[0]
-    fetch = pltpu.make_async_copy(far_table, table, table_sem)
+    fetch = pltpu.make_async_copy(far_table.at[:part], table, table_sems.at[0])
+    fetch_rest = pltpu.make_async_copy(far_table.at[part:], table_rest, table_sems.at[1])
     fetch.start()
+    fetch_rest.start()
     count = gather_levels(
         sources, nvar, chunks, base, levels, own, oth, cue, scalar_cue, sem, store, queue, level_of
     )
     spread(wide, levels, base, width, first, queue, level_of, count, field)
     fetch.wait()
-    filter_levels(levels, base, width, table, field, slab)
+    fetch_rest.wait()
+    filter_levels(0, part, base, width, table, field, slab)
+
+
+def rest_kernel(width, start, field, table, slab):
+    part = table.shape[0]
+    filter_levels(part, part, start[0], width, table, field, slab)
 
 
 def make_field(own, oth, band_width, first, base, table, nvar, levels, wide):
@@ -387,63 +428,78 @@
     return pl.pallas_call(
         functools.partial(field_kernel, sources, wide, nvar),
         in_specs=[smem] * 3 + [whole] * 2 + [pl.BlockSpec(memory_space=pltpu.HBM)],
-        out_specs=whole,
-        out_shape=jax.ShapeDtypeStruct((NX_DEV, 4, 2 * nvar * levels, LANES), F32),
+        out_specs=(whole, whole, whole),
+        out_shape=(
+            jax.ShapeDtypeStruct((NX_DEV, 4, nvar * levels, LANES), F32),
+            jax.ShapeDtypeStruct((levels + 1, 32 * NX_DEV, LANES), F32),
+            jax.ShapeDtypeStruct((levels // 2,) + table.shape[1:], BF16),
+        ),
         scratch_shapes=[
-            pltpu.VMEM(table.shape, BF16),
-            pltpu.SemaphoreType.DMA,
+            pltpu.VMEM((levels // 2,) + table.shape[1:], BF16),
+            pltpu.SemaphoreType.DMA((2,)),
             pltpu.VMEM((CUES * sources + 8, LANES), jnp.int32),
             pltpu.SMEM((CUES * sources + 8, LANES), jnp.int32),
             pltpu.SemaphoreType.DMA,
             pltpu.VMEM((sources, 16 * chunks + 16, LANES), F32),
             pltpu.VMEM((32 * pairs, LANES), F32),
             pltpu.SMEM((pairs + sources,), jnp.int32),
-            pltpu.VMEM((levels + 1, 32 * NX_DEV, LANES), F32),
         ],
-        compiler_params=pltpu.CompilerParams(vmem_limit_bytes=50 << 20),
+        compiler_params=pltpu.CompilerParams(vmem_limit_bytes=46 << 20),
         name="field",
     )(band_width, first, base, own, oth, table)
 
 
-def mix_kernel(slab, high, low, *refs):
+def filter_rest(band_width, base, field, table, shape):
+    whole = pl.BlockSpec(memory_space=pltpu.VMEM)
+    smem = pl.BlockSpec(memory_space=pltpu.SMEM)
+    return pl.pallas_call(
+        rest_kernel,
+        in_specs=[smem, smem, whole, whole],
+        out_specs=whole,
+        out_shape=jax.ShapeDtypeStruct(shape, F32),
+        compiler_params=pltpu.CompilerParams(vmem_limit_bytes=16 << 20),
+        cost_estimate=pl.CostEstimate(flops=1 << 33, bytes_accessed=32 << 20, transcendentals=0),
+        name="rest",
+    )(band_width, base, field, table)
+
+
+def mix_kernel(slab, more, high, low, *refs):
     out = refs[-1]
     rows = high.shape[0]
+    half = pl.program_id(0)
     for x in range(NX_DEV):
-        part = jnp.concatenate([slab[x, 0], slab[x, 1]], 1)
+        part = jnp.concatenate([jnp.concatenate([some[x, 2 * half], some[x, 2 * half + 1]], 1) for some in (slab, more)], 0)
         top = part.astype(BF16)
         rest = (part - top.astype(F32)).astype(BF16)
         term = nn_dot(jnp.concatenate([high[...], low[...]], 0), top)
         term = term[:rows] + term[rows:] + nn_dot(high[...], rest)
         if len(refs) == 1:
-            out[0, x] = term
+            out[half, x] = term
         else:
-            term = term + refs[0][0, x]
+            term = term + refs[0][half, x]
             flat = out.reshape(8 * term.shape[0], LANES)
             for g in range(2):
                 flat[pl.ds(4 * g + x, term.shape[0], stride=8), :] = term[:, g * LANES : (g + 1) * LANES]
 
 
-def mix(slab, mats, *before):
-    rows, depth = mats[0].shape
-    strip = pl.BlockSpec((NX_DEV, 2, depth, LANES), lambda i: (0, i, 0, 0))
-    matrix = pl.BlockSpec((rows, depth), lambda i: (0, 0))
-    partial = pl.BlockSpec((1, NX_DEV, rows, HALF), lambda i: (i, 0, 0, 0))
+def mix(slab, more, mats, *before):
+    rows = mats[0].shape[0]
+    whole = pl.BlockSpec(memory_space=pltpu.VMEM)
     if before:
         shape = (rows, 16, LANES)
         out_spec = pl.BlockSpec((rows, 8, LANES), lambda i: (0, i, 0))
     else:
         shape = (2, NX_DEV, rows, HALF)
-        out_spec = partial
+        out_spec = whole
     return pl.pallas_call(
         mix_kernel,
         grid=(2,),
-        in_specs=[strip, matrix, matrix] + [partial] * len(before),
+        in_specs=[whole] * (4 + len(before)),
         out_specs=out_spec,
         out_shape=jax.ShapeDtypeStruct(shape, F32),
         compiler_params=pltpu.CompilerParams(vmem_limit_bytes=16 << 20),
-        cost_estimate=pl.CostEstimate(flops=1 << 30, bytes_accessed=6 << 20, transcendentals=0),
         name="mix",
-    )(slab, *mats, *before)
+    )(slab, more, *mats, *before)
 
 
 def on_device(innovations, obs_owner, obs_local, obs_level, band_width, vert_scale, sigma, balance):
@@ -454,26 +510,28 @@
     unit = route(innovations, obs_owner, obs_level, obs_local, levels)
     side = lax.axis_index("var").astype(jnp.int32)
     half = levels // 2
-    base, last = half * side, half * (1 - side)
+    base = half * side
     theirs = lax.ppermute(vert_scale, "var", swap)
-    weights = jnp.where(side == 0, balance, jnp.roll(balance, nvar, 1))
-    own_mats = mix_matrix(jnp.concatenate([vert_scale, theirs], 0), sigma, weights, base, half)
-    oth_mats = mix_matrix(jnp.concatenate([theirs, vert_scale], 0), sigma, jnp.roll(weights, nvar, 1), last, half)
+    own_mats, oth_mats = mix_matrices(side.reshape(1), vert_scale, theirs, sigma, balance)
     first = (lax.axis_index("sub") * NX_DEV).astype(jnp.int32).reshape(1)
     base = base.reshape(1)
     own = [unit]
     for k in range(2, groups, 2):
         own.append(lax.ppermute(unit, "sub", [(i, (i + k) % groups) for i in range(groups)]))
     far = len(own) // 2
-    own[far], own_mats, oth_mats, when = lax.optimization_barrier((own[far], own_mats, oth_mats, base))
-    table = tables(band_width, when, half)
-    own += [lax.ppermute(held, "sub", [(i, i ^ 1) for i in range(groups)]) for held in own]
-    own[-1], table = lax.optimization_barrier((own[-1], table))
+    beside = [(i, i ^ 1) for i in range(groups)]
+    near = lax.ppermute(unit, "sub", beside)
+    table = tables(band_width, base, half)
+    own[far], near, own_mats, oth_mats, table = lax.optimization_barrier((own[far], near, own_mats, oth_mats, table))
+    own += [near] + [lax.ppermute(held, "sub", beside) for held in own[1:]]
     own = jnp.stack(own)
     oth = lax.ppermute(own, "var", swap)
-    slab = make_field(own, oth, band_width, first, base, table, nvar, half, NX_DEV * groups)
+    slab, grids, table = make_field(own, oth, band_width, first, base, table, nvar, half, NX_DEV * groups)
     swapped = lax.ppermute(slab, "var", swap)
-    out = mix(swapped, oth_mats, mix(slab, own_mats))
+    more = filter_rest(band_width, base, grids, table, slab.shape)
+    more_swapped = lax.ppermute(more, "var", swap)
+    swapped, more = lax.optimization_barrier((swapped, more))
+    out = mix(swapped, more_swapped, oth_mats, mix(slab, more, own_mats))
     out = out.reshape(nvar, levels, NY // LANES, NX_DEV, LANES)
     return jnp.swapaxes(out, 2, 3).reshape(nvar, levels, NX_DEV, NY)
 

time: 45.6 us -> 44.5 us (0.976)
  local copies, waits for them, and re-layouts: 3.67 us -> 1 us
  other arithmetic: 2.15 us -> 0 us
  waiting for transfers between devices: 6.91 us -> 8.67 us
  starting transfers between devices: 10.4 us -> 11.5 us
  Pallas kernels: 21.9 us -> 22.9 us
    ppermute x4 -> x5, waiting for transfers between devices: 1.19 us -> 5.89 us  [the longest x3 4.83 us: on_device(): own += [near] + [lax.ppermute(held, 'sub', beside) for held in own[1:]]]
    ppermute x1, waiting for transfers between devices: 2.79 us -> 0.05 us  [on_device(): swapped = lax.ppermute(slab, 'var', swap)]
    pallas_call x2 -> x4, Pallas kernels: 3.75 us -> 6.32 us  [the longest x2 3.41 us: mix(): pl.pallas_call(mix_kernel, grid=(2,), in_specs=[whole] * (4 + len(before)...]
    pallas_call x1, Pallas kernels: 10.5 us -> 8.98 us  [make_field(): pl.pallas_call(functools.partial(field_kernel, sources, wide, nvar), in_s...]
    ppermute x3, starting transfers between devices: 4.61 us -> 6.12 us  [on_device(): lax.ppermute(unit, 'sub', [(i, (i + k) % groups) for i in range(groups)])]
    mul x5 -> x0, local copies, waits for them, and re-layouts: 1.1 us -> none  [the longest x1 0.76 us: mix_matrix(): sigma[:, :, None] * jnp.tile(weights, (1, depth))[:, None, :] * corr[None]]
    select_n x2 -> x0, other arithmetic: 0.98 us -> none  [the longest x1 0.76 us: on_device(): weights = jnp.where(side == 0, balance, jnp.roll(balance, nvar, 1))]
    slice x2 -> x0, local copies, waits for them, and re-layouts: 0.9 us -> none  [the longest x1 0.83 us: on_device(): weights = jnp.where(side == 0, balance, jnp.roll(balance, nvar, 1))]
  transfers between devices with their start and end apart: 10 -> 11, of which waited for: 5 -> 5; matrix products, arithmetic and copies ran while one was open for 13% -> 2% of each run, Pallas kernels for 11% -> 17%
where the time goes in v6:
time: 44.5 us; the launch traced here: 44.2 us
  Pallas kernels  22.9 us (51%)
  starting transfers between devices  11.5 us (26%)
  waiting for transfers between devices  8.67 us (19%)
  local copies, waits for them, and re-layouts  1 us (2%)
    pallas_call x1, Pallas kernels, make_field(): pl.pallas_call(functools.partial(field_kernel, sources, wide, nvar), in_s...  8.98 us
    ppermute x3, starting transfers between devices, on_device(): lax.ppermute(unit, 'sub', [(i, (i + k) % groups) for i in range(groups)])  6.12 us
    ppermute x3, waiting for transfers between devices, on_device(): own += [near] + [lax.ppermute(held, 'sub', beside) for held in own[1:]]  4.83 us
    pallas_call x1, Pallas kernels, route(): pl.pallas_call(route_kernel, out_shape=jax.ShapeDtypeStruct(((nvar + 1) *...  3.95 us
    pallas_call x1, Pallas kernels, tables(): pl.pallas_call(table_kernel, grid=(levels // depth,), in_specs=[pl.BlockS...  3.66 us
    pallas_call x2, Pallas kernels, mix(): pl.pallas_call(mix_kernel, grid=(2,), in_specs=[whole] * (4 + len(before)...  3.41 us
    ppermute x3, starting transfers between devices, on_device(): own += [near] + [lax.ppermute(held, 'sub', beside) for held in own[1:]]  3.16 us
    ppermute x1, waiting for transfers between devices, on_device(): oth = lax.ppermute(own, 'var', swap)  2.13 us
  transfers between devices with their start and end apart: 11, of which 5 were waited for; matrix products, arithmetic and copies ran while one was open for 2% of the time, Pallas kernels for 17%

profile of v6, /device:TPU:0, one launch (start us, length us, event | category | flops | bytes accessed | tf_op | source)
XLA Modules:
  0.0 44.2 jit_solution(6696578600074844753)
XLA Ops:
  0.0 3.9 %route.1 = f32[168,128]{1,0:T(8,128)} custom-call(f32[4,4096]{1,0:T(4,128)} %inn_ref.1, s32[32,128]{1,0:T(8,128)} %bitcast.27, s32[32,128]{1,0:T(8,128)} %bitcast.28, s32[32,128]{1,0:T(8,128)} %bitcast.29), custom_call_target="tpu_custom_call" | custom-call | tf_op jit(solution)/shard_map/route/pallas_call | solution.py:92
  4.0 5.1 %collective-permute-start.4 = (f32[168,128]{1,0:T(8,128)}, f32[168,128]{1,0:T(8,128)S(1)}, u32[]{:S(2)}, u32[]{:S(2)}) collective-permute-start(f32[168,128]{1,0:T(8,128)} %route.1), channel_id=1, source_target_pairs={{0,12},{2,14},{4,0},{6,2},{8,4},{10,6},{12,8},{14,10},{1,13},{3,15... | collective-permute-start | bytes 258056 | tf_op jit(solution)/shard_map/ppermute | solution.py:520
  9.1 1.5 %collective-permute-start.2 = (f32[168,128]{1,0:T(8,128)}, f32[168,128]{1,0:T(8,128)S(1)}, u32[]{:S(2)}, u32[]{:S(2)}) collective-permute-start(f32[168,128]{1,0:T(8,128)} %route.1), channel_id=1, source_target_pairs={{0,2},{2,0},{4,6},{6,4},{8,10},{10,8},{12,14},{14,12},{1,3},{3,1},... | collective-permute-start | bytes 258056 | tf_op jit(solution)/shard_map/ppermute | solution.py:523
  10.6 0.0 collective-permute-start.1
  10.6 1.0 %collective-permute-start = (f32[168,128]{1,0:T(8,128)}, f32[168,128]{1,0:T(8,128)S(1)}, u32[]{:S(2)}, u32[]{:S(2)}) collective-permute-start(f32[168,128]{1,0:T(8,128)} %route.1), channel_id=1, source_target_pairs={{0,4},{2,6},{4,8},{6,10},{8,12},{10,14},{12,0},{14,2},{1,5},{3,7},... | collective-permute-start | bytes 258056 | tf_op jit(solution)/shard_map/ppermute | solution.py:520
  11.6 0.0 collective-permute-start.3
  11.6 0.9 %bitcast_dynamic-update-slice_fusion.7 = f32[8,168,128]{2,1,0:T(8,128)S(1)} fusion(f32[168,128]{1,0:T(8,128)} %route.1), kind=kLoop, calls=%fused_computation.7 | loop fusion | bytes 172032
  12.5 0.0 copy-start.1
  12.5 0.0 copy-start.2
  12.5 0.0 copy-start.3
  12.5 0.0 copy-start
  12.6 3.7 %tables.1.far_table = bf16[32,256,256]{2,1,0:T(8,128)(2,1)} custom-call(s32[64]{0:T(128)} %width.5, s32[1]{0:T(128)} %bitcast.1.base.start), custom_call_target="tpu_custom_call" | custom-call | flops 16777216 | bytes 8388608 | tf_op jit(solution)/shard_map/tables/pallas_call | solution.py:131
  16.2 0.0 collective-permute-done.3.theirs
  16.2 0.0 copy-done.1
  16.2 0.0 copy-done.2
  16.2 0.0 copy-done.3
  16.2 0.9 %matrices.1 = (bf16[256,256]{1,0:T(8,128)(2,1)S(1)}, bf16[256,256]{1,0:T(8,128)(2,1)S(1)}, bf16[256,256]{1,0:T(8,128)(2,1)S(1)}, bf16[256,256]{1,0:T(8,128)(2,1)S(1)}) custom-call(s32[1]{0:T(128)} %bitcast.7.side, f32[4,64]{1,0:T(4,128)S(1)} %copy-done.1, f32[4,64]{1,0:T(4,128)S(1)} %collective-permute-done.3.theirs, f32[4,64]{1,0:T(4,128)S(1)} %copy-done.2, ...), custom_call_target="tpu_custom_call" | custom-call | tf_op jit(solution)/shard_map/matrices/pallas_call | solution.py:179
  17.1 0.0 collective-permute-done.2
  17.1 0.6 %collective-permute-done.1 = f32[168,128]{1,0:T(8,128)S(1)} collective-permute-done((f32[168,128]{1,0:T(8,128)}, f32[168,128]{1,0:T(8,128)S(1)}, u32[]{:S(2)}, u32[]{:S(2)}) %collective-permute-start.1) | collective-permute-done | bytes 86048 | tf_op jit(solution)/shard_map/ppermute | solution.py:520
  17.7 1.0 %collective-permute-start.6 = (f32[168,128]{1,0:T(8,128)S(1)}, f32[168,128]{1,0:T(8,128)S(1)}, u32[]{:S(2)}, u32[]{:S(2)}) collective-permute-start(f32[168,128]{1,0:T(8,128)S(1)} %collective-permute-done.1), channel_id=1, source_target_pairs={{0,2},{2,0},{4,6},{6,4},{8,10},{10,8},{12,14},{14,12},{1,3},{3,1},... | collective-permute-start | bytes 258056 | tf_op jit(solution)/shard_map/ppermute | solution.py:526
  18.7 0.0 collective-permute-done
  18.8 1.1 %collective-permute-start.5 = (f32[168,128]{1,0:T(8,128)S(1)}, f32[168,128]{1,0:T(8,128)S(1)}, u32[]{:S(2)}, u32[]{:S(2)}) collective-permute-start(f32[168,128]{1,0:T(8,128)S(1)} %collective-permute-done), channel_id=1, source_target_pairs={{0,2},{2,0},{4,6},{6,4},{8,10},{10,8},{12,14},{14,12},{1,3},{3,1},... | collective-permute-start | bytes 258056 | tf_op jit(solution)/shard_map/ppermute | solution.py:526
  19.9 0.0 collective-permute-done.4
  19.9 1.1 %collective-permute-start.7 = (f32[168,128]{1,0:T(8,128)S(1)}, f32[168,128]{1,0:T(8,128)S(1)}, u32[]{:S(2)}, u32[]{:S(2)}) collective-permute-start(f32[168,128]{1,0:T(8,128)S(1)} %collective-permute-done.4), channel_id=1, source_target_pairs={{0,2},{2,0},{4,6},{6,4},{8,10},{10,8},{12,14},{14,12},{1,3},{3,1},... | collective-permute-start | bytes 258056 | tf_op jit(solution)/shard_map/ppermute | solution.py:526
  20.9 3.9 %collective-permute-done.5 = f32[168,128]{1,0:T(8,128)S(1)} collective-permute-done((f32[168,128]{1,0:T(8,128)S(1)}, f32[168,128]{1,0:T(8,128)S(1)}, u32[]{:S(2)}, u32[]{:S(2)}) %collective-permute-start.5) | collective-permute-done | bytes 86048 | tf_op jit(solution)/shard_map/ppermute | solution.py:526
  24.9 0.0 collective-permute-done.6
  24.9 0.9 %collective-permute-done.7 = f32[168,128]{1,0:T(8,128)S(1)} collective-permute-done((f32[168,128]{1,0:T(8,128)S(1)}, f32[168,128]{1,0:T(8,128)S(1)}, u32[]{:S(2)}, u32[]{:S(2)}) %collective-permute-start.7) | collective-permute-done | bytes 86048 | tf_op jit(solution)/shard_map/ppermute | solution.py:526
  25.8 0.1 collective-permute-start.8
  25.9 2.1 %collective-permute-done.8.oth = f32[8,168,128]{2,1,0:T(8,128)S(1)} collective-permute-done((f32[8,168,128]{2,1,0:T(8,128)S(1)}, f32[8,168,128]{2,1,0:T(8,128)S(1)}, u32[]{:S(2)}, u32[]{:S(2)}) %collective-permute-start.8) | collective-permute-done | bytes 688160 | tf_op jit(solution)/shard_map/ppermute | solution.py:528
  28.0 0.0 copy-done
  28.0 9.0 %field.1 = (f32[4,4,128,128]{3,2,1,0:T(8,128)S(1)}, f32[33,128,128]{2,1,0:T(8,128)S(1)}, bf16[16,256,256]{2,1,0:T(8,128)(2,1)S(1)}) custom-call(s32[64]{0:T(128)S(1)} %copy-done, s32[1]{0:T(128)} %bitcast.first, s32[1]{0:T(128)} %bitcast.1.base.start, f32[8,168,128]{2,1,0:T(8,128)S(1)} %bitcast_dynamic-update-slice_fusion.own, ...), custom_call_target="tpu_custom_call" | custom-call | tf_op jit(solution)/shard_map/field/pallas_call | solution.py:428
  37.0 0.1 collective-permute-start.9
  37.1 2.0 %rest.1.more = f32[4,4,128,128]{3,2,1,0:T(8,128)S(1)} custom-call(s32[64]{0:T(128)S(1)} %copy-done, s32[1]{0:T(128)} %bitcast.1.base.start, f32[33,128,128]{2,1,0:T(8,128)S(1)} %get-tuple-element.29.field, bf16[16,256,256]{2,1,0:T(8,128)(2,1)S(1)} %get-tuple-element.30.table), custom_call_target="tpu_custom_call" | custom-call | flops 8589934592 | bytes 33554432 | tf_op jit(solution)/shard_map/rest/pallas_call | solution.py:455
  39.1 0.6 %collective-permute-start.10 = (f32[4,4,128,128]{3,2,1,0:T(8,128)S(1)}, f32[4,4,128,128]{3,2,1,0:T(8,128)S(1)}, u32[]{:S(2)}, u32[]{:S(2)}) collective-permute-start(f32[4,4,128,128]{3,2,1,0:T(8,128)S(1)} %rest.1.more), channel_id=1, source_target_pairs={{0,1},{1,0},{2,3},{3,2},{4,5},{5,4},{6,7},{7,6},{8,9},{9,8},{10,11... | collective-permute-start | bytes 3145736 | tf_op jit(solution)/shard_map/ppermute | solution.py:532
  39.7 0.0 collective-permute-done.9.slab
  39.7 1.2 %mix.2.refs_0_ = f32[2,4,256,256]{3,2,1,0:T(8,128)S(1)} custom-call(f32[4,4,128,128]{3,2,1,0:T(8,128)S(1)} %get-tuple-element.28.slab, f32[4,4,128,128]{3,2,1,0:T(8,128)S(1)} %rest.1.more, bf16[256,256]{1,0:T(8,128)(2,1)S(1)} %get-tuple-element.35.high, bf16[256,256]{1,0:T(8,128)(2,1)S(1)} %get-tuple-element.36.low), custom_call_target="tpu_custom_call" | custom-call | tf_op jit(solution)/shard_map/mix/pallas_call | solution.py:494
  40.9 1.1 %collective-permute-done.10.more = f32[4,4,128,128]{3,2,1,0:T(8,128)S(1)} collective-permute-done((f32[4,4,128,128]{3,2,1,0:T(8,128)S(1)}, f32[4,4,128,128]{3,2,1,0:T(8,128)S(1)}, u32[]{:S(2)}, u32[]{:S(2)}) %collective-permute-start.10) | collective-permute-done | bytes 1048608 | tf_op jit(solution)/shard_map/ppermute | solution.py:532
  42.0 2.2 %mix.3 = f32[256,16,128]{2,1,0:T(8,128)} custom-call(f32[4,4,128,128]{3,2,1,0:T(8,128)S(1)} %collective-permute-done.9.slab, f32[4,4,128,128]{3,2,1,0:T(8,128)S(1)} %collective-permute-done.10.more, bf16[256,256]{1,0:T(8,128)(2,1)S(1)} %get-tuple-element.32.high, bf16[256,256]{1,0:T(8,128)(2,1)S(1)} %get-tuple-element.33.low, f32[2,4,256,256]{3,2,1,0:T(8,128)S(1)} %mix.2.refs_0_), custom_call_target="tpu_custom_call" | custom-call | tf_op jit(solution)/shard_map/mix/pallas_call | solution.py:494
  (7 shorter events, 0.1 us)
Async XLA Ops:
  4.0 15.9 %collective-permute-start.4 = (f32[168,128]{1,0:T(8,128)}, f32[168,128]{1,0:T(8,128)S(1)}, u32[]{:S(2)}, u32[]{:S(2)}) collective-permute-start(f32[168,128]{1,0:T(8,128)} %route.1), channel_id=1, source_target_pairs={{0,12},{2,14},{4,0},{6,2},{8,4},{10,6},{12,8},{14,10},{1,13},{3,15... | collective-permute-start | bytes 258056 | tf_op jit(solution)/shard_map/ppermute | solution.py:520
  9.1 8.1 %collective-permute-start.2 = (f32[168,128]{1,0:T(8,128)}, f32[168,128]{1,0:T(8,128)S(1)}, u32[]{:S(2)}, u32[]{:S(2)}) collective-permute-start(f32[168,128]{1,0:T(8,128)} %route.1), channel_id=1, source_target_pairs={{0,2},{2,0},{4,6},{6,4},{8,10},{10,8},{12,14},{14,12},{1,3},{3,1},... | collective-permute-start | bytes 258056 | tf_op jit(solution)/shard_map/ppermute | solution.py:523
  10.6 7.1 %collective-permute-start.1 = (f32[168,128]{1,0:T(8,128)}, f32[168,128]{1,0:T(8,128)S(1)}, u32[]{:S(2)}, u32[]{:S(2)}) collective-permute-start(f32[168,128]{1,0:T(8,128)} %route.1), channel_id=1, source_target_pairs={{0,8},{2,10},{4,12},{6,14},{8,0},{10,2},{12,4},{14,6},{1,9},{3,11}... | collective-permute-start | bytes 258056 | tf_op jit(solution)/shard_map/ppermute | solution.py:520
  10.6 8.2 %collective-permute-start = (f32[168,128]{1,0:T(8,128)}, f32[168,128]{1,0:T(8,128)S(1)}, u32[]{:S(2)}, u32[]{:S(2)}) collective-permute-start(f32[168,128]{1,0:T(8,128)} %route.1), channel_id=1, source_target_pairs={{0,4},{2,6},{4,8},{6,10},{8,12},{10,14},{12,0},{14,2},{1,5},{3,7},... | collective-permute-start | bytes 258056 | tf_op jit(solution)/shard_map/ppermute | solution.py:520
  11.6 4.6 %collective-permute-start.3 = (f32[4,64]{1,0:T(4,128)}, f32[4,64]{1,0:T(4,128)S(1)}, u32[]{:S(2)}, u32[]{:S(2)}) collective-permute-start(f32[4,64]{1,0:T(4,128)} %scale.1), channel_id=1, source_target_pairs={{0,1},{1,0},{2,3},{3,2},{4,5},{5,4},{6,7},{7,6},{8,9},{9,8},{10,11... | collective-permute-start | bytes 3080 | tf_op jit(solution)/shard_map/ppermute | solution.py:514
  12.5 3.7 %copy-start.1 = (f32[4,64]{1,0:T(4,128)S(1)}, f32[4,64]{1,0:T(4,128)}, u32[]{:S(2)}) copy-start(f32[4,64]{1,0:T(4,128)} %scale.1) | copy-start | bytes 3076
  12.5 3.7 %copy-start.2 = (f32[4,64]{1,0:T(4,128)S(1)}, f32[4,64]{1,0:T(4,128)}, u32[]{:S(2)}) copy-start(f32[4,64]{1,0:T(4,128)} %sigma.1) | copy-start | bytes 3076
  12.5 3.7 %copy-start.3 = (f32[4,8]{1,0:T(4,128)S(1)}, f32[4,8]{1,0:T(4,128)}, u32[]{:S(2)}) copy-start(f32[4,8]{1,0:T(4,128)} %balance.1) | copy-start | bytes 388
  12.5 15.5 %copy-start = (s32[64]{0:T(128)S(1)}, s32[64]{0:T(128)}, u32[]{:S(2)}) copy-start(s32[64]{0:T(128)} %width.5) | copy-start | bytes 772
  17.7 7.2 %collective-permute-start.6 = (f32[168,128]{1,0:T(8,128)S(1)}, f32[168,128]{1,0:T(8,128)S(1)}, u32[]{:S(2)}, u32[]{:S(2)}) collective-permute-start(f32[168,128]{1,0:T(8,128)S(1)} %collective-permute-done.1), channel_id=1, source_target_pairs={{0,2},{2,0},{4,6},{6,4},{8,10},{10,8},{12,14},{14,12},{1,3},{3,1},... | collective-permute-start | bytes 258056 | tf_op jit(solution)/shard_map/ppermute | solution.py:526
  18.8 6.1 %collective-permute-start.5 = (f32[168,128]{1,0:T(8,128)S(1)}, f32[168,128]{1,0:T(8,128)S(1)}, u32[]{:S(2)}, u32[]{:S(2)}) collective-permute-start(f32[168,128]{1,0:T(8,128)S(1)} %collective-permute-done), channel_id=1, source_target_pairs={{0,2},{2,0},{4,6},{6,4},{8,10},{10,8},{12,14},{14,12},{1,3},{3,1},... | collective-permute-start | bytes 258056 | tf_op jit(solution)/shard_map/ppermute | solution.py:526
  19.9 5.9 %collective-permute-start.7 = (f32[168,128]{1,0:T(8,128)S(1)}, f32[168,128]{1,0:T(8,128)S(1)}, u32[]{:S(2)}, u32[]{:S(2)}) collective-permute-start(f32[168,128]{1,0:T(8,128)S(1)} %collective-permute-done.4), channel_id=1, source_target_pairs={{0,2},{2,0},{4,6},{6,4},{8,10},{10,8},{12,14},{14,12},{1,3},{3,1},... | collective-permute-start | bytes 258056 | tf_op jit(solution)/shard_map/ppermute | solution.py:526
  25.8 2.2 %collective-permute-start.8 = (f32[8,168,128]{2,1,0:T(8,128)S(1)}, f32[8,168,128]{2,1,0:T(8,128)S(1)}, u32[]{:S(2)}, u32[]{:S(2)}) collective-permute-start(f32[8,168,128]{2,1,0:T(8,128)S(1)} %bitcast_dynamic-update-slice_fusion.own), channel_id=1, source_target_pairs={{0,1},{1,0},{2,3},{3,2},{4,5},{5,4},{6,7},{7,6},{8,9},{9,8},{10,11... | collective-permute-start | bytes 2064392 | tf_op jit(solution)/shard_map/ppermute | solution.py:528
  37.0 2.7 %collective-permute-start.9 = (f32[4,4,128,128]{3,2,1,0:T(8,128)S(1)}, f32[4,4,128,128]{3,2,1,0:T(8,128)S(1)}, u32[]{:S(2)}, u32[]{:S(2)}) collective-permute-start(f32[4,4,128,128]{3,2,1,0:T(8,128)S(1)} %get-tuple-element.28.slab), channel_id=1, source_target_pairs={{0,1},{1,0},{2,3},{3,2},{4,5},{5,4},{6,7},{7,6},{8,9},{9,8},{10,11... | collective-permute-start | bytes 3145736 | tf_op jit(solution)/shard_map/ppermute | solution.py:530
  39.1 2.8 %collective-permute-start.10 = (f32[4,4,128,128]{3,2,1,0:T(8,128)S(1)}, f32[4,4,128,128]{3,2,1,0:T(8,128)S(1)}, u32[]{:S(2)}, u32[]{:S(2)}) collective-permute-start(f32[4,4,128,128]{3,2,1,0:T(8,128)S(1)} %rest.1.more), channel_id=1, source_target_pairs={{0,1},{1,0},{2,3},{3,2},{4,5},{5,4},{6,7},{7,6},{8,9},{9,8},{10,11... | collective-permute-start | bytes 3145736 | tf_op jit(solution)/shard_map/ppermute | solution.py:532

commit v7 on v6

--- a/solution.py
+++ b/solution.py
@@ -28,7 +28,7 @@
     return lax.broadcasted_iota(jnp.int32, shape, dim)
 
 
-def route_kernel(inn_ref, level_ref, owner_ref, local_ref, pay, inn, level, owner, local, sems, hot, pre, dest, left, right):
+def route_kernel(side, inn_ref, level_ref, owner_ref, local_ref, pay, inn, level, owner, local, sems, hot, pre, dest, left, right):
     pairs = ((level_ref, level), (inn_ref, inn), (owner_ref, owner), (local_ref, local))
     copies = [pltpu.make_async_copy(src, dst, sems.at[k]) for k, (src, dst) in enumerate(pairs)]
     for copy in copies:
@@ -81,18 +81,21 @@
         both = packed[2 * v * chunks : (2 * v + 1) * chunks] + packed[(2 * v + 1) * chunks : (2 * v + 2) * chunks]
         pay[pl.ds(v, chunks, stride=nvar), :] = both
     high, low = packed[2 * nvar * chunks : (2 * nvar + 1) * chunks], packed[(2 * nvar + 1) * chunks :]
-    pay[nvar * chunks : (nvar + 1) * chunks, :] = high * float(HALF) + low
-    pay[(nvar + 1) * chunks :, :] = starts
-
-
-def route(innovations, owner, level, local, levels):
+    spots = high * float(HALF) + low
+    part = chunks // 2
+    low_side = jnp.full((part, LANES), side[0], jnp.int32) == 0
+    pay[nvar * chunks : nvar * chunks + part, :] = jnp.where(low_side, spots[:part], spots[part:])
+    pay[nvar * chunks + part :, :] = starts
+
+
+def route(side, innovations, owner, level, local, levels):
     nvar, nobs = innovations.shape
     chunks = nobs // LANES
     pieces = 2 * nvar + 2
     return pl.pallas_call(
         route_kernel,
-        out_shape=jax.ShapeDtypeStruct(((nvar + 1) * chunks + 8, LANES), F32),
-        in_specs=[pl.BlockSpec(memory_space=pltpu.HBM)] * 4,
+        out_shape=jax.ShapeDtypeStruct((nvar * chunks + chunks // 2 + 8, LANES), F32),
+        in_specs=[pl.BlockSpec(memory_space=pltpu.SMEM)] + [pl.BlockSpec(memory_space=pltpu.HBM)] * 4,
         scratch_shapes=[
             pltpu.VMEM((nvar, nobs), F32),
             pltpu.VMEM((chunks, LANES), jnp.int32),
@@ -107,7 +110,7 @@
         ],
         compiler_params=pltpu.CompilerParams(vmem_limit_bytes=60 << 20),
         name="route",
-    )(innovations, level.reshape(chunks, LANES), owner.reshape(chunks, LANES), local.reshape(chunks, LANES))
+    )(side, innovations, level.reshape(chunks, LANES), owner.reshape(chunks, LANES), local.reshape(chunks, LANES))
 
 
 def table_kernel(width, base, table):
@@ -219,7 +222,7 @@
 def gather_levels(sources, nvar, chunks, base, levels, own, oth, cue, scalar_cue, sem, store, queue, level_of):
     lane = iota((8, LANES), 1)
     sub = iota((8, LANES), 0)
-    make_cues(sources, (nvar + 1) * chunks, chunks, base, levels, own, cue)
+    make_cues(sources, nvar * chunks + chunks // 2, chunks, base, levels, own, cue)
     copy = pltpu.make_async_copy(cue, scalar_cue, sem)
     copy.start()
     nothing = jnp.zeros((8, LANES), F32)
@@ -228,9 +231,14 @@
             here, there = own[s, 4 * c : 4 * c + 8, :], oth[s, 4 * c : 4 * c + 8, :]
             store[s, 16 * c : 16 * c + 8, :] = jnp.where(sub < 4, here, pltpu.roll(there, 4, 0))
             store[s, 16 * c + 16 : 16 * c + 24, :] = jnp.where(sub < 4, pltpu.roll(here, 4, 0), there)
-        for c in range(chunks):
-            spot = own[s, nvar * chunks + c : nvar * chunks + c + 1, :]
-            store[s, 16 * c + 8 : 16 * c + 16, :] = jnp.broadcast_to(spot, (8, LANES))
+        part = chunks // 2
+        halves = own[s, nvar * chunks : nvar * chunks + part, :], oth[s, nvar * chunks : nvar * chunks + part, :]
+        low_side = jnp.full((part, LANES), base, jnp.int32) == 0
+        for h in range(2):
+            spot = jnp.where(low_side, halves[h], halves[1 - h])
+            for c in range(part):
+                at = 16 * (h * part + c) + 8
+                store[s, at : at + 8, :] = jnp.broadcast_to(spot[c : c + 1, :], (8, LANES))
         store[s, 16 * chunks :, :] = jnp.zeros((16, LANES), F32)
     copy.wait()
     last = CUES * sources
@@ -398,7 +406,7 @@
 
 def field_kernel(sources, wide, nvar, width, first, start, own, oth, far_table, slab, field, table_rest, *scratch):
     table, table_sems, cue, scalar_cue, sem, store, queue, level_of = scratch
-    chunks = (own.shape[1] - 8) // (nvar + 1)
+    chunks = 2 * (own.shape[1] - 8) // (2 * nvar + 1)
     levels, part = far_table.shape[0], table.shape[0]
     base = start[0]
     fetch = pltpu.make_async_copy(far_table.at[:part], table, table_sems.at[0])
@@ -421,7 +429,7 @@
 
 def make_field(own, oth, band_width, first, base, table, nvar, levels, wide):
     sources, rows, _ = own.shape
-    chunks = (rows - 8) // (nvar + 1)
+    chunks = 2 * (rows - 8) // (2 * nvar + 1)
     whole = pl.BlockSpec(memory_space=pltpu.VMEM)
     smem = pl.BlockSpec(memory_space=pltpu.SMEM)
     pairs = levels * sources // 2 + UNROLL + 1
@@ -507,8 +515,8 @@
     nvar, _ = innovations.shape
     levels = band_width.shape[0]
     swap = [(0, 1), (1, 0)]
-    unit = route(innovations, obs_owner, obs_level, obs_local, levels)
     side = lax.axis_index("var").astype(jnp.int32)
+    unit = route(side.reshape(1), innovations, obs_owner, obs_level, obs_local, levels)
     half = levels // 2
     base = half * side
     theirs = lax.ppermute(vert_scale, "var", swap)
@@ -521,9 +529,10 @@
     far = len(own) // 2
     beside = [(i, i ^ 1) for i in range(groups)]
     near = lax.ppermute(unit, "sub", beside)
-    table = tables(band_width, base, half)
-    own[far], near, own_mats, oth_mats, table = lax.optimization_barrier((own[far], near, own_mats, oth_mats, table))
+    own[far], near, own_mats, oth_mats, when = lax.optimization_barrier((own[far], near, own_mats, oth_mats, base))
+    table = tables(band_width, when, half)
     own += [near] + [lax.ppermute(held, "sub", beside) for held in own[1:]]
+    own[-1], table = lax.optimization_barrier((own[-1], table))
     own = jnp.stack(own)
     oth = lax.ppermute(own, "var", swap)
     slab, grids, table = make_field(own, oth, band_width, first, base, table, nvar, half, NX_DEV * groups)

time: 44.5 us -> 43.6 us (0.980)
  waiting for transfers between devices: 8.67 us -> 6 us
  local copies, waits for them, and re-layouts: 1 us -> 3.02 us
    ppermute x3, waiting for transfers between devices: 4.83 us -> 0.78 us  [on_device(): own += [near] + [lax.ppermute(held, 'sub', beside) for held in own[1:]]]
    unnamed x15, local copies, waits for them, and re-layouts: 0.99 us -> 3.01 us
    ppermute x3, waiting for transfers between devices: 0.6 us -> 1.4 us  [on_device(): lax.ppermute(unit, 'sub', [(i, (i + k) % groups) for i in range(groups)])]
  transfers between devices with their start and end apart: 11 -> 11, of which waited for: 5 -> 6; matrix products, arithmetic and copies ran while one was open for 2% -> 2% of each run, Pallas kernels for 17% -> 18%
where the time goes in v7:
time: 43.6 us; the launch traced here: 43.3 us
  Pallas kernels  22.8 us (52%)
  starting transfers between devices  11.5 us (26%)
  waiting for transfers between devices  6 us (14%)
  local copies, waits for them, and re-layouts  3.02 us (7%)
    pallas_call x1, Pallas kernels, make_field(): pl.pallas_call(functools.partial(field_kernel, sources, wide, nvar), in_s...  8.85 us
    ppermute x3, starting transfers between devices, on_device(): lax.ppermute(unit, 'sub', [(i, (i + k) % groups) for i in range(groups)])  6.11 us
    pallas_call x1, Pallas kernels, route(): pl.pallas_call(route_kernel, out_shape=jax.ShapeDtypeStruct((nvar * chunk...  3.95 us
    pallas_call x1, Pallas kernels, tables(): pl.pallas_call(table_kernel, grid=(levels // depth,), in_specs=[pl.BlockS...  3.6 us
    pallas_call x2, Pallas kernels, mix(): pl.pallas_call(mix_kernel, grid=(2,), in_specs=[whole] * (4 + len(before)...  3.46 us
    ppermute x3, starting transfers between devices, on_device(): own += [near] + [lax.ppermute(held, 'sub', beside) for held in own[1:]]  3.11 us
    unnamed x15, local copies, waits for them, and re-layouts  3.01 us
    ppermute x1, waiting for transfers between devices, on_device(): oth = lax.ppermute(own, 'var', swap)  2.03 us
  transfers between devices with their start and end apart: 11, of which 6 were waited for; matrix products, arithmetic and copies ran while one was open for 2% of the time, Pallas kernels for 18%

profile of v7, /device:TPU:0, one launch (start us, length us, event | category | flops | bytes accessed | tf_op | source)
XLA Modules:
  0.0 43.3 jit_solution(2130910069782777971)
XLA Ops:
  0.0 3.9 %route.1 = f32[152,128]{1,0:T(8,128)} custom-call(s32[1]{0:T(128)} %bitcast.2.side, f32[4,4096]{1,0:T(4,128)} %inn_ref.1, s32[32,128]{1,0:T(8,128)} %bitcast.27, s32[32,128]{1,0:T(8,128)} %bitcast.28, s32[32,128]{1,0:T(8,128)} %bitcast.29), custom_call_target="tpu_custom_call" | custom-call | tf_op jit(solution)/shard_map/route/pallas_call | solution.py:95
  4.0 5.1 %collective-permute-start.4 = (f32[152,128]{1,0:T(8,128)}, f32[152,128]{1,0:T(8,128)S(1)}, u32[]{:S(2)}, u32[]{:S(2)}) collective-permute-start(f32[152,128]{1,0:T(8,128)} %route.1), channel_id=1, source_target_pairs={{0,12},{2,14},{4,0},{6,2},{8,4},{10,6},{12,8},{14,10},{1,13},{3,15... | collective-permute-start | bytes 233480 | tf_op jit(solution)/shard_map/ppermute | solution.py:528
  9.1 1.5 %collective-permute-start.2 = (f32[152,128]{1,0:T(8,128)}, f32[152,128]{1,0:T(8,128)S(1)}, u32[]{:S(2)}, u32[]{:S(2)}) collective-permute-start(f32[152,128]{1,0:T(8,128)} %route.1), channel_id=1, source_target_pairs={{0,2},{2,0},{4,6},{6,4},{8,10},{10,8},{12,14},{14,12},{1,3},{3,1},... | collective-permute-start | bytes 233480 | tf_op jit(solution)/shard_map/ppermute | solution.py:531
  10.6 0.0 collective-permute-start.1
  10.6 1.0 %collective-permute-start = (f32[152,128]{1,0:T(8,128)}, f32[152,128]{1,0:T(8,128)S(1)}, u32[]{:S(2)}, u32[]{:S(2)}) collective-permute-start(f32[152,128]{1,0:T(8,128)} %route.1), channel_id=1, source_target_pairs={{0,4},{2,6},{4,8},{6,10},{8,12},{10,14},{12,0},{14,2},{1,5},{3,7},... | collective-permute-start | bytes 233480 | tf_op jit(solution)/shard_map/ppermute | solution.py:528
  11.6 0.0 collective-permute-start.3
  11.6 0.9 %bitcast_dynamic-update-slice_fusion.7 = f32[8,152,128]{2,1,0:T(8,128)S(1)} fusion(f32[152,128]{1,0:T(8,128)} %route.1), kind=kLoop, calls=%fused_computation.7 | loop fusion | bytes 155648
  12.5 0.4 %collective-permute-done.3.theirs = f32[4,64]{1,0:T(4,128)S(1)} collective-permute-done((f32[4,64]{1,0:T(4,128)}, f32[4,64]{1,0:T(4,128)S(1)}, u32[]{:S(2)}, u32[]{:S(2)}) %collective-permute-start.3) | collective-permute-done | bytes 1056 | tf_op jit(solution)/shard_map/ppermute | solution.py:522
  13.0 0.0 copy-start.1
  13.0 0.7 %copy-done.1 = f32[4,64]{1,0:T(4,128)S(1)} copy-done((f32[4,64]{1,0:T(4,128)S(1)}, f32[4,64]{1,0:T(4,128)}, u32[]{:S(2)}) %copy-start.1) | copy-done | bytes 1048
  13.6 0.0 copy-start.2
  13.6 0.7 %copy-done.2 = f32[4,64]{1,0:T(4,128)S(1)} copy-done((f32[4,64]{1,0:T(4,128)S(1)}, f32[4,64]{1,0:T(4,128)}, u32[]{:S(2)}) %copy-start.2) | copy-done | bytes 1048
  14.3 0.0 copy-start.3
  14.3 0.7 %copy-done.3 = f32[4,8]{1,0:T(4,128)S(1)} copy-done((f32[4,8]{1,0:T(4,128)S(1)}, f32[4,8]{1,0:T(4,128)}, u32[]{:S(2)}) %copy-start.3) | copy-done | bytes 152
  15.0 0.9 %matrices.1 = (bf16[256,256]{1,0:T(8,128)(2,1)S(1)}, bf16[256,256]{1,0:T(8,128)(2,1)S(1)}, bf16[256,256]{1,0:T(8,128)(2,1)S(1)}, bf16[256,256]{1,0:T(8,128)(2,1)S(1)}) custom-call(s32[1]{0:T(128)} %bitcast.2.side, f32[4,64]{1,0:T(4,128)S(1)} %copy-done.1, f32[4,64]{1,0:T(4,128)S(1)} %collective-permute-done.3.theirs, f32[4,64]{1,0:T(4,128)S(1)} %copy-done.2, ...), custom_call_target="tpu_custom_call" | custom-call | tf_op jit(solution)/shard_map/matrices/pallas_call | solution.py:182
  15.9 0.0 collective-permute-done.2
  15.9 1.4 %collective-permute-done.1 = f32[152,128]{1,0:T(8,128)S(1)} collective-permute-done((f32[152,128]{1,0:T(8,128)}, f32[152,128]{1,0:T(8,128)S(1)}, u32[]{:S(2)}, u32[]{:S(2)}) %collective-permute-start.1) | collective-permute-done | bytes 77856 | tf_op jit(solution)/shard_map/ppermute | solution.py:528
  17.3 1.0 %collective-permute-start.6 = (f32[152,128]{1,0:T(8,128)S(1)}, f32[152,128]{1,0:T(8,128)S(1)}, u32[]{:S(2)}, u32[]{:S(2)}) collective-permute-start(f32[152,128]{1,0:T(8,128)S(1)} %collective-permute-done.1), channel_id=1, source_target_pairs={{0,2},{2,0},{4,6},{6,4},{8,10},{10,8},{12,14},{14,12},{1,3},{3,1},... | collective-permute-start | bytes 233480 | tf_op jit(solution)/shard_map/ppermute | solution.py:534
  18.2 0.0 collective-permute-done
  18.3 1.1 %collective-permute-start.5 = (f32[152,128]{1,0:T(8,128)S(1)}, f32[152,128]{1,0:T(8,128)S(1)}, u32[]{:S(2)}, u32[]{:S(2)}) collective-permute-start(f32[152,128]{1,0:T(8,128)S(1)} %collective-permute-done), channel_id=1, source_target_pairs={{0,2},{2,0},{4,6},{6,4},{8,10},{10,8},{12,14},{14,12},{1,3},{3,1},... | collective-permute-start | bytes 233480 | tf_op jit(solution)/shard_map/ppermute | solution.py:534
  19.4 0.0 collective-permute-done.4
  19.4 0.0 copy-start
  19.4 1.0 %collective-permute-start.7 = (f32[152,128]{1,0:T(8,128)S(1)}, f32[152,128]{1,0:T(8,128)S(1)}, u32[]{:S(2)}, u32[]{:S(2)}) collective-permute-start(f32[152,128]{1,0:T(8,128)S(1)} %collective-permute-done.4), channel_id=1, source_target_pairs={{0,2},{2,0},{4,6},{6,4},{8,10},{10,8},{12,14},{14,12},{1,3},{3,1},... | collective-permute-start | bytes 233480 | tf_op jit(solution)/shard_map/ppermute | solution.py:534
  20.5 3.6 %tables.1.far_table = bf16[32,256,256]{2,1,0:T(8,128)(2,1)} custom-call(s32[64]{0:T(128)} %width.5, s32[1]{0:T(128)} %bitcast.1.base.start), custom_call_target="tpu_custom_call" | custom-call | flops 16777216 | bytes 8388608 | tf_op jit(solution)/shard_map/tables/pallas_call | solution.py:134
  24.1 0.0 collective-permute-done.5
  24.1 0.8 %collective-permute-done.7 = f32[152,128]{1,0:T(8,128)S(1)} collective-permute-done((f32[152,128]{1,0:T(8,128)S(1)}, f32[152,128]{1,0:T(8,128)S(1)}, u32[]{:S(2)}, u32[]{:S(2)}) %collective-permute-start.7) | collective-permute-done | bytes 77856 | tf_op jit(solution)/shard_map/ppermute | solution.py:534
  24.8 0.0 collective-permute-done.6
  24.9 0.1 collective-permute-start.8
  25.0 2.0 %collective-permute-done.8.oth = f32[8,152,128]{2,1,0:T(8,128)S(1)} collective-permute-done((f32[8,152,128]{2,1,0:T(8,128)S(1)}, f32[8,152,128]{2,1,0:T(8,128)S(1)}, u32[]{:S(2)}, u32[]{:S(2)}) %collective-permute-start.8) | collective-permute-done | bytes 622624 | tf_op jit(solution)/shard_map/ppermute | solution.py:537
  27.0 0.0 copy-done
  27.0 8.9 %field.1 = (f32[4,4,128,128]{3,2,1,0:T(8,128)S(1)}, f32[33,128,128]{2,1,0:T(8,128)S(1)}, bf16[16,256,256]{2,1,0:T(8,128)(2,1)S(1)}) custom-call(s32[64]{0:T(128)S(1)} %copy-done, s32[1]{0:T(128)} %bitcast.first, s32[1]{0:T(128)} %bitcast.1.base.start, f32[8,152,128]{2,1,0:T(8,128)S(1)} %bitcast_dynamic-update-slice_fusion.own, ...), custom_call_target="tpu_custom_call" | custom-call | tf_op jit(solution)/shard_map/field/pallas_call | solution.py:436
  35.8 0.4 %collective-permute-start.9 = (f32[4,4,128,128]{3,2,1,0:T(8,128)S(1)}, f32[4,4,128,128]{3,2,1,0:T(8,128)S(1)}, u32[]{:S(2)}, u32[]{:S(2)}) collective-permute-start(f32[4,4,128,128]{3,2,1,0:T(8,128)S(1)} %get-tuple-element.32.slab), channel_id=1, source_target_pairs={{0,1},{1,0},{2,3},{3,2},{4,5},{5,4},{6,7},{7,6},{8,9},{9,8},{10,11... | collective-permute-start | bytes 3145736 | tf_op jit(solution)/shard_map/ppermute | solution.py:539
  36.3 2.0 %rest.1.more = f32[4,4,128,128]{3,2,1,0:T(8,128)S(1)} custom-call(s32[64]{0:T(128)S(1)} %copy-done, s32[1]{0:T(128)} %bitcast.1.base.start, f32[33,128,128]{2,1,0:T(8,128)S(1)} %get-tuple-element.33.field, bf16[16,256,256]{2,1,0:T(8,128)(2,1)S(1)} %get-tuple-element.34.table), custom_call_target="tpu_custom_call" | custom-call | flops 8589934592 | bytes 33554432 | tf_op jit(solution)/shard_map/rest/pallas_call | solution.py:463
  38.3 0.2 collective-permute-start.10
  38.5 0.1 collective-permute-done.9.slab
  38.6 1.2 %mix.2.refs_0_ = f32[2,4,256,256]{3,2,1,0:T(8,128)S(1)} custom-call(f32[4,4,128,128]{3,2,1,0:T(8,128)S(1)} %get-tuple-element.32.slab, f32[4,4,128,128]{3,2,1,0:T(8,128)S(1)} %rest.1.more, bf16[256,256]{1,0:T(8,128)(2,1)S(1)} %get-tuple-element.39.high, bf16[256,256]{1,0:T(8,128)(2,1)S(1)} %get-tuple-element.40.low), custom_call_target="tpu_custom_call" | custom-call | tf_op jit(solution)/shard_map/mix/pallas_call | solution.py:502
  39.8 1.3 %collective-permute-done.10.more = f32[4,4,128,128]{3,2,1,0:T(8,128)S(1)} collective-permute-done((f32[4,4,128,128]{3,2,1,0:T(8,128)S(1)}, f32[4,4,128,128]{3,2,1,0:T(8,128)S(1)}, u32[]{:S(2)}, u32[]{:S(2)}) %collective-permute-start.10) | collective-permute-done | bytes 1048608 | tf_op jit(solution)/shard_map/ppermute | solution.py:541
  41.1 2.3 %mix.3 = f32[256,16,128]{2,1,0:T(8,128)} custom-call(f32[4,4,128,128]{3,2,1,0:T(8,128)S(1)} %collective-permute-done.9.slab, f32[4,4,128,128]{3,2,1,0:T(8,128)S(1)} %collective-permute-done.10.more, bf16[256,256]{1,0:T(8,128)(2,1)S(1)} %get-tuple-element.36.high, bf16[256,256]{1,0:T(8,128)(2,1)S(1)} %get-tuple-element.37.low, f32[2,4,256,256]{3,2,1,0:T(8,128)S(1)} %mix.2.refs_0_), custom_call_target="tpu_custom_call" | custom-call | tf_op jit(solution)/shard_map/mix/pallas_call | solution.py:502
  (7 shorter events, 0.0 us)
Async XLA Ops:
  4.0 15.4 %collective-permute-start.4 = (f32[152,128]{1,0:T(8,128)}, f32[152,128]{1,0:T(8,128)S(1)}, u32[]{:S(2)}, u32[]{:S(2)}) collective-permute-start(f32[152,128]{1,0:T(8,128)} %route.1), channel_id=1, source_target_pairs={{0,12},{2,14},{4,0},{6,2},{8,4},{10,6},{12,8},{14,10},{1,13},{3,15... | collective-permute-start | bytes 233480 | tf_op jit(solution)/shard_map/ppermute | solution.py:528
  9.1 6.8 %collective-permute-start.2 = (f32[152,128]{1,0:T(8,128)}, f32[152,128]{1,0:T(8,128)S(1)}, u32[]{:S(2)}, u32[]{:S(2)}) collective-permute-start(f32[152,128]{1,0:T(8,128)} %route.1), channel_id=1, source_target_pairs={{0,2},{2,0},{4,6},{6,4},{8,10},{10,8},{12,14},{14,12},{1,3},{3,1},... | collective-permute-start | bytes 233480 | tf_op jit(solution)/shard_map/ppermute | solution.py:531
  10.6 6.7 %collective-permute-start.1 = (f32[152,128]{1,0:T(8,128)}, f32[152,128]{1,0:T(8,128)S(1)}, u32[]{:S(2)}, u32[]{:S(2)}) collective-permute-start(f32[152,128]{1,0:T(8,128)} %route.1), channel_id=1, source_target_pairs={{0,8},{2,10},{4,12},{6,14},{8,0},{10,2},{12,4},{14,6},{1,9},{3,11}... | collective-permute-start | bytes 233480 | tf_op jit(solution)/shard_map/ppermute | solution.py:528
  10.6 7.7 %collective-permute-start = (f32[152,128]{1,0:T(8,128)}, f32[152,128]{1,0:T(8,128)S(1)}, u32[]{:S(2)}, u32[]{:S(2)}) collective-permute-start(f32[152,128]{1,0:T(8,128)} %route.1), channel_id=1, source_target_pairs={{0,4},{2,6},{4,8},{6,10},{8,12},{10,14},{12,0},{14,2},{1,5},{3,7},... | collective-permute-start | bytes 233480 | tf_op jit(solution)/shard_map/ppermute | solution.py:528
  11.6 1.4 %collective-permute-start.3 = (f32[4,64]{1,0:T(4,128)}, f32[4,64]{1,0:T(4,128)S(1)}, u32[]{:S(2)}, u32[]{:S(2)}) collective-permute-start(f32[4,64]{1,0:T(4,128)} %scale.1), channel_id=1, source_target_pairs={{0,1},{1,0},{2,3},{3,2},{4,5},{5,4},{6,7},{7,6},{8,9},{9,8},{10,11... | collective-permute-start | bytes 3080 | tf_op jit(solution)/shard_map/ppermute | solution.py:522
  13.0 0.7 %copy-start.1 = (f32[4,64]{1,0:T(4,128)S(1)}, f32[4,64]{1,0:T(4,128)}, u32[]{:S(2)}) copy-start(f32[4,64]{1,0:T(4,128)} %scale.1) | copy-start | bytes 3076
  13.6 0.7 %copy-start.2 = (f32[4,64]{1,0:T(4,128)S(1)}, f32[4,64]{1,0:T(4,128)}, u32[]{:S(2)}) copy-start(f32[4,64]{1,0:T(4,128)} %sigma.1) | copy-start | bytes 3076
  14.3 0.7 %copy-start.3 = (f32[4,8]{1,0:T(4,128)S(1)}, f32[4,8]{1,0:T(4,128)}, u32[]{:S(2)}) copy-start(f32[4,8]{1,0:T(4,128)} %balance.1) | copy-start | bytes 388
  17.3 7.6 %collective-permute-start.6 = (f32[152,128]{1,0:T(8,128)S(1)}, f32[152,128]{1,0:T(8,128)S(1)}, u32[]{:S(2)}, u32[]{:S(2)}) collective-permute-start(f32[152,128]{1,0:T(8,128)S(1)} %collective-permute-done.1), channel_id=1, source_target_pairs={{0,2},{2,0},{4,6},{6,4},{8,10},{10,8},{12,14},{14,12},{1,3},{3,1},... | collective-permute-start | bytes 233480 | tf_op jit(solution)/shard_map/ppermute | solution.py:534
  18.3 5.8 %collective-permute-start.5 = (f32[152,128]{1,0:T(8,128)S(1)}, f32[152,128]{1,0:T(8,128)S(1)}, u32[]{:S(2)}, u32[]{:S(2)}) collective-permute-start(f32[152,128]{1,0:T(8,128)S(1)} %collective-permute-done), channel_id=1, source_target_pairs={{0,2},{2,0},{4,6},{6,4},{8,10},{10,8},{12,14},{14,12},{1,3},{3,1},... | collective-permute-start | bytes 233480 | tf_op jit(solution)/shard_map/ppermute | solution.py:534
  19.4 7.6 %copy-start = (s32[64]{0:T(128)S(1)}, s32[64]{0:T(128)}, u32[]{:S(2)}) copy-start(s32[64]{0:T(128)} %width.5) | copy-start | bytes 772
  19.4 5.4 %collective-permute-start.7 = (f32[152,128]{1,0:T(8,128)S(1)}, f32[152,128]{1,0:T(8,128)S(1)}, u32[]{:S(2)}, u32[]{:S(2)}) collective-permute-start(f32[152,128]{1,0:T(8,128)S(1)} %collective-permute-done.4), channel_id=1, source_target_pairs={{0,2},{2,0},{4,6},{6,4},{8,10},{10,8},{12,14},{14,12},{1,3},{3,1},... | collective-permute-start | bytes 233480 | tf_op jit(solution)/shard_map/ppermute | solution.py:534
  24.9 2.1 %collective-permute-start.8 = (f32[8,152,128]{2,1,0:T(8,128)S(1)}, f32[8,152,128]{2,1,0:T(8,128)S(1)}, u32[]{:S(2)}, u32[]{:S(2)}) collective-permute-start(f32[8,152,128]{2,1,0:T(8,128)S(1)} %bitcast_dynamic-update-slice_fusion.own), channel_id=1, source_target_pairs={{0,1},{1,0},{2,3},{3,2},{4,5},{5,4},{6,7},{7,6},{8,9},{9,8},{10,11... | collective-permute-start | bytes 1867784 | tf_op jit(solution)/shard_map/ppermute | solution.py:537
  35.8 2.7 %collective-permute-start.9 = (f32[4,4,128,128]{3,2,1,0:T(8,128)S(1)}, f32[4,4,128,128]{3,2,1,0:T(8,128)S(1)}, u32[]{:S(2)}, u32[]{:S(2)}) collective-permute-start(f32[4,4,128,128]{3,2,1,0:T(8,128)S(1)} %get-tuple-element.32.slab), channel_id=1, source_target_pairs={{0,1},{1,0},{2,3},{3,2},{4,5},{5,4},{6,7},{7,6},{8,9},{9,8},{10,11... | collective-permute-start | bytes 3145736 | tf_op jit(solution)/shard_map/ppermute | solution.py:539
  38.3 2.7 %collective-permute-start.10 = (f32[4,4,128,128]{3,2,1,0:T(8,128)S(1)}, f32[4,4,128,128]{3,2,1,0:T(8,128)S(1)}, u32[]{:S(2)}, u32[]{:S(2)}) collective-permute-start(f32[4,4,128,128]{3,2,1,0:T(8,128)S(1)} %rest.1.more), channel_id=1, source_target_pairs={{0,1},{1,0},{2,3},{3,2},{4,5},{5,4},{6,7},{7,6},{8,9},{9,8},{10,11... | collective-permute-start | bytes 3145736 | tf_op jit(solution)/shard_map/ppermute | solution.py:541

commit v8 on v7

--- a/solution.py
+++ b/solution.py
@@ -277,11 +277,11 @@
             level_of[pair + p] = k
 
     def group(g, carry):
-        for p in range(2):
-            per_level(2 * g + p)
+        for p in range(4):
+            per_level(4 * g + p)
         return carry
 
-    lax.fori_loop(0, levels // 2, group, 0)
+    lax.fori_loop(0, levels // 4, group, 0)
     pair = scalar_cue[last + 2, 0]
     for p in range(UNROLL):
         level_of[pair + p] = levels
@@ -397,11 +397,11 @@
                 bound = bound * hop
 
     def group(g, carry):
-        for p in range(4):
-            one_level(4 * g + p)
+        for p in range(8):
+            one_level(8 * g + p)
         return carry
 
-    lax.fori_loop(0, levels // 4, group, 0)
+    lax.fori_loop(0, levels // 8, group, 0)
 
 
 def field_kernel(sources, wide, nvar, width, first, start, own, oth, far_table, slab, field, table_rest, *scratch):

time: 43.6 us -> 42.3 us (0.970)
  Pallas kernels: 22.8 us -> 21.3 us
    pallas_call x1, Pallas kernels: 8.85 us -> 7.88 us  [make_field(): pl.pallas_call(functools.partial(field_kernel, sources, wide, nvar), in_s...]
    ppermute x1, waiting for transfers between devices: 0.06 us -> 0.59 us  [on_device(): swapped = lax.ppermute(slab, 'var', swap)]
    ppermute x1, waiting for transfers between devices: 1.28 us -> 0.84 us  [on_device(): more_swapped = lax.ppermute(more, 'var', swap)]
    pallas_call x1, Pallas kernels: 2.03 us -> 1.59 us  [filter_rest(): pl.pallas_call(rest_kernel, in_specs=[smem, smem, whole, whole], out_spec...]
  transfers between devices with their start and end apart: 11 -> 11, of which waited for: 6 -> 6; matrix products, arithmetic and copies ran while one was open for 2% -> 2% of each run, Pallas kernels for 18% -> 17%
where the time goes in v8:
time: 42.3 us; the launch traced here: 42 us
  Pallas kernels  21.3 us (50%)
  starting transfers between devices  11.5 us (27%)
  waiting for transfers between devices  6.08 us (14%)
  local copies, waits for them, and re-layouts  3.02 us (7%)
    pallas_call x1, Pallas kernels, make_field(): pl.pallas_call(functools.partial(field_kernel, sources, wide, nvar), in_s...  7.88 us
    ppermute x3, starting transfers between devices, on_device(): lax.ppermute(unit, 'sub', [(i, (i + k) % groups) for i in range(groups)])  6.11 us
    pallas_call x1, Pallas kernels, route(): pl.pallas_call(route_kernel, out_shape=jax.ShapeDtypeStruct((nvar * chunk...  3.95 us
    pallas_call x1, Pallas kernels, tables(): pl.pallas_call(table_kernel, grid=(levels // depth,), in_specs=[pl.BlockS...  3.6 us
    pallas_call x2, Pallas kernels, mix(): pl.pallas_call(mix_kernel, grid=(2,), in_specs=[whole] * (4 + len(before)...  3.47 us
    ppermute x3, starting transfers between devices, on_device(): own += [near] + [lax.ppermute(held, 'sub', beside) for held in own[1:]]  3.11 us
    unnamed x15, local copies, waits for them, and re-layouts  3.01 us
    ppermute x1, waiting for transfers between devices, on_device(): oth = lax.ppermute(own, 'var', swap)  2.03 us
  transfers between devices with their start and end apart: 11, of which 6 were waited for; matrix products, arithmetic and copies ran while one was open for 2% of the time, Pallas kernels for 17%

profile of v8, /device:TPU:0, one launch (start us, length us, event | category | flops | bytes accessed | tf_op | source)
XLA Modules:
  0.0 42.0 jit_solution(14929373072460979161)
XLA Ops:
  0.0 3.9 %route.1 = f32[152,128]{1,0:T(8,128)} custom-call(s32[1]{0:T(128)} %bitcast.2.side, f32[4,4096]{1,0:T(4,128)} %inn_ref.1, s32[32,128]{1,0:T(8,128)} %bitcast.27, s32[32,128]{1,0:T(8,128)} %bitcast.28, s32[32,128]{1,0:T(8,128)} %bitcast.29), custom_call_target="tpu_custom_call" | custom-call | tf_op jit(solution)/shard_map/route/pallas_call | solution.py:95
  4.0 5.1 %collective-permute-start.4 = (f32[152,128]{1,0:T(8,128)}, f32[152,128]{1,0:T(8,128)S(1)}, u32[]{:S(2)}, u32[]{:S(2)}) collective-permute-start(f32[152,128]{1,0:T(8,128)} %route.1), channel_id=1, source_target_pairs={{0,12},{2,14},{4,0},{6,2},{8,4},{10,6},{12,8},{14,10},{1,13},{3,15... | collective-permute-start | bytes 233480 | tf_op jit(solution)/shard_map/ppermute | solution.py:528
  9.1 1.5 %collective-permute-start.2 = (f32[152,128]{1,0:T(8,128)}, f32[152,128]{1,0:T(8,128)S(1)}, u32[]{:S(2)}, u32[]{:S(2)}) collective-permute-start(f32[152,128]{1,0:T(8,128)} %route.1), channel_id=1, source_target_pairs={{0,2},{2,0},{4,6},{6,4},{8,10},{10,8},{12,14},{14,12},{1,3},{3,1},... | collective-permute-start | bytes 233480 | tf_op jit(solution)/shard_map/ppermute | solution.py:531
  10.6 0.0 collective-permute-start.1
  10.6 1.0 %collective-permute-start = (f32[152,128]{1,0:T(8,128)}, f32[152,128]{1,0:T(8,128)S(1)}, u32[]{:S(2)}, u32[]{:S(2)}) collective-permute-start(f32[152,128]{1,0:T(8,128)} %route.1), channel_id=1, source_target_pairs={{0,4},{2,6},{4,8},{6,10},{8,12},{10,14},{12,0},{14,2},{1,5},{3,7},... | collective-permute-start | bytes 233480 | tf_op jit(solution)/shard_map/ppermute | solution.py:528
  11.6 0.0 collective-permute-start.3
  11.6 0.9 %bitcast_dynamic-update-slice_fusion.7 = f32[8,152,128]{2,1,0:T(8,128)S(1)} fusion(f32[152,128]{1,0:T(8,128)} %route.1), kind=kLoop, calls=%fused_computation.7 | loop fusion | bytes 155648
  12.5 0.4 %collective-permute-done.3.theirs = f32[4,64]{1,0:T(4,128)S(1)} collective-permute-done((f32[4,64]{1,0:T(4,128)}, f32[4,64]{1,0:T(4,128)S(1)}, u32[]{:S(2)}, u32[]{:S(2)}) %collective-permute-start.3) | collective-permute-done | bytes 1056 | tf_op jit(solution)/shard_map/ppermute | solution.py:522
  13.0 0.0 copy-start.1
  13.0 0.7 %copy-done.1 = f32[4,64]{1,0:T(4,128)S(1)} copy-done((f32[4,64]{1,0:T(4,128)S(1)}, f32[4,64]{1,0:T(4,128)}, u32[]{:S(2)}) %copy-start.1) | copy-done | bytes 1048
  13.6 0.0 copy-start.2
  13.6 0.7 %copy-done.2 = f32[4,64]{1,0:T(4,128)S(1)} copy-done((f32[4,64]{1,0:T(4,128)S(1)}, f32[4,64]{1,0:T(4,128)}, u32[]{:S(2)}) %copy-start.2) | copy-done | bytes 1048
  14.3 0.0 copy-start.3
  14.3 0.7 %copy-done.3 = f32[4,8]{1,0:T(4,128)S(1)} copy-done((f32[4,8]{1,0:T(4,128)S(1)}, f32[4,8]{1,0:T(4,128)}, u32[]{:S(2)}) %copy-start.3) | copy-done | bytes 152
  15.0 0.9 %matrices.1 = (bf16[256,256]{1,0:T(8,128)(2,1)S(1)}, bf16[256,256]{1,0:T(8,128)(2,1)S(1)}, bf16[256,256]{1,0:T(8,128)(2,1)S(1)}, bf16[256,256]{1,0:T(8,128)(2,1)S(1)}) custom-call(s32[1]{0:T(128)} %bitcast.2.side, f32[4,64]{1,0:T(4,128)S(1)} %copy-done.1, f32[4,64]{1,0:T(4,128)S(1)} %collective-permute-done.3.theirs, f32[4,64]{1,0:T(4,128)S(1)} %copy-done.2, ...), custom_call_target="tpu_custom_call" | custom-call | tf_op jit(solution)/shard_map/matrices/pallas_call | solution.py:182
  15.9 0.0 collective-permute-done.2
  15.9 1.4 %collective-permute-done.1 = f32[152,128]{1,0:T(8,128)S(1)} collective-permute-done((f32[152,128]{1,0:T(8,128)}, f32[152,128]{1,0:T(8,128)S(1)}, u32[]{:S(2)}, u32[]{:S(2)}) %collective-permute-start.1) | collective-permute-done | bytes 77856 | tf_op jit(solution)/shard_map/ppermute | solution.py:528
  17.3 1.0 %collective-permute-start.6 = (f32[152,128]{1,0:T(8,128)S(1)}, f32[152,128]{1,0:T(8,128)S(1)}, u32[]{:S(2)}, u32[]{:S(2)}) collective-permute-start(f32[152,128]{1,0:T(8,128)S(1)} %collective-permute-done.1), channel_id=1, source_target_pairs={{0,2},{2,0},{4,6},{6,4},{8,10},{10,8},{12,14},{14,12},{1,3},{3,1},... | collective-permute-start | bytes 233480 | tf_op jit(solution)/shard_map/ppermute | solution.py:534
  18.2 0.0 collective-permute-done
  18.3 1.1 %collective-permute-start.5 = (f32[152,128]{1,0:T(8,128)S(1)}, f32[152,128]{1,0:T(8,128)S(1)}, u32[]{:S(2)}, u32[]{:S(2)}) collective-permute-start(f32[152,128]{1,0:T(8,128)S(1)} %collective-permute-done), channel_id=1, source_target_pairs={{0,2},{2,0},{4,6},{6,4},{8,10},{10,8},{12,14},{14,12},{1,3},{3,1},... | collective-permute-start | bytes 233480 | tf_op jit(solution)/shard_map/ppermute | solution.py:534
  19.4 0.0 collective-permute-done.4
  19.4 0.0 copy-start
  19.4 1.0 %collective-permute-start.7 = (f32[152,128]{1,0:T(8,128)S(1)}, f32[152,128]{1,0:T(8,128)S(1)}, u32[]{:S(2)}, u32[]{:S(2)}) collective-permute-start(f32[152,128]{1,0:T(8,128)S(1)} %collective-permute-done.4), channel_id=1, source_target_pairs={{0,2},{2,0},{4,6},{6,4},{8,10},{10,8},{12,14},{14,12},{1,3},{3,1},... | collective-permute-start | bytes 233480 | tf_op jit(solution)/shard_map/ppermute | solution.py:534
  20.5 3.6 %tables.1.far_table = bf16[32,256,256]{2,1,0:T(8,128)(2,1)} custom-call(s32[64]{0:T(128)} %width.5, s32[1]{0:T(128)} %bitcast.1.base.start), custom_call_target="tpu_custom_call" | custom-call | flops 16777216 | bytes 8388608 | tf_op jit(solution)/shard_map/tables/pallas_call | solution.py:134
  24.1 0.0 collective-permute-done.5
  24.1 0.8 %collective-permute-done.7 = f32[152,128]{1,0:T(8,128)S(1)} collective-permute-done((f32[152,128]{1,0:T(8,128)S(1)}, f32[152,128]{1,0:T(8,128)S(1)}, u32[]{:S(2)}, u32[]{:S(2)}) %collective-permute-start.7) | collective-permute-done | bytes 77856 | tf_op jit(solution)/shard_map/ppermute | solution.py:534
  24.8 0.0 collective-permute-done.6
  24.9 0.1 collective-permute-start.8
  25.0 2.0 %collective-permute-done.8.oth = f32[8,152,128]{2,1,0:T(8,128)S(1)} collective-permute-done((f32[8,152,128]{2,1,0:T(8,128)S(1)}, f32[8,152,128]{2,1,0:T(8,128)S(1)}, u32[]{:S(2)}, u32[]{:S(2)}) %collective-permute-start.8) | collective-permute-done | bytes 622624 | tf_op jit(solution)/shard_map/ppermute | solution.py:537
  27.0 0.0 copy-done
  27.0 7.9 %field.1 = (f32[4,4,128,128]{3,2,1,0:T(8,128)S(1)}, f32[33,128,128]{2,1,0:T(8,128)S(1)}, bf16[16,256,256]{2,1,0:T(8,128)(2,1)S(1)}) custom-call(s32[64]{0:T(128)S(1)} %copy-done, s32[1]{0:T(128)} %bitcast.first, s32[1]{0:T(128)} %bitcast.1.base.start, f32[8,152,128]{2,1,0:T(8,128)S(1)} %bitcast_dynamic-update-slice_fusion.own, ...), custom_call_target="tpu_custom_call" | custom-call | tf_op jit(solution)/shard_map/field/pallas_call | solution.py:436
  34.9 0.5 %collective-permute-start.9 = (f32[4,4,128,128]{3,2,1,0:T(8,128)S(1)}, f32[4,4,128,128]{3,2,1,0:T(8,128)S(1)}, u32[]{:S(2)}, u32[]{:S(2)}) collective-permute-start(f32[4,4,128,128]{3,2,1,0:T(8,128)S(1)} %get-tuple-element.32.slab), channel_id=1, source_target_pairs={{0,1},{1,0},{2,3},{3,2},{4,5},{5,4},{6,7},{7,6},{8,9},{9,8},{10,11... | collective-permute-start | bytes 3145736 | tf_op jit(solution)/shard_map/ppermute | solution.py:539
  35.4 1.6 %rest.1.more = f32[4,4,128,128]{3,2,1,0:T(8,128)S(1)} custom-call(s32[64]{0:T(128)S(1)} %copy-done, s32[1]{0:T(128)} %bitcast.1.base.start, f32[33,128,128]{2,1,0:T(8,128)S(1)} %get-tuple-element.33.field, bf16[16,256,256]{2,1,0:T(8,128)(2,1)S(1)} %get-tuple-element.34.table), custom_call_target="tpu_custom_call" | custom-call | flops 8589934592 | bytes 33554432 | tf_op jit(solution)/shard_map/rest/pallas_call | solution.py:463
  37.0 0.1 collective-permute-start.10
  37.1 0.6 %collective-permute-done.9.slab = f32[4,4,128,128]{3,2,1,0:T(8,128)S(1)} collective-permute-done((f32[4,4,128,128]{3,2,1,0:T(8,128)S(1)}, f32[4,4,128,128]{3,2,1,0:T(8,128)S(1)}, u32[]{:S(2)}, u32[]{:S(2)}) %collective-permute-start.9) | collective-permute-done | bytes 1048608 | tf_op jit(solution)/shard_map/ppermute | solution.py:539
  37.7 1.2 %mix.2.refs_0_ = f32[2,4,256,256]{3,2,1,0:T(8,128)S(1)} custom-call(f32[4,4,128,128]{3,2,1,0:T(8,128)S(1)} %get-tuple-element.32.slab, f32[4,4,128,128]{3,2,1,0:T(8,128)S(1)} %rest.1.more, bf16[256,256]{1,0:T(8,128)(2,1)S(1)} %get-tuple-element.39.high, bf16[256,256]{1,0:T(8,128)(2,1)S(1)} %get-tuple-element.40.low), custom_call_target="tpu_custom_call" | custom-call | tf_op jit(solution)/shard_map/mix/pallas_call | solution.py:502
  38.9 0.8 %collective-permute-done.10.more = f32[4,4,128,128]{3,2,1,0:T(8,128)S(1)} collective-permute-done((f32[4,4,128,128]{3,2,1,0:T(8,128)S(1)}, f32[4,4,128,128]{3,2,1,0:T(8,128)S(1)}, u32[]{:S(2)}, u32[]{:S(2)}) %collective-permute-start.10) | collective-permute-done | bytes 1048608 | tf_op jit(solution)/shard_map/ppermute | solution.py:541
  39.7 2.3 %mix.3 = f32[256,16,128]{2,1,0:T(8,128)} custom-call(f32[4,4,128,128]{3,2,1,0:T(8,128)S(1)} %collective-permute-done.9.slab, f32[4,4,128,128]{3,2,1,0:T(8,128)S(1)} %collective-permute-done.10.more, bf16[256,256]{1,0:T(8,128)(2,1)S(1)} %get-tuple-element.36.high, bf16[256,256]{1,0:T(8,128)(2,1)S(1)} %get-tuple-element.37.low, f32[2,4,256,256]{3,2,1,0:T(8,128)S(1)} %mix.2.refs_0_), custom_call_target="tpu_custom_call" | custom-call | tf_op jit(solution)/shard_map/mix/pallas_call | solution.py:502
  (7 shorter events, 0.0 us)
Async XLA Ops:
  4.0 15.4 %collective-permute-start.4 = (f32[152,128]{1,0:T(8,128)}, f32[152,128]{1,0:T(8,128)S(1)}, u32[]{:S(2)}, u32[]{:S(2)}) collective-permute-start(f32[152,128]{1,0:T(8,128)} %route.1), channel_id=1, source_target_pairs={{0,12},{2,14},{4,0},{6,2},{8,4},{10,6},{12,8},{14,10},{1,13},{3,15... | collective-permute-start | bytes 233480 | tf_op jit(solution)/shard_map/ppermute | solution.py:528
  9.1 6.8 %collective-permute-start.2 = (f32[152,128]{1,0:T(8,128)}, f32[152,128]{1,0:T(8,128)S(1)}, u32[]{:S(2)}, u32[]{:S(2)}) collective-permute-start(f32[152,128]{1,0:T(8,128)} %route.1), channel_id=1, source_target_pairs={{0,2},{2,0},{4,6},{6,4},{8,10},{10,8},{12,14},{14,12},{1,3},{3,1},... | collective-permute-start | bytes 233480 | tf_op jit(solution)/shard_map/ppermute | solution.py:531
  10.6 6.7 %collective-permute-start.1 = (f32[152,128]{1,0:T(8,128)}, f32[152,128]{1,0:T(8,128)S(1)}, u32[]{:S(2)}, u32[]{:S(2)}) collective-permute-start(f32[152,128]{1,0:T(8,128)} %route.1), channel_id=1, source_target_pairs={{0,8},{2,10},{4,12},{6,14},{8,0},{10,2},{12,4},{14,6},{1,9},{3,11}... | collective-permute-start | bytes 233480 | tf_op jit(solution)/shard_map/ppermute | solution.py:528
  10.6 7.7 %collective-permute-start = (f32[152,128]{1,0:T(8,128)}, f32[152,128]{1,0:T(8,128)S(1)}, u32[]{:S(2)}, u32[]{:S(2)}) collective-permute-start(f32[152,128]{1,0:T(8,128)} %route.1), channel_id=1, source_target_pairs={{0,4},{2,6},{4,8},{6,10},{8,12},{10,14},{12,0},{14,2},{1,5},{3,7},... | collective-permute-start | bytes 233480 | tf_op jit(solution)/shard_map/ppermute | solution.py:528
  11.6 1.4 %collective-permute-start.3 = (f32[4,64]{1,0:T(4,128)}, f32[4,64]{1,0:T(4,128)S(1)}, u32[]{:S(2)}, u32[]{:S(2)}) collective-permute-start(f32[4,64]{1,0:T(4,128)} %scale.1), channel_id=1, source_target_pairs={{0,1},{1,0},{2,3},{3,2},{4,5},{5,4},{6,7},{7,6},{8,9},{9,8},{10,11... | collective-permute-start | bytes 3080 | tf_op jit(solution)/shard_map/ppermute | solution.py:522
  13.0 0.7 %copy-start.1 = (f32[4,64]{1,0:T(4,128)S(1)}, f32[4,64]{1,0:T(4,128)}, u32[]{:S(2)}) copy-start(f32[4,64]{1,0:T(4,128)} %scale.1) | copy-start | bytes 3076
  13.6 0.7 %copy-start.2 = (f32[4,64]{1,0:T(4,128)S(1)}, f32[4,64]{1,0:T(4,128)}, u32[]{:S(2)}) copy-start(f32[4,64]{1,0:T(4,128)} %sigma.1) | copy-start | bytes 3076
  14.3 0.7 %copy-start.3 = (f32[4,8]{1,0:T(4,128)S(1)}, f32[4,8]{1,0:T(4,128)}, u32[]{:S(2)}) copy-start(f32[4,8]{1,0:T(4,128)} %balance.1) | copy-start | bytes 388
  17.3 7.6 %collective-permute-start.6 = (f32[152,128]{1,0:T(8,128)S(1)}, f32[152,128]{1,0:T(8,128)S(1)}, u32[]{:S(2)}, u32[]{:S(2)}) collective-permute-start(f32[152,128]{1,0:T(8,128)S(1)} %collective-permute-done.1), channel_id=1, source_target_pairs={{0,2},{2,0},{4,6},{6,4},{8,10},{10,8},{12,14},{14,12},{1,3},{3,1},... | collective-permute-start | bytes 233480 | tf_op jit(solution)/shard_map/ppermute | solution.py:534
  18.3 5.8 %collective-permute-start.5 = (f32[152,128]{1,0:T(8,128)S(1)}, f32[152,128]{1,0:T(8,128)S(1)}, u32[]{:S(2)}, u32[]{:S(2)}) collective-permute-start(f32[152,128]{1,0:T(8,128)S(1)} %collective-permute-done), channel_id=1, source_target_pairs={{0,2},{2,0},{4,6},{6,4},{8,10},{10,8},{12,14},{14,12},{1,3},{3,1},... | collective-permute-start | bytes 233480 | tf_op jit(solution)/shard_map/ppermute | solution.py:534
  19.4 7.6 %copy-start = (s32[64]{0:T(128)S(1)}, s32[64]{0:T(128)}, u32[]{:S(2)}) copy-start(s32[64]{0:T(128)} %width.5) | copy-start | bytes 772
  19.4 5.4 %collective-permute-start.7 = (f32[152,128]{1,0:T(8,128)S(1)}, f32[152,128]{1,0:T(8,128)S(1)}, u32[]{:S(2)}, u32[]{:S(2)}) collective-permute-start(f32[152,128]{1,0:T(8,128)S(1)} %collective-permute-done.4), channel_id=1, source_target_pairs={{0,2},{2,0},{4,6},{6,4},{8,10},{10,8},{12,14},{14,12},{1,3},{3,1},... | collective-permute-start | bytes 233480 | tf_op jit(solution)/shard_map/ppermute | solution.py:534
  24.9 2.1 %collective-permute-start.8 = (f32[8,152,128]{2,1,0:T(8,128)S(1)}, f32[8,152,128]{2,1,0:T(8,128)S(1)}, u32[]{:S(2)}, u32[]{:S(2)}) collective-permute-start(f32[8,152,128]{2,1,0:T(8,128)S(1)} %bitcast_dynamic-update-slice_fusion.own), channel_id=1, source_target_pairs={{0,1},{1,0},{2,3},{3,2},{4,5},{5,4},{6,7},{7,6},{8,9},{9,8},{10,11... | collective-permute-start | bytes 1867784 | tf_op jit(solution)/shard_map/ppermute | solution.py:537
  34.9 2.8 %collective-permute-start.9 = (f32[4,4,128,128]{3,2,1,0:T(8,128)S(1)}, f32[4,4,128,128]{3,2,1,0:T(8,128)S(1)}, u32[]{:S(2)}, u32[]{:S(2)}) collective-permute-start(f32[4,4,128,128]{3,2,1,0:T(8,128)S(1)} %get-tuple-element.32.slab), channel_id=1, source_target_pairs={{0,1},{1,0},{2,3},{3,2},{4,5},{5,4},{6,7},{7,6},{8,9},{9,8},{10,11... | collective-permute-start | bytes 3145736 | tf_op jit(solution)/shard_map/ppermute | solution.py:539
  37.0 2.7 %collective-permute-start.10 = (f32[4,4,128,128]{3,2,1,0:T(8,128)S(1)}, f32[4,4,128,128]{3,2,1,0:T(8,128)S(1)}, u32[]{:S(2)}, u32[]{:S(2)}) collective-permute-start(f32[4,4,128,128]{3,2,1,0:T(8,128)S(1)} %rest.1.more), channel_id=1, source_target_pairs={{0,1},{1,0},{2,3},{3,2},{4,5},{5,4},{6,7},{7,6},{8,9},{9,8},{10,11... | collective-permute-start | bytes 3145736 | tf_op jit(solution)/shard_map/ppermute | solution.py:541

commit v9 on v8

--- a/solution.py
+++ b/solution.py
@@ -277,11 +277,11 @@
             level_of[pair + p] = k
 
     def group(g, carry):
-        for p in range(4):
-            per_level(4 * g + p)
+        for p in range(8):
+            per_level(8 * g + p)
         return carry
 
-    lax.fori_loop(0, levels // 4, group, 0)
+    lax.fori_loop(0, levels // 8, group, 0)
     pair = scalar_cue[last + 2, 0]
     for p in range(UNROLL):
         level_of[pair + p] = levels
@@ -397,11 +397,11 @@
                 bound = bound * hop
 
     def group(g, carry):
-        for p in range(8):
-            one_level(8 * g + p)
+        for p in range(16):
+            one_level(16 * g + p)
         return carry
 
-    lax.fori_loop(0, levels // 8, group, 0)
+    lax.fori_loop(0, levels // 16, group, 0)
 
 
 def field_kernel(sources, wide, nvar, width, first, start, own, oth, far_table, slab, field, table_rest, *scratch):

time: 42.3 us -> 41.9 us (level)
  no operation moved by 1% of the time
where the time goes in v9:
time: 41.9 us; the launch traced here: 41.7 us
  Pallas kernels  21.1 us (50%)
  starting transfers between devices  11.5 us (27%)
  waiting for transfers between devices  6 us (14%)
  local copies, waits for them, and re-layouts  3.02 us (7%)
    pallas_call x1, Pallas kernels, make_field(): pl.pallas_call(functools.partial(field_kernel, sources, wide, nvar), in_s...  7.79 us
    ppermute x3, starting transfers between devices, on_device(): lax.ppermute(unit, 'sub', [(i, (i + k) % groups) for i in range(groups)])  6.11 us
    pallas_call x1, Pallas kernels, route(): pl.pallas_call(route_kernel, out_shape=jax.ShapeDtypeStruct((nvar * chunk...  3.95 us
    pallas_call x1, Pallas kernels, tables(): pl.pallas_call(table_kernel, grid=(levels // depth,), in_specs=[pl.BlockS...  3.6 us
    pallas_call x2, Pallas kernels, mix(): pl.pallas_call(mix_kernel, grid=(2,), in_specs=[whole] * (4 + len(before)...  3.46 us
    ppermute x3, starting transfers between devices, on_device(): own += [near] + [lax.ppermute(held, 'sub', beside) for held in own[1:]]  3.11 us
    unnamed x15, local copies, waits for them, and re-layouts  3.01 us
    ppermute x1, waiting for transfers between devices, on_device(): oth = lax.ppermute(own, 'var', swap)  2.03 us
  transfers between devices with their start and end apart: 11, of which 6 were waited for; matrix products, arithmetic and copies ran while one was open for 2% of the time, Pallas kernels for 17%

profile of v9, /device:TPU:0, one launch (start us, length us, event | category | flops | bytes accessed | tf_op | source)
XLA Modules:
  0.0 41.7 jit_solution(1904259207780945040)
XLA Ops:
  0.0 3.9 %route.1 = f32[152,128]{1,0:T(8,128)} custom-call(s32[1]{0:T(128)} %bitcast.2.side, f32[4,4096]{1,0:T(4,128)} %inn_ref.1, s32[32,128]{1,0:T(8,128)} %bitcast.27, s32[32,128]{1,0:T(8,128)} %bitcast.28, s32[32,128]{1,0:T(8,128)} %bitcast.29), custom_call_target="tpu_custom_call" | custom-call | tf_op jit(solution)/shard_map/route/pallas_call | solution.py:95
  4.0 5.1 %collective-permute-start.4 = (f32[152,128]{1,0:T(8,128)}, f32[152,128]{1,0:T(8,128)S(1)}, u32[]{:S(2)}, u32[]{:S(2)}) collective-permute-start(f32[152,128]{1,0:T(8,128)} %route.1), channel_id=1, source_target_pairs={{0,12},{2,14},{4,0},{6,2},{8,4},{10,6},{12,8},{14,10},{1,13},{3,15... | collective-permute-start | bytes 233480 | tf_op jit(solution)/shard_map/ppermute | solution.py:528
  9.1 1.5 %collective-permute-start.2 = (f32[152,128]{1,0:T(8,128)}, f32[152,128]{1,0:T(8,128)S(1)}, u32[]{:S(2)}, u32[]{:S(2)}) collective-permute-start(f32[152,128]{1,0:T(8,128)} %route.1), channel_id=1, source_target_pairs={{0,2},{2,0},{4,6},{6,4},{8,10},{10,8},{12,14},{14,12},{1,3},{3,1},... | collective-permute-start | bytes 233480 | tf_op jit(solution)/shard_map/ppermute | solution.py:531
  10.6 0.0 collective-permute-start.1
  10.6 1.0 %collective-permute-start = (f32[152,128]{1,0:T(8,128)}, f32[152,128]{1,0:T(8,128)S(1)}, u32[]{:S(2)}, u32[]{:S(2)}) collective-permute-start(f32[152,128]{1,0:T(8,128)} %route.1), channel_id=1, source_target_pairs={{0,4},{2,6},{4,8},{6,10},{8,12},{10,14},{12,0},{14,2},{1,5},{3,7},... | collective-permute-start | bytes 233480 | tf_op jit(solution)/shard_map/ppermute | solution.py:528
  11.6 0.0 collective-permute-start.3
  11.6 0.9 %bitcast_dynamic-update-slice_fusion.7 = f32[8,152,128]{2,1,0:T(8,128)S(1)} fusion(f32[152,128]{1,0:T(8,128)} %route.1), kind=kLoop, calls=%fused_computation.7 | loop fusion | bytes 155648
  12.5 0.4 %collective-permute-done.3.theirs = f32[4,64]{1,0:T(4,128)S(1)} collective-permute-done((f32[4,64]{1,0:T(4,128)}, f32[4,64]{1,0:T(4,128)S(1)}, u32[]{:S(2)}, u32[]{:S(2)}) %collective-permute-start.3) | collective-permute-done | bytes 1056 | tf_op jit(solution)/shard_map/ppermute | solution.py:522
  13.0 0.0 copy-start.1
  13.0 0.7 %copy-done.1 = f32[4,64]{1,0:T(4,128)S(1)} copy-done((f32[4,64]{1,0:T(4,128)S(1)}, f32[4,64]{1,0:T(4,128)}, u32[]{:S(2)}) %copy-start.1) | copy-done | bytes 1048
  13.6 0.0 copy-start.2
  13.6 0.7 %copy-done.2 = f32[4,64]{1,0:T(4,128)S(1)} copy-done((f32[4,64]{1,0:T(4,128)S(1)}, f32[4,64]{1,0:T(4,128)}, u32[]{:S(2)}) %copy-start.2) | copy-done | bytes 1048
  14.3 0.0 copy-start.3
  14.3 0.7 %copy-done.3 = f32[4,8]{1,0:T(4,128)S(1)} copy-done((f32[4,8]{1,0:T(4,128)S(1)}, f32[4,8]{1,0:T(4,128)}, u32[]{:S(2)}) %copy-start.3) | copy-done | bytes 152
  15.0 0.9 %matrices.1 = (bf16[256,256]{1,0:T(8,128)(2,1)S(1)}, bf16[256,256]{1,0:T(8,128)(2,1)S(1)}, bf16[256,256]{1,0:T(8,128)(2,1)S(1)}, bf16[256,256]{1,0:T(8,128)(2,1)S(1)}) custom-call(s32[1]{0:T(128)} %bitcast.2.side, f32[4,64]{1,0:T(4,128)S(1)} %copy-done.1, f32[4,64]{1,0:T(4,128)S(1)} %collective-permute-done.3.theirs, f32[4,64]{1,0:T(4,128)S(1)} %copy-done.2, ...), custom_call_target="tpu_custom_call" | custom-call | tf_op jit(solution)/shard_map/matrices/pallas_call | solution.py:182
  15.9 0.0 collective-permute-done.2
  15.9 1.4 %collective-permute-done.1 = f32[152,128]{1,0:T(8,128)S(1)} collective-permute-done((f32[152,128]{1,0:T(8,128)}, f32[152,128]{1,0:T(8,128)S(1)}, u32[]{:S(2)}, u32[]{:S(2)}) %collective-permute-start.1) | collective-permute-done | bytes 77856 | tf_op jit(solution)/shard_map/ppermute | solution.py:528
  17.3 1.0 %collective-permute-start.6 = (f32[152,128]{1,0:T(8,128)S(1)}, f32[152,128]{1,0:T(8,128)S(1)}, u32[]{:S(2)}, u32[]{:S(2)}) collective-permute-start(f32[152,128]{1,0:T(8,128)S(1)} %collective-permute-done.1), channel_id=1, source_target_pairs={{0,2},{2,0},{4,6},{6,4},{8,10},{10,8},{12,14},{14,12},{1,3},{3,1},... | collective-permute-start | bytes 233480 | tf_op jit(solution)/shard_map/ppermute | solution.py:534
  18.2 0.0 collective-permute-done
  18.3 1.1 %collective-permute-start.5 = (f32[152,128]{1,0:T(8,128)S(1)}, f32[152,128]{1,0:T(8,128)S(1)}, u32[]{:S(2)}, u32[]{:S(2)}) collective-permute-start(f32[152,128]{1,0:T(8,128)S(1)} %collective-permute-done), channel_id=1, source_target_pairs={{0,2},{2,0},{4,6},{6,4},{8,10},{10,8},{12,14},{14,12},{1,3},{3,1},... | collective-permute-start | bytes 233480 | tf_op jit(solution)/shard_map/ppermute | solution.py:534
  19.4 0.0 collective-permute-done.4
  19.4 0.0 copy-start
  19.4 1.0 %collective-permute-start.7 = (f32[152,128]{1,0:T(8,128)S(1)}, f32[152,128]{1,0:T(8,128)S(1)}, u32[]{:S(2)}, u32[]{:S(2)}) collective-permute-start(f32[152,128]{1,0:T(8,128)S(1)} %collective-permute-done.4), channel_id=1, source_target_pairs={{0,2},{2,0},{4,6},{6,4},{8,10},{10,8},{12,14},{14,12},{1,3},{3,1},... | collective-permute-start | bytes 233480 | tf_op jit(solution)/shard_map/ppermute | solution.py:534
  20.5 3.6 %tables.1.far_table = bf16[32,256,256]{2,1,0:T(8,128)(2,1)} custom-call(s32[64]{0:T(128)} %width.5, s32[1]{0:T(128)} %bitcast.1.base.start), custom_call_target="tpu_custom_call" | custom-call | flops 16777216 | bytes 8388608 | tf_op jit(solution)/shard_map/tables/pallas_call | solution.py:134
  24.1 0.0 collective-permute-done.5
  24.1 0.8 %collective-permute-done.7 = f32[152,128]{1,0:T(8,128)S(1)} collective-permute-done((f32[152,128]{1,0:T(8,128)S(1)}, f32[152,128]{1,0:T(8,128)S(1)}, u32[]{:S(2)}, u32[]{:S(2)}) %collective-permute-start.7) | collective-permute-done | bytes 77856 | tf_op jit(solution)/shard_map/ppermute | solution.py:534
  24.8 0.0 collective-permute-done.6
  24.9 0.1 collective-permute-start.8
  25.0 2.0 %collective-permute-done.8.oth = f32[8,152,128]{2,1,0:T(8,128)S(1)} collective-permute-done((f32[8,152,128]{2,1,0:T(8,128)S(1)}, f32[8,152,128]{2,1,0:T(8,128)S(1)}, u32[]{:S(2)}, u32[]{:S(2)}) %collective-permute-start.8) | collective-permute-done | bytes 622624 | tf_op jit(solution)/shard_map/ppermute | solution.py:537
  27.0 0.0 copy-done
  27.0 7.8 %field.1 = (f32[4,4,128,128]{3,2,1,0:T(8,128)S(1)}, f32[33,128,128]{2,1,0:T(8,128)S(1)}, bf16[16,256,256]{2,1,0:T(8,128)(2,1)S(1)}) custom-call(s32[64]{0:T(128)S(1)} %copy-done, s32[1]{0:T(128)} %bitcast.first, s32[1]{0:T(128)} %bitcast.1.base.start, f32[8,152,128]{2,1,0:T(8,128)S(1)} %bitcast_dynamic-update-slice_fusion.own, ...), custom_call_target="tpu_custom_call" | custom-call | tf_op jit(solution)/shard_map/field/pallas_call | solution.py:436
  34.8 0.4 %collective-permute-start.9 = (f32[4,4,128,128]{3,2,1,0:T(8,128)S(1)}, f32[4,4,128,128]{3,2,1,0:T(8,128)S(1)}, u32[]{:S(2)}, u32[]{:S(2)}) collective-permute-start(f32[4,4,128,128]{3,2,1,0:T(8,128)S(1)} %get-tuple-element.32.slab), channel_id=1, source_target_pairs={{0,1},{1,0},{2,3},{3,2},{4,5},{5,4},{6,7},{7,6},{8,9},{9,8},{10,11... | collective-permute-start | bytes 3145736 | tf_op jit(solution)/shard_map/ppermute | solution.py:539
  35.2 1.4 %rest.1.more = f32[4,4,128,128]{3,2,1,0:T(8,128)S(1)} custom-call(s32[64]{0:T(128)S(1)} %copy-done, s32[1]{0:T(128)} %bitcast.1.base.start, f32[33,128,128]{2,1,0:T(8,128)S(1)} %get-tuple-element.33.field, bf16[16,256,256]{2,1,0:T(8,128)(2,1)S(1)} %get-tuple-element.34.table), custom_call_target="tpu_custom_call" | custom-call | flops 8589934592 | bytes 33554432 | tf_op jit(solution)/shard_map/rest/pallas_call | solution.py:463
  36.7 0.2 collective-permute-start.10
  36.8 0.7 %collective-permute-done.9.slab = f32[4,4,128,128]{3,2,1,0:T(8,128)S(1)} collective-permute-done((f32[4,4,128,128]{3,2,1,0:T(8,128)S(1)}, f32[4,4,128,128]{3,2,1,0:T(8,128)S(1)}, u32[]{:S(2)}, u32[]{:S(2)}) %collective-permute-start.9) | collective-permute-done | bytes 1048608 | tf_op jit(solution)/shard_map/ppermute | solution.py:539
  37.5 1.2 %mix.2.refs_0_ = f32[2,4,256,256]{3,2,1,0:T(8,128)S(1)} custom-call(f32[4,4,128,128]{3,2,1,0:T(8,128)S(1)} %get-tuple-element.32.slab, f32[4,4,128,128]{3,2,1,0:T(8,128)S(1)} %rest.1.more, bf16[256,256]{1,0:T(8,128)(2,1)S(1)} %get-tuple-element.39.high, bf16[256,256]{1,0:T(8,128)(2,1)S(1)} %get-tuple-element.40.low), custom_call_target="tpu_custom_call" | custom-call | tf_op jit(solution)/shard_map/mix/pallas_call | solution.py:502
  38.7 0.7 %collective-permute-done.10.more = f32[4,4,128,128]{3,2,1,0:T(8,128)S(1)} collective-permute-done((f32[4,4,128,128]{3,2,1,0:T(8,128)S(1)}, f32[4,4,128,128]{3,2,1,0:T(8,128)S(1)}, u32[]{:S(2)}, u32[]{:S(2)}) %collective-permute-start.10) | collective-permute-done | bytes 1048608 | tf_op jit(solution)/shard_map/ppermute | solution.py:541
  39.4 2.3 %mix.3 = f32[256,16,128]{2,1,0:T(8,128)} custom-call(f32[4,4,128,128]{3,2,1,0:T(8,128)S(1)} %collective-permute-done.9.slab, f32[4,4,128,128]{3,2,1,0:T(8,128)S(1)} %collective-permute-done.10.more, bf16[256,256]{1,0:T(8,128)(2,1)S(1)} %get-tuple-element.36.high, bf16[256,256]{1,0:T(8,128)(2,1)S(1)} %get-tuple-element.37.low, f32[2,4,256,256]{3,2,1,0:T(8,128)S(1)} %mix.2.refs_0_), custom_call_target="tpu_custom_call" | custom-call | tf_op jit(solution)/shard_map/mix/pallas_call | solution.py:502
  (7 shorter events, 0.0 us)
Async XLA Ops:
  4.0 15.4 %collective-permute-start.4 = (f32[152,128]{1,0:T(8,128)}, f32[152,128]{1,0:T(8,128)S(1)}, u32[]{:S(2)}, u32[]{:S(2)}) collective-permute-start(f32[152,128]{1,0:T(8,128)} %route.1), channel_id=1, source_target_pairs={{0,12},{2,14},{4,0},{6,2},{8,4},{10,6},{12,8},{14,10},{1,13},{3,15... | collective-permute-start | bytes 233480 | tf_op jit(solution)/shard_map/ppermute | solution.py:528
  9.1 6.8 %collective-permute-start.2 = (f32[152,128]{1,0:T(8,128)}, f32[152,128]{1,0:T(8,128)S(1)}, u32[]{:S(2)}, u32[]{:S(2)}) collective-permute-start(f32[152,128]{1,0:T(8,128)} %route.1), channel_id=1, source_target_pairs={{0,2},{2,0},{4,6},{6,4},{8,10},{10,8},{12,14},{14,12},{1,3},{3,1},... | collective-permute-start | bytes 233480 | tf_op jit(solution)/shard_map/ppermute | solution.py:531
  10.6 6.7 %collective-permute-start.1 = (f32[152,128]{1,0:T(8,128)}, f32[152,128]{1,0:T(8,128)S(1)}, u32[]{:S(2)}, u32[]{:S(2)}) collective-permute-start(f32[152,128]{1,0:T(8,128)} %route.1), channel_id=1, source_target_pairs={{0,8},{2,10},{4,12},{6,14},{8,0},{10,2},{12,4},{14,6},{1,9},{3,11}... | collective-permute-start | bytes 233480 | tf_op jit(solution)/shard_map/ppermute | solution.py:528
  10.6 7.7 %collective-permute-start = (f32[152,128]{1,0:T(8,128)}, f32[152,128]{1,0:T(8,128)S(1)}, u32[]{:S(2)}, u32[]{:S(2)}) collective-permute-start(f32[152,128]{1,0:T(8,128)} %route.1), channel_id=1, source_target_pairs={{0,4},{2,6},{4,8},{6,10},{8,12},{10,14},{12,0},{14,2},{1,5},{3,7},... | collective-permute-start | bytes 233480 | tf_op jit(solution)/shard_map/ppermute | solution.py:528
  11.6 1.4 %collective-permute-start.3 = (f32[4,64]{1,0:T(4,128)}, f32[4,64]{1,0:T(4,128)S(1)}, u32[]{:S(2)}, u32[]{:S(2)}) collective-permute-start(f32[4,64]{1,0:T(4,128)} %scale.1), channel_id=1, source_target_pairs={{0,1},{1,0},{2,3},{3,2},{4,5},{5,4},{6,7},{7,6},{8,9},{9,8},{10,11... | collective-permute-start | bytes 3080 | tf_op jit(solution)/shard_map/ppermute | solution.py:522
  13.0 0.7 %copy-start.1 = (f32[4,64]{1,0:T(4,128)S(1)}, f32[4,64]{1,0:T(4,128)}, u32[]{:S(2)}) copy-start(f32[4,64]{1,0:T(4,128)} %scale.1) | copy-start | bytes 3076
  13.6 0.7 %copy-start.2 = (f32[4,64]{1,0:T(4,128)S(1)}, f32[4,64]{1,0:T(4,128)}, u32[]{:S(2)}) copy-start(f32[4,64]{1,0:T(4,128)} %sigma.1) | copy-start | bytes 3076
  14.3 0.7 %copy-start.3 = (f32[4,8]{1,0:T(4,128)S(1)}, f32[4,8]{1,0:T(4,128)}, u32[]{:S(2)}) copy-start(f32[4,8]{1,0:T(4,128)} %balance.1) | copy-start | bytes 388
  17.3 7.6 %collective-permute-start.6 = (f32[152,128]{1,0:T(8,128)S(1)}, f32[152,128]{1,0:T(8,128)S(1)}, u32[]{:S(2)}, u32[]{:S(2)}) collective-permute-start(f32[152,128]{1,0:T(8,128)S(1)} %collective-permute-done.1), channel_id=1, source_target_pairs={{0,2},{2,0},{4,6},{6,4},{8,10},{10,8},{12,14},{14,12},{1,3},{3,1},... | collective-permute-start | bytes 233480 | tf_op jit(solution)/shard_map/ppermute | solution.py:534
  18.3 5.8 %collective-permute-start.5 = (f32[152,128]{1,0:T(8,128)S(1)}, f32[152,128]{1,0:T(8,128)S(1)}, u32[]{:S(2)}, u32[]{:S(2)}) collective-permute-start(f32[152,128]{1,0:T(8,128)S(1)} %collective-permute-done), channel_id=1, source_target_pairs={{0,2},{2,0},{4,6},{6,4},{8,10},{10,8},{12,14},{14,12},{1,3},{3,1},... | collective-permute-start | bytes 233480 | tf_op jit(solution)/shard_map/ppermute | solution.py:534
  19.4 7.6 %copy-start = (s32[64]{0:T(128)S(1)}, s32[64]{0:T(128)}, u32[]{:S(2)}) copy-start(s32[64]{0:T(128)} %width.5) | copy-start | bytes 772
  19.4 5.4 %collective-permute-start.7 = (f32[152,128]{1,0:T(8,128)S(1)}, f32[152,128]{1,0:T(8,128)S(1)}, u32[]{:S(2)}, u32[]{:S(2)}) collective-permute-start(f32[152,128]{1,0:T(8,128)S(1)} %collective-permute-done.4), channel_id=1, source_target_pairs={{0,2},{2,0},{4,6},{6,4},{8,10},{10,8},{12,14},{14,12},{1,3},{3,1},... | collective-permute-start | bytes 233480 | tf_op jit(solution)/shard_map/ppermute | solution.py:534
  24.9 2.1 %collective-permute-start.8 = (f32[8,152,128]{2,1,0:T(8,128)S(1)}, f32[8,152,128]{2,1,0:T(8,128)S(1)}, u32[]{:S(2)}, u32[]{:S(2)}) collective-permute-start(f32[8,152,128]{2,1,0:T(8,128)S(1)} %bitcast_dynamic-update-slice_fusion.own), channel_id=1, source_target_pairs={{0,1},{1,0},{2,3},{3,2},{4,5},{5,4},{6,7},{7,6},{8,9},{9,8},{10,11... | collective-permute-start | bytes 1867784 | tf_op jit(solution)/shard_map/ppermute | solution.py:537
  34.8 2.7 %collective-permute-start.9 = (f32[4,4,128,128]{3,2,1,0:T(8,128)S(1)}, f32[4,4,128,128]{3,2,1,0:T(8,128)S(1)}, u32[]{:S(2)}, u32[]{:S(2)}) collective-permute-start(f32[4,4,128,128]{3,2,1,0:T(8,128)S(1)} %get-tuple-element.32.slab), channel_id=1, source_target_pairs={{0,1},{1,0},{2,3},{3,2},{4,5},{5,4},{6,7},{7,6},{8,9},{9,8},{10,11... | collective-permute-start | bytes 3145736 | tf_op jit(solution)/shard_map/ppermute | solution.py:539
  36.7 2.7 %collective-permute-start.10 = (f32[4,4,128,128]{3,2,1,0:T(8,128)S(1)}, f32[4,4,128,128]{3,2,1,0:T(8,128)S(1)}, u32[]{:S(2)}, u32[]{:S(2)}) collective-permute-start(f32[4,4,128,128]{3,2,1,0:T(8,128)S(1)} %rest.1.more), channel_id=1, source_target_pairs={{0,1},{1,0},{2,3},{3,2},{4,5},{5,4},{6,7},{7,6},{8,9},{9,8},{10,11... | collective-permute-start | bytes 3145736 | tf_op jit(solution)/shard_map/ppermute | solution.py:541
